TPU v7x, 32 devices: a whole 2x2x4 slice. The times are simulated.
32 devices in a mesh: dp: 4 (over z), ctx: 8 (over y, x, core).
Axes of the slice: x: 2, y: 2, z: 4, core: 2. Of those that a mesh axis runs over, the one named last changes fastest.
Arguments:
- block_input: bfloat16 [2, 4, 1024, 768], P(None, 'dp', 'ctx'), may hold values from -6 to 6
- out_grad: bfloat16 [2, 4, 1024, 768], P(None, 'dp', 'ctx'), may hold values from -6 to 6
- prefix_len: int32 [2, 4], P(None, 'dp'), may hold values from 102 to 512
- attn_gain: bfloat16 [768], P(('dp', 'ctx')), may hold values from 0.5 to 1.5
- q_weight: bfloat16 [768, 768], P(('dp', 'ctx')), may hold values from -0.21875 to 0.21875
- k_weight: bfloat16 [768, 768], P(('dp', 'ctx')), may hold values from -0.21875 to 0.21875
- v_weight: bfloat16 [768, 768], P(('dp', 'ctx')), may hold values from -0.21875 to 0.21875
- conv_q: bfloat16 [3, 768], P(None, ('dp', 'ctx')), may hold values from -2.5 to 2.5
- conv_k: bfloat16 [3, 768], P(None, ('dp', 'ctx')), may hold values from -2.5 to 2.5
- conv_v: bfloat16 [3, 768], P(None, ('dp', 'ctx')), may hold values from -2.5 to 2.5
- out_weight: bfloat16 [768, 768], P(('dp', 'ctx')), may hold values from -3 to 3
- out_bias: bfloat16 [768], P(('dp', 'ctx')), may hold values from -1.75 to 1.75
- ffn_gain: bfloat16 [768], P(('dp', 'ctx')), may hold values from 0.5 to 1.5
- up_weight: bfloat16 [768, 3072], P(('dp', 'ctx')), may hold values from -0.21875 to 0.21875
- up_bias: bfloat16 [3072], P(('dp', 'ctx')), may hold values from -3 to 3
- down_weight: bfloat16 [3072, 768], P(('dp', 'ctx')), may hold values from -0.109375 to 0.109375
- down_bias: bfloat16 [768], P(('dp', 'ctx')), may hold values from -1.75 to 1.75
Outputs:
- block_output: bfloat16 [2, 4, 1024, 768], P(None, 'dp', 'ctx')
- input_grad: float32 [2, 4, 1024, 768], P(None, 'dp', 'ctx')
- attn_gain_grad: float32 [768], P(('dp', 'ctx'))
- q_weight_grad: float32 [768, 768], P(('dp', 'ctx'))
- k_weight_grad: float32 [768, 768], P(('dp', 'ctx'))
- v_weight_grad: float32 [768, 768], P(('dp', 'ctx'))
- conv_q_grad: float32 [3, 768], P(None, ('dp', 'ctx'))
- conv_k_grad: float32 [3, 768], P(None, ('dp', 'ctx'))
- conv_v_grad: float32 [3, 768], P(None, ('dp', 'ctx'))
- out_weight_grad: float32 [768, 768], P(('dp', 'ctx'))
- out_bias_grad: float32 [768], P(('dp', 'ctx'))
- ffn_gain_grad: float32 [768], P(('dp', 'ctx'))
- up_weight_grad: float32 [768, 3072], P(('dp', 'ctx'))
- up_bias_grad: float32 [3072], P(('dp', 'ctx'))
- down_weight_grad: float32 [3072, 768], P(('dp', 'ctx'))
- down_bias_grad: float32 [768], P(('dp', 'ctx'))
All inputs are finite; a program needn't handle non-finite values.
Results may differ from a plain program's by a relative error of at most 0.019.
Values may be sent and summed in bfloat16 or wider, within the bound.
No kernel may reach another device: no remote copies, remote signals or barrier semaphores. Data moves between devices by JAX's collectives and lax.ppermute only.
A program may use at most 192 MiB of HBM per device.

v0:
```python
import jax
import jax.numpy as jnp
from jax import lax
from jax.sharding import PartitionSpec as P

HEADS = 12
HEAD = 64


EPS = 1e-06
NEG = -1e30


def shifted(shard, axis, by):
    peers = lax.axis_size(axis)
    pairs = [(i, i + by) for i in range(peers) if 0 <= i + by < peers]
    return lax.ppermute(shard, axis, pairs)


def norm_rows(values, gain_vec):
    factor = lax.rsqrt(jnp.mean(values * values, axis=-1, keepdims=True) + EPS)
    return (factor, values * factor * gain_vec)


def norm_back(values, factor, gain_vec, grad_out):
    weighted = grad_out * gain_vec
    inner = jnp.mean(weighted * values, axis=-1, keepdims=True)
    return (
        factor * weighted - values * factor**3 * inner,
        jnp.sum(grad_out * values * factor, axis=0),
    )


def outer_sum(left, right):
    return lax.dot_general(
        left, right, (((0,), (0,)), ((), ())), preferred_element_type=jnp.float32
    )


def back_prod(grad_rows, weight):
    return lax.dot_general(
        grad_rows, weight, (((1,), (1,)), ((), ())), preferred_element_type=jnp.float32
    )


def scores_of(query, key_part, key_start, offset, prefix):
    raw_scores = jnp.einsum("sthe,skhe->shtk", query, key_part, preferred_element_type=jnp.float32)
    row_ids = offset + jnp.arange(query.shape[1], dtype=jnp.int32)
    col_ids = key_start + jnp.arange(key_part.shape[1], dtype=jnp.int32)
    allowed = (col_ids[None, None, :] <= row_ids[None, :, None]) | (
        col_ids[None, None, :] < prefix[:, None, None]
    )
    return jnp.where(allowed[:, None], raw_scores * HEAD ** (-0.5), NEG)


def forward_pass(inputs, prefix, weights, offset):
    (
        gain_attn,
        w_query,
        w_key,
        w_value,
        conv_query,
        conv_key,
        conv_value,
        w_out,
        b_out,
        gain_ffn,
        w_up,
        b_up,
        w_down,
        b_down,
    ) = weights
    seq_count, tok_len, features = inputs.shape
    length = tok_len * lax.axis_size("ctx")
    key_block = min(512, length)
    block_count = length // key_block
    rows_in = inputs.reshape(seq_count * tok_len, features)
    factor_attn, normed = norm_rows(rows_in, gain_attn.astype(jnp.float32))
    normed_low = normed.astype(jnp.bfloat16)
    w_joint = jnp.concatenate([w_query, w_key, w_value], axis=1)
    kernel = jnp.concatenate([conv_query, conv_key, conv_value], axis=1).astype(jnp.float32)
    linear = jnp.dot(normed_low, w_joint, preferred_element_type=jnp.float32).reshape(
        seq_count, tok_len, 3 * features
    )
    before = shifted(linear[:, tok_len - 2 :], "ctx", 1)
    padded = jnp.concatenate([before, linear], axis=1)
    mixed = (
        kernel[0] * padded[:, 2:]
        + kernel[1] * padded[:, 1 : tok_len + 1]
        + kernel[2] * padded[:, :tok_len]
    ).astype(jnp.bfloat16)
    query = mixed[:, :, :features].reshape(seq_count, tok_len, HEADS, HEAD)
    keys_all, values_all = (
        lax.all_gather(mixed[:, :, features : 2 * features], "ctx", axis=1, tiled=True),
        lax.all_gather(mixed[:, :, 2 * features :], "ctx", axis=1, tiled=True),
    )
    keys_all = keys_all.reshape(seq_count, length, HEADS, HEAD)
    values_all = values_all.reshape(seq_count, length, HEADS, HEAD)
    block_ids = jnp.arange(block_count, dtype=jnp.int32)

    def max_turn(carry, key_index):
        row_top, row_total = carry
        key_start = key_index * key_block
        key_part = lax.dynamic_slice_in_dim(keys_all, key_start, key_block, 1)
        scores = scores_of(query, key_part, key_start, offset, prefix)
        new_top = jnp.maximum(row_top, jnp.max(scores, axis=-1))
        row_total = row_total * jnp.exp(row_top - new_top) + jnp.sum(
            jnp.exp(scores - new_top[..., None]), axis=-1
        )
        return ((new_top, row_total), None)

    stat_shape = (seq_count, HEADS, tok_len)
    (row_top, row_total), unused = lax.scan(
        max_turn,
        (jnp.full(stat_shape, NEG, jnp.float32), jnp.zeros(stat_shape, jnp.float32)),
        block_ids,
    )
    log_total = row_top + jnp.log(row_total)

    def out_turn(summed, key_index):
        key_start = key_index * key_block
        key_part = lax.dynamic_slice_in_dim(keys_all, key_start, key_block, 1)
        value_part = lax.dynamic_slice_in_dim(values_all, key_start, key_block, 1)
        scores = scores_of(query, key_part, key_start, offset, prefix)
        probs = jnp.exp(scores - log_total[..., None]).astype(jnp.bfloat16)
        return (
            summed
            + jnp.einsum("shtk,skhe->sthe", probs, value_part, preferred_element_type=jnp.float32),
            None,
        )

    attended, unused = lax.scan(out_turn, jnp.zeros(query.shape, jnp.float32), block_ids)
    attn_low = attended.astype(jnp.bfloat16).reshape(seq_count * tok_len, features)
    resid = rows_in + (
        jnp.dot(attn_low, w_out, preferred_element_type=jnp.float32) + b_out.astype(jnp.float32)
    )
    factor_ffn, normed2 = norm_rows(resid, gain_ffn.astype(jnp.float32))
    normed_ffn = normed2.astype(jnp.bfloat16)
    pre_act = jnp.dot(normed_ffn, w_up, preferred_element_type=jnp.float32) + b_up.astype(
        jnp.float32
    )
    hidden_low = jnp.square(jax.nn.relu(pre_act)).astype(jnp.bfloat16)
    result = (
        resid
        + jnp.dot(hidden_low, w_down, preferred_element_type=jnp.float32)
        + b_down.astype(jnp.float32)
    )
    saved = (
        rows_in,
        factor_attn,
        normed_low,
        padded,
        query,
        keys_all,
        values_all,
        log_total,
        attended,
        attn_low,
        resid,
        factor_ffn,
        normed_ffn,
        pre_act,
        hidden_low,
    )
    return (saved, result)


def backward_pass(saved, cot_low, prefix, weights, offset):
    (
        rows_in,
        factor_attn,
        normed_low,
        padded,
        query,
        keys_all,
        values_all,
        log_total,
        attended,
        attn_low,
        resid,
        factor_ffn,
        normed_ffn,
        pre_act,
        hidden_low,
    ) = saved
    (
        gain_attn,
        w_query,
        w_key,
        w_value,
        conv_query,
        conv_key,
        conv_value,
        w_out,
        b_out,
        gain_ffn,
        w_up,
        b_up,
        w_down,
        b_down,
    ) = weights
    seq_count, tok_len = (query.shape[0], query.shape[1])
    features = rows_in.shape[1]
    length = keys_all.shape[1]
    key_block = min(512, length)
    block_count = length // key_block
    cot_rows = cot_low.reshape(seq_count * tok_len, features)
    cot_full = cot_rows.astype(jnp.float32)
    grad_bdown = jnp.sum(cot_full, axis=0)
    grad_wdown = outer_sum(hidden_low, cot_rows)
    grad_hidden = back_prod(cot_rows, w_down).astype(jnp.bfloat16)
    grad_pre = (grad_hidden.astype(jnp.float32) * 2.0 * jax.nn.relu(pre_act)).astype(jnp.bfloat16)
    grad_bup = jnp.sum(grad_pre.astype(jnp.float32), axis=0)
    grad_wup = outer_sum(normed_ffn, grad_pre)
    grad_normed = back_prod(grad_pre, w_up)
    resid_part, grad_gffn = norm_back(resid, factor_ffn, gain_ffn.astype(jnp.float32), grad_normed)
    grad_resid = cot_full + resid_part
    grad_branch = grad_resid.astype(jnp.bfloat16)
    grad_bout = jnp.sum(grad_branch.astype(jnp.float32), axis=0)
    grad_wout = outer_sum(attn_low, grad_branch)
    grad_attn = (
        back_prod(grad_branch, w_out).astype(jnp.bfloat16).reshape(seq_count, tok_len, HEADS, HEAD)
    )
    delta = jnp.einsum("sthe,sthe->sht", grad_attn.astype(jnp.float32), attended)
    block_ids = jnp.arange(block_count, dtype=jnp.int32)

    def grad_terms(key_index):
        key_start = key_index * key_block
        key_part = lax.dynamic_slice_in_dim(keys_all, key_start, key_block, 1)
        value_part = lax.dynamic_slice_in_dim(values_all, key_start, key_block, 1)
        scores = scores_of(query, key_part, key_start, offset, prefix)
        probs = jnp.exp(scores - log_total[..., None])
        grad_probs = jnp.einsum(
            "sthe,skhe->shtk", grad_attn, value_part, preferred_element_type=jnp.float32
        )
        grad_scores = (probs * (grad_probs - delta[..., None]) * HEAD ** (-0.5)).astype(
            jnp.bfloat16
        )
        return (key_part, probs, grad_scores)

    def back_turn(summed, key_index):
        key_part, probs, grad_scores = grad_terms(key_index)
        summed = summed + jnp.einsum(
            "shtk,skhe->sthe", grad_scores, key_part, preferred_element_type=jnp.float32
        )
        grad_keys = jnp.einsum(
            "shtk,sthe->skhe", grad_scores, query, preferred_element_type=jnp.float32
        )
        grad_values = jnp.einsum(
            "shtk,sthe->skhe",
            probs.astype(jnp.bfloat16),
            grad_attn,
            preferred_element_type=jnp.float32,
        )
        return (summed, (grad_keys, grad_values))

    grad_query, (grad_keys, grad_values) = lax.scan(
        back_turn, jnp.zeros(query.shape, jnp.float32), block_ids
    )
    grad_keys = jnp.moveaxis(grad_keys, 0, 1).reshape(seq_count, length, features)
    grad_values = jnp.moveaxis(grad_values, 0, 1).reshape(seq_count, length, features)
    own_keys, own_values = (
        lax.psum_scatter(
            grad_keys.astype(jnp.bfloat16), "ctx", scatter_dimension=1, tiled=True
        ).astype(jnp.float32),
        lax.psum_scatter(
            grad_values.astype(jnp.bfloat16), "ctx", scatter_dimension=1, tiled=True
        ).astype(jnp.float32),
    )
    grad_mixed = jnp.concatenate(
        [grad_query.reshape(seq_count, tok_len, features), own_keys, own_values], axis=2
    )
    after = shifted(grad_mixed[:, :2], "ctx", -1)
    extended = jnp.concatenate([grad_mixed, after], axis=1)
    kernel = jnp.concatenate([conv_query, conv_key, conv_value], axis=1).astype(jnp.float32)
    grad_linear = (
        kernel[0] * extended[:, :tok_len]
        + kernel[1] * extended[:, 1 : tok_len + 1]
        + kernel[2] * extended[:, 2:]
    ).astype(jnp.bfloat16)
    grad_kernel = jnp.stack(
        [
            jnp.sum(grad_mixed * padded[:, 2:], axis=(0, 1)),
            jnp.sum(grad_mixed * padded[:, 1 : tok_len + 1], axis=(0, 1)),
            jnp.sum(grad_mixed * padded[:, :tok_len], axis=(0, 1)),
        ]
    )
    grad_lin_rows = grad_linear.reshape(seq_count * tok_len, 3 * features)
    w_joint = jnp.concatenate([w_query, w_key, w_value], axis=1)
    grad_joint = outer_sum(normed_low, grad_lin_rows)
    grad_norm1 = back_prod(grad_lin_rows, w_joint)
    input_part, grad_gattn = norm_back(
        rows_in, factor_attn, gain_attn.astype(jnp.float32), grad_norm1
    )
    input_grad = grad_resid + input_part
    grads = (
        grad_gattn,
        grad_joint[:, :features],
        grad_joint[:, features : 2 * features],
        grad_joint[:, 2 * features :],
        grad_kernel[:, :features],
        grad_kernel[:, features : 2 * features],
        grad_kernel[:, 2 * features :],
        grad_wout,
        grad_bout,
        grad_gffn,
        grad_wup,
        grad_bup,
        grad_wdown,
        grad_bdown,
    )
    return (grads, input_grad)


def shards(
    block_input,
    out_grad,
    prefix_len,
    attn_gain,
    q_weight,
    k_weight,
    v_weight,
    conv_q,
    conv_k,
    conv_v,
    out_weight,
    out_bias,
    ffn_gain,
    up_weight,
    up_bias,
    down_weight,
    down_bias,
):
    micro_count = block_input.shape[0]
    local_shape = block_input.shape[1:]
    offset = lax.axis_index("ctx") * block_input.shape[2]
    outputs = []
    input_grads = []
    totals = ()
    for microstep in range(micro_count):
        weights = (
            lax.all_gather(attn_gain, ("dp", "ctx"), axis=0, tiled=True),
            lax.all_gather(q_weight, ("dp", "ctx"), axis=0, tiled=True),
            lax.all_gather(k_weight, ("dp", "ctx"), axis=0, tiled=True),
            lax.all_gather(v_weight, ("dp", "ctx"), axis=0, tiled=True),
            lax.all_gather(conv_q, ("dp", "ctx"), axis=1, tiled=True),
            lax.all_gather(conv_k, ("dp", "ctx"), axis=1, tiled=True),
            lax.all_gather(conv_v, ("dp", "ctx"), axis=1, tiled=True),
            lax.all_gather(out_weight, ("dp", "ctx"), axis=0, tiled=True),
            lax.all_gather(out_bias, ("dp", "ctx"), axis=0, tiled=True),
            lax.all_gather(ffn_gain, ("dp", "ctx"), axis=0, tiled=True),
            lax.all_gather(up_weight, ("dp", "ctx"), axis=0, tiled=True),
            lax.all_gather(up_bias, ("dp", "ctx"), axis=0, tiled=True),
            lax.all_gather(down_weight, ("dp", "ctx"), axis=0, tiled=True),
            lax.all_gather(down_bias, ("dp", "ctx"), axis=0, tiled=True),
        )
        inputs = block_input[microstep].astype(jnp.float32)
        prefix = prefix_len[microstep]
        saved, result = forward_pass(inputs, prefix, weights, offset)
        weights = (
            lax.all_gather(attn_gain, ("dp", "ctx"), axis=0, tiled=True),
            lax.all_gather(q_weight, ("dp", "ctx"), axis=0, tiled=True),
            lax.all_gather(k_weight, ("dp", "ctx"), axis=0, tiled=True),
            lax.all_gather(v_weight, ("dp", "ctx"), axis=0, tiled=True),
            lax.all_gather(conv_q, ("dp", "ctx"), axis=1, tiled=True),
            lax.all_gather(conv_k, ("dp", "ctx"), axis=1, tiled=True),
            lax.all_gather(conv_v, ("dp", "ctx"), axis=1, tiled=True),
            lax.all_gather(out_weight, ("dp", "ctx"), axis=0, tiled=True),
            lax.all_gather(out_bias, ("dp", "ctx"), axis=0, tiled=True),
            lax.all_gather(ffn_gain, ("dp", "ctx"), axis=0, tiled=True),
            lax.all_gather(up_weight, ("dp", "ctx"), axis=0, tiled=True),
            lax.all_gather(up_bias, ("dp", "ctx"), axis=0, tiled=True),
            lax.all_gather(down_weight, ("dp", "ctx"), axis=0, tiled=True),
            lax.all_gather(down_bias, ("dp", "ctx"), axis=0, tiled=True),
        )
        grads, input_grad = backward_pass(saved, out_grad[microstep], prefix, weights, offset)
        totals = (
            grads
            if microstep == 0
            else tuple((earlier + later for earlier, later in zip(totals, grads)))
        )
        outputs.append(result.astype(jnp.bfloat16).reshape(local_shape))
        input_grads.append(input_grad.reshape(local_shape))
    owned = (
        lax.psum_scatter(totals[0], ("dp", "ctx"), scatter_dimension=0, tiled=True),
        lax.psum_scatter(totals[1], ("dp", "ctx"), scatter_dimension=0, tiled=True),
        lax.psum_scatter(totals[2], ("dp", "ctx"), scatter_dimension=0, tiled=True),
        lax.psum_scatter(totals[3], ("dp", "ctx"), scatter_dimension=0, tiled=True),
        lax.psum_scatter(totals[4], ("dp", "ctx"), scatter_dimension=1, tiled=True),
        lax.psum_scatter(totals[5], ("dp", "ctx"), scatter_dimension=1, tiled=True),
        lax.psum_scatter(totals[6], ("dp", "ctx"), scatter_dimension=1, tiled=True),
        lax.psum_scatter(totals[7], ("dp", "ctx"), scatter_dimension=0, tiled=True),
        lax.psum_scatter(totals[8], ("dp", "ctx"), scatter_dimension=0, tiled=True),
        lax.psum_scatter(totals[9], ("dp", "ctx"), scatter_dimension=0, tiled=True),
        lax.psum_scatter(totals[10], ("dp", "ctx"), scatter_dimension=0, tiled=True),
        lax.psum_scatter(totals[11], ("dp", "ctx"), scatter_dimension=0, tiled=True),
        lax.psum_scatter(totals[12], ("dp", "ctx"), scatter_dimension=0, tiled=True),
        lax.psum_scatter(totals[13], ("dp", "ctx"), scatter_dimension=0, tiled=True),
    )
    return (
        jnp.stack(outputs),
        jnp.stack(input_grads),
        owned[0],
        owned[1],
        owned[2],
        owned[3],
        owned[4],
        owned[5],
        owned[6],
        owned[7],
        owned[8],
        owned[9],
        owned[10],
        owned[11],
        owned[12],
        owned[13],
    )


def solution(mesh):
    in_specs = (
        P(None, "dp", "ctx", None),
        P(None, "dp", "ctx", None),
        P(None, "dp"),
        P(("dp", "ctx")),
        P(("dp", "ctx"), None),
        P(("dp", "ctx"), None),
        P(("dp", "ctx"), None),
        P(None, ("dp", "ctx")),
        P(None, ("dp", "ctx")),
        P(None, ("dp", "ctx")),
        P(("dp", "ctx"), None),
        P(("dp", "ctx")),
        P(("dp", "ctx")),
        P(("dp", "ctx"), None),
        P(("dp", "ctx")),
        P(("dp", "ctx"), None),
        P(("dp", "ctx")),
    )
    out_specs = (
        P(None, "dp", "ctx", None),
        P(None, "dp", "ctx", None),
        P(("dp", "ctx")),
        P(("dp", "ctx"), None),
        P(("dp", "ctx"), None),
        P(("dp", "ctx"), None),
        P(None, ("dp", "ctx")),
        P(None, ("dp", "ctx")),
        P(None, ("dp", "ctx")),
        P(("dp", "ctx"), None),
        P(("dp", "ctx")),
        P(("dp", "ctx")),
        P(("dp", "ctx"), None),
        P(("dp", "ctx")),
        P(("dp", "ctx"), None),
        P(("dp", "ctx")),
    )
    return jax.shard_map(shards, mesh=mesh, in_specs=in_specs, out_specs=out_specs, check_vma=False)
```

profile of v0, /device:TPU:0, one launch (start us, length us, event | category | flops | bytes accessed | tf_op | source)
XLA Modules:
  0.0 1521.4 jit_solution(16771068781345439575)
XLA Ops:
  13.7 42.3 %all-reduce.14 = (bf16[768]{0:T(1024)(128)(2,1)S(1)}, bf16[768]{0:T(1024)(128)(2,1)}, bf16[3072]{0:T(1024)(128)(2,1)}, bf16[768]{0:T(1024)(128)(2,1)}, bf16[768]{0:T(1024)(128)(2,1)}) all-reduce(bf16[768]{0:T(1024)(128)(2,1)S(1)} %dynamic-update-slice, ...), channel_id=1, replica_groups=mesh['dp'=4,'ctx'=8] {'dp','ctx'}, use_global_device_ids=true, to_apply=%add | all-reduce | flops 6144 | bytes 24576
  58.2 9.5 all-gather.14.cloned.1.call-done
  69.1 54.5 %all-gather.16.cloned.1.call-done = bf16[768,768]{1,0:T(8,128)(2,1)} async-done(((bf16[24,768]{1,0:T(8,128)(2,1)}), bf16[768,768]{1,0:T(8,128)(2,1)}) %all-gather.16.cloned.1.call-update) | async-done | bytes 1179664 | tf_op jit(solution)/shard_map/all_gather | solution.py:344
  124.9 54.6 %all-gather.18.cloned.1.call-done = bf16[768,768]{1,0:T(8,128)(2,1)} async-done(((bf16[24,768]{1,0:T(8,128)(2,1)}), bf16[768,768]{1,0:T(8,128)(2,1)}) %all-gather.18.cloned.1.call-update) | async-done | bytes 1179664 | tf_op jit(solution)/shard_map/all_gather | solution.py:345
  182.7 2.8 collective-permute-start
  187.3 2.6 collective-permute-start.1
  189.9 38.2 %all-gather.2 = bf16[32,24,3]{1,2,0:T(4,128)(2,1)S(1)} all-gather(bf16[1,24,3]{1,2,0:T(4,128)(2,1)S(1)} %bitcast.659), channel_id=1, replica_groups=mesh['dp'=4,'ctx'=8] {'dp','ctx'}, dimensions={0}, use_global_device_ids=true | all-gather | bytes 4752 | tf_op jit(solution)/shard_map/all_gather | solution.py:348
  228.2 36.7 %all-gather.1 = bf16[32,24,3]{1,2,0:T(4,128)(2,1)S(1)} all-gather(bf16[1,24,3]{1,2,0:T(4,128)(2,1)S(1)} %bitcast.660), channel_id=1, replica_groups=mesh['dp'=4,'ctx'=8] {'dp','ctx'}, dimensions={0}, use_global_device_ids=true | all-gather | bytes 4752 | tf_op jit(solution)/shard_map/all_gather | solution.py:347
  265.0 38.3 %all-gather = bf16[32,24,3]{1,2,0:T(4,128)(2,1)S(1)} all-gather(bf16[1,24,3]{1,2,0:T(4,128)(2,1)} %bitcast.661), channel_id=1, replica_groups=mesh['dp'=4,'ctx'=8] {'dp','ctx'}, dimensions={0}, use_global_device_ids=true | all-gather | bytes 4752 | tf_op jit(solution)/shard_map/all_gather | solution.py:346
  303.5 4.0 fusion.135
  315.8 14.6 all-gather.32.cloned.1.call-done
  330.4 2.6 copy.117
  333.5 17.5 %while.80 = (s32[]{:T(128)}, f32[1,12,128]{2,1,0:T(8,128)S(1)}, f32[1,12,128]{2,1,0:T(8,128)}, s32[2]{0:T(128)}, s32[]{:T(128)}, /*index=5*/s32[1,1]{1,0:T(1,128...) while((s32[]{:T(128)}, f32[1,12,128]{2,1,0:T(8,128)S(1)}, ...), condition=%wide.region_12.13_spmd.clone, body=%wide.region_9.12_spmd.clone.sunk | while | flops 106308744 | bytes 7606542 | solution.py:113
  336.9 2.5 fusion.295
  345.6 2.5 fusion.295
  351.0 7.5 all-gather.30.cloned.1.call-done
  358.4 2.6 copy.115
  361.1 9.3 while.81
  363.2 2.5 fusion.299
  367.9 2.5 fusion.299
  371.2 14.7 all-gather.20.cloned.1.call-done
  385.9 2.6 copy.111
  388.5 25.6 %all-gather.22.cloned.1.call-done = bf16[1,1024,768]{2,1,0:T(8,128)(2,1)} async-done(((bf16[1,128,768]{2,1,0:T(8,128)(2,1)}), bf16[1,1024,768]{2,1,0:T(8,128)(2,1)}) %all-gather.22.cloned.1.call-update) | async-done | bytes 1572880 | tf_op jit(solution)/shard_map/all_gather | solution.py:94
  414.1 2.7 copy.113
  417.3 14.9 while.78
  432.9 11.6 while.79
  435.1 3.4 fusion.294
  440.6 3.6 fusion.294
  446.2 24.9 %all-gather.24.cloned.1.call-done = bf16[768,768]{1,0:T(8,128)(2,1)} async-done(((bf16[24,768]{1,0:T(8,128)(2,1)}), bf16[768,768]{1,0:T(8,128)(2,1)}) %all-gather.24.cloned.1.call-update) | async-done | bytes 1179664 | tf_op jit(solution)/shard_map/all_gather | solution.py:349
  471.1 2.5 multiply_reduce_fusion.8
  475.1 61.4 %all-gather.26.cloned.1.call-done = bf16[768,3072]{1,0:T(8,128)(2,1)} async-done(((bf16[24,3072]{1,0:T(8,128)(2,1)}), bf16[768,3072]{1,0:T(8,128)(2,1)}) %all-gather.26.cloned.1.call-update) | async-done | bytes 4718608 | tf_op jit(solution)/shard_map/all_gather | solution.py:352
  536.6 3.2 fusion.108
  539.8 62.0 %all-gather.28.cloned.1.call-done = bf16[3072,768]{1,0:T(8,128)(2,1)} async-done(((bf16[96,768]{1,0:T(8,128)(2,1)}), bf16[3072,768]{1,0:T(8,128)(2,1)}) %all-gather.28.cloned.1.call-update) | async-done | bytes 4718608 | tf_op jit(solution)/shard_map/all_gather | solution.py:354
  601.8 4.8 convert_reduce_fusion
  609.4 2.3 convert_reduce_fusion.1
  619.3 25.3 %while.83 = (s32[]{:T(128)}, f32[1,128,12,64]{1,3,2,0:T(8,128)}, bf16[2,1,512,12,64]{2,4,3,1,0:T(8,128)(2,1)}, bf16[2,1,512,12,64]{2,4,3,1,0:T(8,128)(2,1)}, s32...) while((s32[]{:T(128)}, f32[1,128,12,64]{1,3,2,0:T(8,128)}, ...), condition=%wide.region_24.25_spmd.clone, body=%wide.region_23.24_spmd.clone.sunk | while | flops 512296576 | bytes 79491736 | solution.py:257
  622.2 2.1 fusion.324
  628.4 1.9 bitcast_dynamic-update-slice_fusion.11
  634.4 2.1 fusion.324
  636.6 2.3 fusion.325
  641.4 1.9 bitcast_dynamic-update-slice_fusion.11
  644.7 3.0 copy.130
  653.4 2.3 convert_element_type.290
  655.8 2.8 copy.129
  662.6 21.7 %while.82 = (s32[]{:T(128)}, f32[1,128,12,64]{1,3,2,0:T(8,128)}, bf16[2,1,512,12,64]{2,4,3,1,0:T(8,128)(2,1)}, bf16[2,1,512,12,64]{2,4,3,1,0:T(8,128)(2,1)}, s32...) while((s32[]{:T(128)}, f32[1,128,12,64]{1,3,2,0:T(8,128)}, ...), condition=%wide.region_18.19_spmd.clone, body=%wide.region_17.18_spmd.clone.sunk | while | flops 512296576 | bytes 79657480 | solution.py:257
  677.4 2.3 fusion.312
  684.3 3.0 copy.123
  702.1 27.4 %reduce-scatter.18.cloned.1.call-done = bf16[1,128,768]{2,1,0:T(8,128)(2,1)} async-done(((bf16[1,1024,768]{2,1,0:T(8,128)(2,1)}), bf16[1,128,768]{2,1,0:T(8,128)(2,1)}) %reduce-scatter.18.cloned.1.call-update) | async-done | bytes 196624 | tf_op jit(solution)/shard_map/reduce_scatter | solution.py:263
  733.2 38.1 %reduce-scatter.16.cloned.1.call-done = bf16[1,128,768]{2,1,0:T(8,128)(2,1)} async-done(((bf16[1,1024,768]{2,1,0:T(8,128)(2,1)}), bf16[1,128,768]{2,1,0:T(8,128)(2,1)}) %reduce-scatter.16.cloned.1.call-update) | async-done | bytes 196624 | tf_op jit(solution)/shard_map/reduce_scatter | solution.py:266
  773.0 39.9 %reduce-scatter.14.cloned.1.call-done = bf16[1,128,768]{2,1,0:T(8,128)(2,1)} async-done(((bf16[1,1024,768]{2,1,0:T(8,128)(2,1)}), bf16[1,128,768]{2,1,0:T(8,128)(2,1)}) %reduce-scatter.14.cloned.1.call-update) | async-done | bytes 196624 | tf_op jit(solution)/shard_map/reduce_scatter | solution.py:263
  819.2 2.1 multiply_reduce_fusion.3
  823.8 3.3 slice_add_fusion
  830.5 5.2 convolution_add_fusion.1
  837.1 2.4 fusion.178
  839.6 5.0 convolution_add_fusion
  851.8 3.4 fusion.138
  855.3 3.3 fusion.139
  864.7 42.4 %all-reduce.13 = (f32[768]{0:T(1024)S(1)}, f32[3,768]{1,0:T(4,128)S(1)}, f32[3,768]{1,0:T(4,128)S(1)}, f32[3,768]{1,0:T(4,128)S(1)}, f32[768]{0:T(1024)S(1)}, /*...) all-reduce(f32[768]{0:T(1024)S(1)} %add.445, ...), channel_id=6, replica_groups=mesh['dp'=4,'ctx'=8] {'dp','ctx'}, use_global_device_ids=true, to_apply=%region_30.31.clone | all-reduce | flops 13056 | bytes 104448
  913.2 4.7 reduce-scatter.28.cloned.1.call-done
  917.9 104.8 %reduce-scatter.22.cloned.1.call-done = f32[24,768]{1,0:T(8,128)} async-done(((f32[768,768]{1,0:T(8,128)}), f32[24,768]{1,0:T(8,128)}) %reduce-scatter.22.cloned.1.call-update) | async-done | bytes 73744 | tf_op jit(solution)/shard_map/reduce_scatter | solution.py:386
  1022.7 103.8 %reduce-scatter.24.cloned.1.call-done = f32[24,768]{1,0:T(8,128)} async-done(((f32[768,768]{1,0:T(8,128)}), f32[24,768]{1,0:T(8,128)}) %reduce-scatter.24.cloned.1.call-update) | async-done | bytes 73744 | tf_op jit(solution)/shard_map/reduce_scatter | solution.py:387
  1126.4 104.7 %reduce-scatter.26.cloned.1.call-done = f32[24,768]{1,0:T(8,128)} async-done(((f32[768,768]{1,0:T(8,128)}), f32[24,768]{1,0:T(8,128)}) %reduce-scatter.26.cloned.1.call-update) | async-done | bytes 73744 | tf_op jit(solution)/shard_map/reduce_scatter | solution.py:388
  1231.1 141.0 %reduce-scatter.30.cloned.1.call-done = f32[24,3072]{1,0:T(8,128)} async-done(((f32[768,3072]{1,0:T(8,128)}), f32[24,3072]{1,0:T(8,128)}) %reduce-scatter.30.cloned.1.call-update) | async-done | bytes 294928 | tf_op jit(solution)/shard_map/reduce_scatter | solution.py:395
  1372.1 142.0 %reduce-scatter.32.cloned.1.call-done = f32[96,768]{1,0:T(8,128)} async-done(((f32[3072,768]{1,0:T(8,128)}), f32[96,768]{1,0:T(8,128)}) %reduce-scatter.32.cloned.1.call-update) | async-done | bytes 294928 | tf_op jit(solution)/shard_map/reduce_scatter | solution.py:397
  (602 shorter events, 163.9 us)
Async XLA Ops:
  7.2 60.5 %all-gather.14.cloned.1.call-start = ((), (), s32[]{:S(2)}) async-start(), calls=%async_computation.10 | async-start | bytes 1216512 | tf_op jit(solution)/shard_map/all_gather | solution.py:343
  7.9 115.7 %all-gather.16.cloned.1.call-start = ((), (), s32[]{:S(2)}) async-start(), calls=%async_computation.11 | async-start | bytes 1216512 | tf_op jit(solution)/shard_map/all_gather | solution.py:344
  8.7 170.8 %all-gather.18.cloned.1.call-start = ((), (), s32[]{:S(2)}) async-start(), calls=%async_computation.12 | async-start | bytes 1216512 | tf_op jit(solution)/shard_map/all_gather | solution.py:345
  9.4 321.0 %all-gather.32.cloned.1.call-start = ((), (), s32[]{:S(2)}) async-start(), calls=%async_computation.19 | async-start | bytes 1769472 | tf_op jit(solution)/shard_map/all_gather | solution.py:94
  56.0 129.5 %copy-start.81 = (f32[768]{0:T(1024)}, f32[768]{0:T(1024)S(1)}, u32[]{:S(2)}) copy-start(f32[768]{0:T(1024)S(1)} %convert_element_type.251) | copy-start | bytes 9220
  57.6 123.3 %copy-start.108 = (f32[128]{0:T(128)}, f32[128]{0:T(128)S(1)}, u32[]{:S(2)}) copy-start(f32[128]{0:T(128)S(1)} %get-tuple-element.819) | copy-start | bytes 1540
  58.2 127.2 %copy-start.111 = (f32[128]{0:T(128)}, f32[128]{0:T(128)S(1)}, u32[]{:S(2)}) copy-start(f32[128]{0:T(128)S(1)} %get-tuple-element.821) | copy-start | bytes 1540
  180.9 4.6 copy-start.8
  181.6 4.6 copy-start.12
  182.7 120.8 %collective-permute-start = (f32[1,2,2304]{2,1,0:T(2,128)}, f32[1,2,2304]{2,1,0:T(2,128)}, u32[]{:S(2)}, u32[]{:S(2)}) collective-permute-start(f32[1,2,2304]{2,1,0:T(2,128)} %slice.169), channel_id=1, source_target_pairs={{0,1},{1,2},{2,3},{3,4},{4,5},{5,6},{6,7},{8,9},{9,10},{10,11},{11... | collective-permute-start | bytes 55304 | tf_op jit(solution)/shard_map/ppermute | solution.py:17
  185.5 4.4 copy-start.130
  185.5 42.7 %copy-start.131 = (bf16[3,24]{1,0:T(4,128)(2,1)S(1)}, bf16[3,24]{1,0:T(4,128)(2,1)}, u32[]{:S(2)}) copy-start(bf16[3,24]{1,0:T(4,128)(2,1)} %param.37) | copy-start | bytes 436
  187.3 116.2 %collective-permute-start.1 = (f32[1,2,2304]{2,1,0:T(2,128)S(1)}, f32[1,2,2304]{2,1,0:T(2,128)S(1)}, u32[]{:S(2)}, u32[]{:S(2)}) collective-permute-start(f32[1,2,2304]{2,1,0:T(2,128)S(1)} %slice.175), channel_id=1, source_target_pairs={{0,1},{1,2},{2,3},{3,4},{4,5},{5,6},{6,7},{8,9},{9,10},{10,11},{11... | collective-permute-start | bytes 55304 | tf_op jit(solution)/shard_map/ppermute | solution.py:17
  303.5 4.1 copy-start.89
  303.5 4.1 copy-start.91
  303.5 4.1 copy-start.93
  307.6 5.5 copy-start.128
  307.6 6.1 copy-start.129
  307.6 6.6 copy-start.126
  307.6 7.2 copy-start.127
  308.4 50.0 %all-gather.30.cloned.1.call-start = ((), (), s32[]{:S(2)}) async-start(), calls=%async_computation.18 | async-start | bytes 1769472 | tf_op jit(solution)/shard_map/all_gather | solution.py:95
  309.0 76.8 %all-gather.20.cloned.1.call-start = ((), (), s32[]{:S(2)}) async-start(), calls=%async_computation.13 | async-start | bytes 1769472 | tf_op jit(solution)/shard_map/all_gather | solution.py:95
  309.9 104.2 %all-gather.22.cloned.1.call-start = ((), (), s32[]{:S(2)}) async-start(), calls=%async_computation.14 | async-start | bytes 1769472 | tf_op jit(solution)/shard_map/all_gather | solution.py:94
  310.7 160.4 %all-gather.24.cloned.1.call-start = ((), (), s32[]{:S(2)}) async-start(), calls=%async_computation.15 | async-start | bytes 1216512 | tf_op jit(solution)/shard_map/all_gather | solution.py:349
  311.4 225.2 %all-gather.26.cloned.1.call-start = ((), (), s32[]{:S(2)}) async-start(), calls=%async_computation.16 | async-start | bytes 4866048 | tf_op jit(solution)/shard_map/all_gather | solution.py:352
  312.1 289.7 %all-gather.28.cloned.1.call-start = ((), (), s32[]{:S(2)}) async-start(), calls=%async_computation.17 | async-start | bytes 4866048 | tf_op jit(solution)/shard_map/all_gather | solution.py:354
  312.7 387.6 %reduce-scatter.20.cloned.1.call-start = ((), (), s32[]{:S(2)}) async-start(), calls=%async_computation.23 | async-start | bytes 1769472 | tf_op jit(solution)/shard_map/reduce_scatter | solution.py:266
  351.0 10.1 copy-start.88
  351.0 10.1 copy-start
  351.0 10.1 copy-start.72
  370.4 18.1 %copy-start.73 = (f32[1,128,12,64]{1,3,2,0:T(8,128)}, f32[1,128,12,64]{1,3,2,0:T(8,128)S(1)}, u32[]{:S(2)}) copy-start(f32[1,128,12,64]{1,3,2,0:T(8,128)S(1)} %get-tuple-element.339) | copy-start | bytes 1179652
  370.4 18.1 %copy-start.121 = (f32[1,12,128]{2,1,0:T(8,128)}, f32[1,12,128]{2,1,0:T(8,128)S(1)}, u32[]{:S(2)}) copy-start(f32[1,12,128]{2,1,0:T(8,128)S(1)} %get-tuple-element.1555) | copy-start | bytes 18436
  432.9 38.2 %copy-start.25 = (bf16[2,1,128,768]{3,2,1,0:T(8,128)(2,1)S(1)}, bf16[2,1,128,768]{3,2,1,0:T(8,128)(2,1)}, u32[]{:S(2)}) copy-start(bf16[2,1,128,768]{3,2,1,0:T(8,128)(2,1)} %param.29) | copy-start | bytes 1179652
  432.9 38.2 %copy-start.61 = (bf16[1,128,12,64]{1,3,2,0:T(8,128)(2,1)S(1)}, bf16[1,128,12,64]{1,3,2,0:T(8,128)(2,1)}, u32[]{:S(2)}) copy-start(bf16[1,128,12,64]{1,3,2,0:T(8,128)(2,1)} %convert_element_type.266) | copy-start | bytes 589828
  432.9 38.2 %copy-start.102 = (f32[768]{0:T(1024)S(1)}, f32[768]{0:T(1024)}, u32[]{:S(2)}) copy-start(f32[768]{0:T(1024)} %convert_element_type.255) | copy-start | bytes 9220
  446.2 28.4 %copy-start.59 = (bf16[1,128,12,64]{1,3,2,0:T(8,128)(2,1)}, bf16[1,128,12,64]{1,3,2,0:T(8,128)(2,1)S(1)}, u32[]{:S(2)}) copy-start(bf16[1,128,12,64]{1,3,2,0:T(8,128)(2,1)S(1)} %convert_element_type.254) | copy-start | bytes 589828
  471.1 65.5 %copy-start.83 = (f32[768]{0:T(1024)S(1)}, f32[768]{0:T(1024)}, u32[]{:S(2)}) copy-start(f32[768]{0:T(1024)} %convert_element_type.256) | copy-start | bytes 9220
  474.1 65.8 %copy-start.116 = (f32[128]{0:T(128)}, f32[128]{0:T(128)S(1)}, u32[]{:S(2)}) copy-start(f32[128]{0:T(128)S(1)} %get-tuple-element.825) | copy-start | bytes 1540
  474.5 139.0 %copy-start.28 = (f32[128,768]{1,0:T(8,128)}, f32[128,768]{1,0:T(8,128)S(1)}, u32[]{:S(2)}) copy-start(f32[128,768]{1,0:T(8,128)S(1)} %get-tuple-element.831) | copy-start | bytes 1179652
  475.1 138.4 %copy-start.114 = (f32[128]{0:T(128)}, f32[128]{0:T(128)S(1)}, u32[]{:S(2)}) copy-start(f32[128]{0:T(128)S(1)} %get-tuple-element.823) | copy-start | bytes 1540
  539.8 66.8 %copy-start.18 = (f32[128,3072]{1,0:T(8,128)}, f32[128,3072]{1,0:T(8,128)S(1)}, u32[]{:S(2)}) copy-start(f32[128,3072]{1,0:T(8,128)S(1)} %fusion.108) | copy-start | bytes 4718596
  601.8 4.8 copy-start.7
  601.8 7.4 slice-start
  650.4 79.1 %reduce-scatter.18.cloned.1.call-start = ((), (), s32[]{:S(2)}) async-start(), calls=%async_computation.22 | async-start | bytes 1769472 | tf_op jit(solution)/shard_map/reduce_scatter | solution.py:263
  659.7 111.6 %reduce-scatter.16.cloned.1.call-start = ((), (), s32[]{:S(2)}) async-start(), calls=%async_computation.21 | async-start | bytes 1769472 | tf_op jit(solution)/shard_map/reduce_scatter | solution.py:266
  690.1 122.8 %reduce-scatter.14.cloned.1.call-start = ((), (), s32[]{:S(2)}) async-start(), calls=%async_computation.20 | async-start | bytes 1769472 | tf_op jit(solution)/shard_map/reduce_scatter | solution.py:263
  695.9 222.0 %reduce-scatter.28.cloned.1.call-start = ((), (), s32[]{:S(2)}) async-start(), calls=%async_computation.27 | async-start | bytes 2433024 | tf_op jit(solution)/shard_map/reduce_scatter | solution.py:392
  700.3 322.4 %reduce-scatter.22.cloned.1.call-start = ((), (), s32[]{:S(2)}) async-start(), calls=%async_computation.24 | async-start | bytes 2433024 | tf_op jit(solution)/shard_map/reduce_scatter | solution.py:386
  732.0 84.3 %collective-permute-start.3 = (f32[1,2,2304]{2,1,0:T(2,128)}, f32[1,2,2304]{2,1,0:T(2,128)S(1)}, u32[]{:S(2)}, u32[]{:S(2)}) collective-permute-start(f32[1,2,2304]{2,1,0:T(2,128)} %slice.184), channel_id=1, source_target_pairs={{1,0},{2,1},{3,2},{4,3},{5,4},{6,5},{7,6},{9,8},{10,9},{11,10},{12... | collective-permute-start | bytes 55304 | tf_op jit(solution)/shard_map/ppermute | solution.py:17
  814.8 3.2 collective-permute-start.2
  827.1 299.3 %reduce-scatter.24.cloned.1.call-start = ((), (), s32[]{:S(2)}) async-start(), calls=%async_computation.25 | async-start | bytes 2433024 | tf_op jit(solution)/shard_map/reduce_scatter | solution.py:387
  827.7 403.4 %reduce-scatter.26.cloned.1.call-start = ((), (), s32[]{:S(2)}) async-start(), calls=%async_computation.26 | async-start | bytes 2433024 | tf_op jit(solution)/shard_map/reduce_scatter | solution.py:388
  828.3 543.8 %reduce-scatter.30.cloned.1.call-start = ((), (), s32[]{:S(2)}) async-start(), calls=%async_computation.28 | async-start | bytes 9732096 | tf_op jit(solution)/shard_map/reduce_scatter | solution.py:395
  835.7 678.4 %reduce-scatter.32.cloned.1.call-start = ((), (), s32[]{:S(2)}) async-start(), calls=%async_computation.29 | async-start | bytes 9732096 | tf_op jit(solution)/shard_map/reduce_scatter | solution.py:397
  855.2 4.2 copy-start.17
  855.2 4.2 copy-start.68
  855.2 4.2 copy-start.69
  855.3 4.2 copy-start.75
  855.3 4.4 copy-start.70
  855.3 4.4 copy-start.71
  863.1 48.9 %copy-start.49 = (f32[128,768]{1,0:T(8,128)S(1)}, f32[128,768]{1,0:T(8,128)}, u32[]{:S(2)}) copy-start(f32[128,768]{1,0:T(8,128)} %get-tuple-element.802) | copy-start | bytes 1179652
  863.1 48.9 %copy-start.52 = (f32[128,768]{1,0:T(8,128)S(1)}, f32[128,768]{1,0:T(8,128)}, u32[]{:S(2)}) copy-start(f32[128,768]{1,0:T(8,128)} %copy-done.50) | copy-start | bytes 1179652
  863.1 48.9 %copy-start.132 = (f32[128]{0:T(128)S(1)}, f32[128]{0:T(128)}, u32[]{:S(2)}) copy-start(f32[128]{0:T(128)} %get-tuple-element.818) | copy-start | bytes 1540
  863.1 48.9 %copy-start.133 = (f32[128]{0:T(128)S(1)}, f32[128]{0:T(128)}, u32[]{:S(2)}) copy-start(f32[128]{0:T(128)} %get-tuple-element.820) | copy-start | bytes 1540
  (125 other events, 237.8 us)
Sparse Core Ops, SparseCore 0:
  10.9 56.7 all-gather.13
  70.6 52.9 all-gather.15
  126.5 52.9 all-gather.17
  308.6 21.7 all-gather.31
  332.7 25.6 all-gather.29
  360.2 25.6 all-gather.19
  388.3 25.6 all-gather.21
  417.0 54.0 all-gather.23
  473.9 62.5 all-gather.25
  539.3 62.4 all-gather.27
  650.6 37.2 reduce-scatter.19
  691.0 38.4 reduce-scatter.17
  732.8 38.4 reduce-scatter.15
  774.5 38.4 reduce-scatter.13
  818.7 99.1 reduce-scatter.27
  924.5 98.1 reduce-scatter.21
  1028.4 97.9 reduce-scatter.23
  1133.0 98.1 reduce-scatter.25
  1237.6 134.4 reduce-scatter.29
  1379.5 134.6 reduce-scatter.31
where the time goes:
time: 1530 us; the launch traced here: 1520 us
  waiting for transfers between devices  1040 us (68%)
  blocking collectives  198 us (13%)
  local copies, waits for them, and re-layouts  96.2 us (6%)
  matrix products  94.1 us (6%)
  other arithmetic  55.6 us (4%)
  between operations  16.4 us (1%)
    reduce_scatter x1, waiting for transfers between devices, shards(): lax.psum_scatter(totals[12], ('dp', 'ctx'), scatter_dimension=0, tiled=True)  142 us
    reduce_scatter x1, waiting for transfers between devices, shards(): lax.psum_scatter(totals[10], ('dp', 'ctx'), scatter_dimension=0, tiled=True)  141 us
    reduce_scatter x1, waiting for transfers between devices, shards(): lax.psum_scatter(totals[1], ('dp', 'ctx'), scatter_dimension=0, tiled=True)  105 us
    reduce_scatter x1, waiting for transfers between devices, shards(): lax.psum_scatter(totals[3], ('dp', 'ctx'), scatter_dimension=0, tiled=True)  105 us
    reduce_scatter x1, waiting for transfers between devices, shards(): lax.psum_scatter(totals[2], ('dp', 'ctx'), scatter_dimension=0, tiled=True)  104 us
    unnamed x2, blocking collectives  84.7 us
    reduce_scatter x2, waiting for transfers between devices, backward_pass(): lax.psum_scatter(grad_keys.astype(jnp.bfloat16), 'ctx', scatter_dimension...  67.4 us
    all_gather x1, waiting for transfers between devices, shards(): lax.all_gather(down_weight, ('dp', 'ctx'), axis=0, tiled=True)  62 us
  transfers between devices with their start and end apart: 24, of which 20 were waited for; matrix products, arithmetic and copies ran while one was open for 11% of the time, Pallas kernels for 0%

commit v1 on v0

--- a/solution.py
+++ b/solution.py
@@ -1,6 +1,10 @@
+import functools
+
 import jax
 import jax.numpy as jnp
 from jax import lax
+from jax.experimental import pallas as pl
+from jax.experimental.pallas import tpu as pltpu
 from jax.sharding import PartitionSpec as P
 
 HEADS = 12
@@ -312,7 +316,7 @@
     return (grads, input_grad)
 
 
-def shards(
+def general_shards(
     block_input,
     out_grad,
     prefix_len,
@@ -417,7 +421,690 @@
     )
 
 
+CHIPS = 4
+F32 = jnp.float32
+BF16 = jnp.bfloat16
+
+
+def plane_plan(mesh):
+    return mesh.shape["ctx"] == 2 * CHIPS and mesh.shape["dp"] == 4
+
+
+def dot_nn(left, right):
+    return jnp.dot(left, right, preferred_element_type=F32)
+
+
+def dot_nt(left, right):
+    return lax.dot_general(left, right, (((1,), (1,)), ((), ())), preferred_element_type=F32)
+
+
+def dot_tn(left, right):
+    return lax.dot_general(left, right, (((0,), (0,)), ((), ())), preferred_element_type=F32)
+
+
+def call(body, outs, *args, smem=1, hbm=0, scratch=(), name=None, us=0, room=0):
+    out_shape = [jax.ShapeDtypeStruct(shape, dtype) for shape, dtype in outs]
+    scratch_shapes = [pltpu.VMEM(*spec) if isinstance(spec, tuple) else spec for spec in scratch]
+    size = sum(a.size * a.dtype.itemsize for a in args)
+    size += sum(int(jnp.dtype(o.dtype).itemsize) * o.size for o in out_shape)
+    for spec in scratch:
+        if isinstance(spec, tuple):
+            size += int(jnp.dtype(spec[1]).itemsize) * functools.reduce(lambda a, b: a * b, spec[0], 1)
+    spaces = [pltpu.SMEM] * smem + [pltpu.VMEM] * (len(args) - smem - hbm) + [pltpu.HBM] * hbm
+    return pl.pallas_call(
+        body,
+        out_shape=out_shape,
+        compiler_params=pltpu.CompilerParams(vmem_limit_bytes=room or int(size) + (4 << 20)),
+        in_specs=[pl.BlockSpec(memory_space=space) for space in spaces],
+        out_specs=[pl.BlockSpec(memory_space=pltpu.VMEM)] * len(outs),
+        scratch_shapes=scratch_shapes,
+        name=name,
+        cost_estimate=pl.CostEstimate(flops=1 + us * 10**9, transcendentals=0, bytes_accessed=1),
+    )(*args[: len(args) - hbm], *(pltpu.with_memory_space_constraint(a, pltpu.HBM) for a in args[len(args) - hbm :]))
+
+
+def send(value, bits):
+    dp, ctx = lax.axis_size("dp"), lax.axis_size("ctx")
+    pairs = [(i, (i // ctx) * ctx + ((i % ctx) ^ bits)) for i in range(dp * ctx)]
+    return lax.ppermute(value, ("dp", "ctx"), pairs)
+
+
+def send_z(value, bits):
+    dp, ctx = lax.axis_size("dp"), lax.axis_size("ctx")
+    pairs = [(i, ((i // ctx) ^ bits) * ctx + i % ctx) for i in range(dp * ctx)]
+    return lax.ppermute(value, ("dp", "ctx"), pairs)
+
+
+def after(value, *waits):
+    return lax.optimization_barrier((value, *waits))[0]
+
+
+def all_after(values, *waits):
+    return list(lax.optimization_barrier((*values, *waits))[: len(values)])
+
+
+def to_chips(blocks):
+    return [blocks[0]] + [send(blocks[j], 2 * j) for j in range(1, CHIPS)]
+
+
+def to_all_planes(ids, block, *first, direct=False):
+    two, one = send_z(block, 2), send_z(block, 1)
+    three = send_z(block, 3) if direct else send_z(after(two, *first), 1)
+    return call(stack_k, [((4, *block.shape), block.dtype)], ids, block, one, two, three, name="stack")[0]
+
+
+def stack_k(ids, s0, s1, s2, s3, out):
+    for r, ref in enumerate((s0, s1, s2, s3)):
+        out[r] = ref[...]
+
+
+def join_k(ids, mine, other, keep, later, now):
+    n = keep.shape[0]
+    for r, out in ((0, keep), (2, later), (1, now.at[0]), (3, now.at[1])):
+        at = slice(r * n, r * n + n)
+        out[...] = (mine[at].astype(F32) + other[at].astype(F32)).astype(BF16)
+
+
+def pass_on_k(ids, later, got, out):
+    out[...] = (later[...].astype(F32) + got[1].astype(F32)).astype(BF16)
+
+
+def join_cores(ids, keep, away, name):
+    size = (keep.shape[0] // 4, *keep.shape[1:])
+    return call(
+        join_k, [(size, BF16)] * 2 + [((2, *size), BF16)], ids, keep, send(away, 1), name="join_" + name
+    )
+
+
+def to_all_chips(block):
+    half = block.shape[0] // 2
+    one, two = send(block, 2), send(block, 4)
+    return [block, one, two, send(one[:half], 4), send(two[half:], 2)]
+
+
+def add_half_k(ids, one, two, low, high, one_out, two_out):
+    half = low.shape[0]
+    one_out[:half, :] = one[:half, :]
+    one_out[half:, :] = (one[half:, :].astype(F32) + high[...].astype(F32)).astype(BF16)
+    two_out[half:, :] = two[half:, :]
+    two_out[:half, :] = (two[:half, :].astype(F32) + low[...].astype(F32)).astype(BF16)
+
+
+def to_owners(ids, own, one, two, low, high, *first):
+    low, high = all_after([send(low, 2), send(high, 4)], *first)
+    one, two = call(add_half_k, [(one.shape, BF16)] * 2, ids, one, two, low, high, name="add_half")
+    return own, one, two
+
+
+ROWS = ((0, 256), (256, 512), (512, 768), (768, 896), (896, 1024))
+
+
+def place_k(ids, other, mine, out, sem):
+    c = ids[2]
+    rows = other.shape[2]
+    copy = pltpu.make_async_copy(mine.at[c, 0], out.at[pl.ds(pl.multiple_of(c * rows, rows), rows), :], sem)
+    copy.start()
+    out[pl.ds(pl.multiple_of((1 - c) * rows, rows), rows), :] = other[c, 0]
+    copy.wait()
+
+
+def pack_k(ids, *refs):
+    k = ids[1]
+    args, (p0, p1, p2, p3), stage, held, sems = refs[:13], refs[13:17], refs[17], refs[18:31], refs[31]
+    copies = [pltpu.make_async_copy(ref, to, sems.at[i]) for i, (ref, to) in enumerate(zip(args, held))]
+    for copy in copies:
+        copy.start()
+    for copy in copies:
+        copy.wait()
+    wq, wk, wv, up, wo, *vectors, bias_u = held
+    rows = jnp.concatenate([ref[...].astype(F32).reshape(-1, 24) for ref in vectors], axis=0)
+    rows = jnp.concatenate([rows, jnp.zeros((128 - rows.shape[0], 24), F32)], axis=0)
+    rows = jnp.concatenate([rows, jnp.zeros((128, 104), F32)], axis=1)
+    cols = rows.T[:24, :16]
+    bias = bias_u[...].astype(F32).reshape(1, 96)
+    bias = jnp.concatenate([bias[:, 24 * i : 24 * i + 24] for i in range(4)] + [jnp.zeros((20, 24), F32)], axis=0)
+    tail = jnp.concatenate([cols, bias, jnp.zeros((24, 24), F32)], axis=1).astype(BF16)
+    for chip in range(CHIPS):
+        lo = 192 * chip
+        for part, ref in enumerate((wq, wk, wv)):
+            stage[chip, :, 192 * part : 192 * part + 192] = ref[:, lo : lo + 192]
+        stage[chip, :, 576:640] = tail
+        for plane in range(4):
+            at = 640 + 192 * plane
+            stage[chip, :, at : at + 192] = up[:, 768 * plane + lo : 768 * plane + lo + 192]
+        stage[chip, :, 1408:2176] = wo[...]
+    for j, out in enumerate((p0, p1, p2, p3)):
+        out[...] = stage[k ^ j]
+
+
+def split_k(ids, p0, p1, p2, p3, a_out, b_out):
+    for j, ref in enumerate((p0, p1, p2, p3)):
+        a_out[j] = ref[:, :640]
+        b_out[j] = ref[:, 640:1408]
+        b_out[CHIPS + j] = ref[:, 1408:2176]
+
+
+def with_down_k(ids, b, wd, b_out, sems):
+    copies = [
+        pltpu.make_async_copy(wd.at[24 * j : 24 * j + 24, :], b_out.at[8 + j], sems.at[j]) for j in range(CHIPS)
+    ]
+    for copy in copies:
+        copy.start()
+    b_out[0:8] = b[...]
+    for copy in copies:
+        copy.wait()
+
+
+def gather_b_k(ids, mine, other, up_out, wo_out, wd_out):
+    z, k, c = ids[0], ids[1], ids[2]
+    for core, ref in enumerate((mine, other)):
+        for plane in range(4):
+            for j in range(CHIPS):
+                at = (z ^ plane) * 8 + (k ^ j) * 2 + (c ^ core)
+                up_out[at] = ref[plane, j]
+                wo_out[at] = ref[plane, CHIPS + j]
+                wd_out[((z ^ plane) * 2 + (c ^ core)) * 4 + j] = ref[plane, 8 + j]
+
+
+def hidden_grad_k(ids, g0, g1, g2, g3, g4, wd, dh, g_all):
+    for ref, (lo, hi) in zip((g0, g1, g2, g3, g4), ROWS):
+        g_all[lo:hi, :] = ref[...]
+
+    def block(j, carry):
+        at = pl.ds(pl.multiple_of(256 * j, 256), 256)
+        dh[at, :] = dot_nt(g_all[at, :], wd[...]).astype(BF16)
+        return carry
+
+    lax.fori_loop(0, 4, block, 0)
+
+
+def mask_rows(b, prefix, out):
+    cols = max(256 * (b + 1), 512)
+    row_ids = 256 * b + lax.broadcasted_iota(jnp.int32, (256, cols), 0)
+    col_ids = lax.broadcasted_iota(jnp.int32, (256, cols), 1)
+    out[:, :cols] = jnp.where((col_ids <= row_ids) | (col_ids < prefix), 0.0, NEG)
+    return cols
+
+
+def attend_k(
+    ids, pre, *refs,
+):
+    pieces, xs = refs[:2], refs[2:6]
+    w_out, bias_out, a_out, lin, q_out, k_out, v_out, o0, o1, o2, o3, att, lse, small_out, kern_out = refs[6:21]
+    w_scr, stage, mask, mixed = refs[21:]
+    z, k, c = ids[0], ids[1], ids[2]
+    prefix = pre[c, 0]
+    for core in range(2):
+        for plane in range(4):
+            for j in range(CHIPS):
+                w_scr[(z ^ plane) * 8 + (k ^ j) * 2 + (c ^ core)] = pieces[core][plane, j].astype(F32)
+    bias_out[...] = jnp.zeros_like(bias_out)
+    for plane in range(4):
+        for core in range(2):
+            piece = w_scr[plane * 8 + k * 2 + core, :, 512:640]
+            for part in range(4):
+                at = 96 * (2 * plane + core) + 24 * part
+                bias_out[0:1, at : at + 24] = piece[part : part + 1, 80:104]
+    small = w_scr[:, :, 512:640].reshape(768, 128).T[64:80]
+    w_out[...] = w_scr[:, :, 0:576].reshape(768, 576).astype(BF16)
+    small_out[...] = small
+    gain = small[0:1]
+    own = jnp.zeros((9, 192), F32)
+    for chip in range(CHIPS):
+        own = jnp.where(k == chip, small[1:10, 192 * chip : 192 * chip + 192], own)
+    kern = jnp.concatenate([own[0:3], own[3:6], own[6:9]], axis=1)
+    kern_out[...] = kern
+    lin[0:8, :] = jnp.zeros((8, lin.shape[1]), F32)
+    for j, ref in enumerate(xs):
+        at = pl.multiple_of((k ^ j) * 256, 256)
+        x = ref[...].astype(F32)
+        factor = lax.rsqrt(jnp.mean(x * x, axis=-1, keepdims=True) + EPS)
+        a_out[pl.ds(at, 256), :] = (x * factor * gain).astype(BF16)
+
+    def project(b, carry):
+        at = pl.multiple_of(256 * b, 256)
+        lin[pl.ds(pl.multiple_of(at + 8, 8), 256), :] = dot_nn(a_out[pl.ds(at, 256), :], w_out[...])
+        return carry
+
+    lax.fori_loop(0, 4, project, 0)
+    for b in range(4):
+        t = 256 * b
+        mixed[...] = (
+            kern[0:1] * lin[8 + t : 264 + t, :]
+            + kern[1:2] * lin[7 + t : 263 + t, :]
+            + kern[2:3] * lin[6 + t : 262 + t, :]
+        ).astype(BF16)
+        for h in range(3):
+            lo = 64 * h
+            q_out[h, t : t + 256, :] = mixed[:, lo : lo + 64] * BF16(HEAD ** (-0.5))
+            k_out[h, t : t + 256, :] = mixed[:, 192 + lo : 256 + lo]
+            v_out[h, t : t + 256, :] = mixed[:, 384 + lo : 448 + lo]
+    for b in range(4):
+        t = 256 * b
+        cols = mask_rows(b, prefix, mask)
+
+        def one_head(h, carry, t=t, cols=cols):
+            scores = dot_nt(q_out[h, t : t + 256, :], k_out[h, 0:cols, :]) + mask[:, :cols]
+            top = jnp.max(scores, axis=-1, keepdims=True)
+            weight = jnp.exp(scores - top)
+            total = jnp.sum(weight, axis=-1, keepdims=True)
+            probs = (weight * (1.0 / total)).astype(BF16)
+            att[h, t : t + 256, :] = dot_nn(probs, v_out[h, 0:cols, :])
+            lse[h, t : t + 256, :] = top + jnp.log(total)
+            return carry
+
+        lax.fori_loop(0, 3, one_head, 0)
+        stage[b] = jnp.concatenate([att[h, t : t + 256, :] for h in range(3)], axis=1).astype(BF16)
+    for j, out in enumerate((o0, o1, o2, o3)):
+        out[...] = stage[k ^ j]
+
+
+def resid_k(ids, t0, t1, t2, t3, wo, xw, small, x1_out, a2_out):
+    k = ids[1]
+    total = xw[...].astype(F32) + small[10:11]
+    for j, ref in enumerate((t0, t1, t2, t3)):
+        at = pl.multiple_of((k ^ j) * 192, 192)
+        total = total + dot_nn(ref[...], wo[pl.ds(at, 192), :])
+    x1_out[...] = total
+    factor = lax.rsqrt(jnp.mean(total * total, axis=-1, keepdims=True) + EPS)
+    a2_out[...] = (total * factor * small[11:12]).astype(BF16)
+
+
+def ffn_k(ids, a0, a1, a2, a3, a4, dh, up, bias, hsq, du, a_all, p0, p1, p2, p3, p4, stage):
+    for ref, (lo, hi) in zip((a0, a1, a2, a3, a4), ROWS):
+        a_all[lo:hi, :] = ref[...]
+
+    def block(j, carry):
+        at = pl.ds(pl.multiple_of(256 * j, 256), 256)
+        act = jax.nn.relu(dot_nn(a_all[at, :], up[...]) + bias[...])
+        hsq[at, :] = (act * act).astype(BF16)
+        low = (dh[at, :].astype(F32) * 2.0 * act).astype(BF16)
+        du[at, :] = low
+        stage[at, :] = dot_nt(low, up[...]).astype(BF16)
+        return carry
+
+    lax.fori_loop(0, 4, block, 0)
+    for ref, (lo, hi) in zip((p0, p1, p2, p3, p4), ROWS):
+        ref[...] = stage[lo:hi, :]
+
+
+def ffn_out_k(ids, hsq, wd, p0, p1, p2, p3):
+    for j, out in enumerate((p0, p1, p2, p3)):
+        out[...] = dot_nn(hsq[256 * j : 256 * j + 256, :], wd[...]).astype(BF16)
+
+
+def ffn_grads_k(ids, a_all, g_all, hsq, du, keep, away, bias_out, stage):
+    z, k, c = ids[0], ids[1], ids[2]
+    bias_out[...] = jnp.sum(du[...].astype(F32), axis=0, keepdims=True)
+    up_grad = dot_tn(a_all[...], du[...])
+    for plane in range(4):
+        for core in range(2):
+            to, at = c ^ core, (z ^ plane) * 8
+            for chip in range(CHIPS):
+                row = 24 * (plane * 8 + chip * 2 + core)
+                stage[to, at + (k ^ chip)] = up_grad[row : row + 24].astype(BF16)
+    down_grad = dot_tn(hsq[...], g_all[...])
+    for plane in range(4):
+        for core in range(2):
+            to, at = c ^ core, (z ^ plane) * 8
+            for chip in range(CHIPS):
+                row = 96 * (plane * 2 + core) + 24 * chip
+                stage[to, at + 4 + chip] = down_grad[row : row + 24].astype(BF16)
+    keep[...] = stage[0]
+    away[...] = stage[1]
+
+
+def sum_planes_k(ids, *refs):
+    f, o, r, (d_out, *outs) = refs[0:3], refs[3:6], refs[6:9], refs[9:]
+
+    def total(parts, at):
+        return parts[0][at].astype(F32) + parts[1][0, at].astype(F32) + parts[2][at].astype(F32)
+
+    for j, out in enumerate(outs):
+        out[:, 0:640] = total(r, j).astype(BF16)
+        out[:, 640:1408] = total(f, j).astype(BF16)
+        out[:, 1408:2176] = total(o, j).astype(BF16)
+        d_out[24 * j : 24 * j + 24, :] = total(f, CHIPS + j)
+
+
+def mid_grad_k(
+    ids, p0, p1, p2, x1, gw, small, wo, dx_out, dz_out, bias_out, o0, o1, o2, o3
+):
+    k = ids[1]
+    da2 = p0[...].astype(F32) + p1[...].astype(F32) + p2[...].astype(F32)
+    val = x1[...]
+    factor = lax.rsqrt(jnp.mean(val * val, axis=-1, keepdims=True) + EPS)
+    weighted = da2 * small[11:12]
+    inner = jnp.mean(weighted * val, axis=-1, keepdims=True)
+    dx = gw[...].astype(F32) + factor * weighted - val * (factor * factor * factor * inner)
+    dx_out[...] = dx
+    low = dx.astype(BF16)
+    dz_out[...] = low
+    bias_out[...] = jnp.sum(low.astype(F32), axis=0, keepdims=True)
+    for j, out in enumerate((o0, o1, o2, o3)):
+        at = pl.multiple_of((k ^ j) * 192, 192)
+        out[...] = dot_nt(low, wo[pl.ds(at, 192), :]).astype(BF16)
+
+
+def out_grads_k(ids, t0, t1, t2, t3, dz, keep, away, stage):
+    z, k, c = ids[0], ids[1], ids[2]
+    for j, ref in enumerate((t0, t1, t2, t3)):
+        part = dot_tn(ref[...], dz[...])
+        at = ((k ^ j) ^ z) * 4
+        for chip in range(CHIPS):
+            for core in range(2):
+                row = 24 * (2 * chip + core)
+                stage[c ^ core, at + (k ^ chip)] = part[row : row + 24].astype(BF16)
+    keep[...] = stage[0]
+    away[...] = stage[1]
+
+
+def attend_grad_k(
+    ids, pre, d0, d1, d2, d3, q_in, k_in, v_in, att, lse, lin, kern, w,
+    dlin_out, conv_out, p0, p1, p2, p3, p4, do_scr, dm, mask, dq, dk, dv, stage,
+):
+    k, c = ids[1], ids[2]
+    prefix = pre[c, 0]
+    for j, ref in enumerate((d0, d1, d2, d3)):
+        for h in range(3):
+            do_scr[h, pl.ds(pl.multiple_of((k ^ j) * 256, 256), 256), :] = ref[:, 64 * h : 64 * h + 64]
+    dm[1024:1032, :] = jnp.zeros((8, 576), F32)
+    for b in (3, 2, 1, 0):
+        t = 256 * b
+        cols = mask_rows(b, prefix, mask)
+
+        def one_head(h, carry, b=b, t=t, cols=cols):
+            q_rows, do_rows = q_in[h, t : t + 256, :], do_scr[h, t : t + 256, :]
+            scores = dot_nt(q_rows, k_in[h, 0:cols, :]) + mask[:, :cols]
+            probs = jnp.exp(scores - lse[h, t : t + 256, :])
+            delta = jnp.sum(do_rows.astype(F32) * att[h, t : t + 256, :], axis=-1, keepdims=True)
+            dprobs = dot_nt(do_rows, v_in[h, 0:cols, :])
+            dscores = (probs * (dprobs - delta)).astype(BF16)
+            dq[h, t : t + 256, :] = dot_nn(dscores, k_in[h, 0:cols, :]) * HEAD ** (-0.5)
+            dk_part = dot_tn(q_rows, dscores)
+            dv_part = dot_tn(do_rows, probs.astype(BF16))
+            if b == 3:
+                dk[h] = dk_part
+                dv[h] = dv_part
+            else:
+                dk[h, :, 0:cols] = dk[h, :, 0:cols] + dk_part
+                dv[h, :, 0:cols] = dv[h, :, 0:cols] + dv_part
+            return carry
+
+        lax.fori_loop(0, 3, one_head, 0)
+    for h in range(3):
+        dm[0:1024, 64 * h : 64 * h + 64] = dq[h]
+        dm[0:1024, 192 + 64 * h : 256 + 64 * h] = dk[h].T
+        dm[0:1024, 384 + 64 * h : 448 + 64 * h] = dv[h].T
+    taps = kern[...]
+    sums = [jnp.zeros((1, 576), F32) for _ in range(3)]
+    for b in range(4):
+        t = 256 * b
+        here = dm[t : t + 256, :]
+        dlin_out[t : t + 256, :] = (
+            taps[0:1] * here + taps[1:2] * dm[t + 1 : t + 257, :] + taps[2:3] * dm[t + 2 : t + 258, :]
+        ).astype(BF16)
+        for back in range(3):
+            sums[back] = sums[back] + jnp.sum(
+                here * lin[8 - back + t : 264 - back + t, :], axis=0, keepdims=True
+            )
+    conv_out[...] = jnp.concatenate(sums, axis=0)
+
+    def block(j, carry):
+        rows = dlin_out[pl.ds(pl.multiple_of((k ^ j) * 256, 256), 256), :]
+        stage[pl.ds(pl.multiple_of(256 * j, 256), 256), :] = dot_nt(rows, w[...]).astype(BF16)
+        return carry
+
+    lax.fori_loop(0, 4, block, 0)
+    for ref, (lo, hi) in zip((p0, p1, p2, p3, p4), ROWS):
+        ref[...] = stage[lo:hi, :]
+
+
+def proj_grads_k(ids, a1, dlin, conv, up_bias, out_bias, g, keep, away, stage):
+    z, k, c = ids[0], ids[1], ids[2]
+    grad = dot_tn(a1[...], dlin[...])
+    conv_rows = jnp.concatenate([conv[:, 0:192], conv[:, 192:384], conv[:, 384:576]], axis=0)
+    conv_all = jnp.concatenate(
+        [jnp.where(k == chip, conv_rows, 0.0) for chip in range(CHIPS)], axis=1
+    )
+    down_bias = jnp.sum(g[...].astype(F32), axis=0, keepdims=True)
+    rows = jnp.concatenate(
+        [conv_all, out_bias[...], down_bias, jnp.zeros((117, 768), F32)], axis=0
+    )
+    cols = rows.T
+    for plane in range(4):
+        for chip in range(CHIPS):
+            for core in range(2):
+                row = 24 * (plane * 8 + chip * 2 + core)
+                to, at = c ^ core, (z ^ plane) * 4 + (k ^ chip)
+                stage[to, at, :, 0:576] = grad[row : row + 24]
+                stage[to, at, :, 576:640] = cols[row : row + 24, 0:64]
+    for plane in range(4):
+        for core in range(2):
+            for part in range(4):
+                lo = 96 * (2 * plane + core) + 24 * part
+                stage[c ^ core, (z ^ plane) * 4, part : part + 1, 592:616] = up_bias[0:1, lo : lo + 24]
+    keep[...] = stage[0].astype(BF16)
+    away[...] = stage[1].astype(BF16)
+
+
+def halves_k(ids, total_fn, keep, away):
+    c = ids[2]
+    keep[...] = total_fn(pl.ds(pl.multiple_of(c * 128, 128), 128)).astype(keep.dtype)
+    away[...] = total_fn(pl.ds(pl.multiple_of((1 - c) * 128, 128), 128)).astype(away.dtype)
+
+
+def output_k(ids, p0, p1, p2, p3, x1, small, keep, away):
+    def rows_of(at):
+        total = p0[at, :].astype(F32) + p1[at, :].astype(F32) + p2[at, :].astype(F32)
+        return x1[at, :] + (total + p3[at, :].astype(F32)) + small[12:13]
+
+    halves_k(ids, rows_of, keep, away)
+
+
+def input_grad_k(ids, p0, p1, p2, xw, dx, small, keep, away):
+    def rows_of(at):
+        da1 = p0[at, :].astype(F32) + p1[at, :].astype(F32) + p2[at, :].astype(F32)
+        val = xw[at, :].astype(F32)
+        factor = lax.rsqrt(jnp.mean(val * val, axis=-1, keepdims=True) + EPS)
+        weighted = da1 * small[0:1]
+        inner = jnp.mean(weighted * val, axis=-1, keepdims=True)
+        return dx[at, :] + factor * weighted - val * (factor * factor * factor * inner)
+
+    halves_k(ids, rows_of, keep, away)
+
+
+def deliver_k(ids, out_keep, out_recv, in_keep, in_recv, out_ref, in_ref):
+    c = ids[2]
+    out_ref[c, 0] = out_keep[...]
+    out_ref[1 - c, 0] = out_recv[...]
+    in_ref[c, 0] = in_keep[...]
+    in_ref[1 - c, 0] = in_recv[...]
+
+
+def owned_k(
+    ids, s0, s1, s2, s3, wq, wk, wv, up, gain_a, gain_f,
+    gq, gk, gv, cq, ck, cv, go, gu, ga, gf, bo, bd, bu, stage_r, stage_u,
+):
+    k = ids[1]
+    extra = jnp.zeros((24, 128), F32)
+    out_sum = jnp.zeros((24, 768), F32)
+    for j, ref in enumerate((s0, s1, s2, s3)):
+        stage_r[k ^ j] = ref[:, 0:640].astype(F32)
+        stage_u[k ^ j] = ref[:, 640:1408].astype(F32)
+        out_sum = out_sum + ref[:, 1408:2176].astype(F32)
+        extra = extra + ref[:, 512:640].astype(F32)
+    go[...] = out_sum
+    for chip in range(CHIPS):
+        lo = 192 * chip
+        for part, ref in enumerate((gq, gk, gv)):
+            ref[:, lo : lo + 192] = stage_r[chip, :, 192 * part : 192 * part + 192]
+        for plane in range(4):
+            at = 768 * plane + lo
+            gu[:, at : at + 192] = stage_u[chip, :, 192 * plane : 192 * plane + 192]
+    attn = jnp.sum(
+        gq[...] * wq[...].astype(F32) + gk[...] * wk[...].astype(F32) + gv[...] * wv[...].astype(F32),
+        axis=-1, keepdims=True,
+    )
+    ffn = jnp.sum(gu[...] * up[...].astype(F32), axis=-1, keepdims=True)
+    cols = jnp.concatenate([extra[:, 64:75], attn, ffn, jnp.zeros((24, 115), F32)], axis=1)
+    cols = jnp.concatenate([cols, jnp.zeros((104, 128), F32)], axis=0)
+    rows = cols.T[:16, :24]
+    for at, ref in ((0, cq), (3, ck), (6, cv)):
+        ref[...] = rows[at : at + 3]
+    bo[...] = rows[9]
+    bd[...] = rows[10]
+    ga[...] = rows[11] / gain_a[...].astype(F32)
+    gf[...] = rows[12] / gain_f[...].astype(F32)
+    bu[...] = jnp.concatenate([extra[i : i + 1, 80:104] for i in range(4)], axis=1).reshape(96)
+
+
+def plane_shards(
+    block_input, out_grad, prefix_len, attn_gain, q_weight, k_weight, v_weight, conv_q, conv_k, conv_v,
+    out_weight, out_bias, ffn_gain, up_weight, up_bias, down_weight, down_bias,
+):
+    z, place = lax.axis_index("dp"), lax.axis_index("ctx")
+    ids = jnp.stack([z, place // 2, place % 2]).astype(jnp.int32)
+    block, half = ((256, 768), BF16), ((128, 768), BF16)
+    blocks = [block] * 3 + [half] * 2
+    tall, heads = ((1024, 768), BF16), (3, 1024, 64)
+
+    sem = pltpu.SemaphoreType.DMA
+    x_peer = send(block_input, 1)
+    weights = (
+        q_weight, k_weight, v_weight, up_weight, out_weight, attn_gain, conv_q, conv_k, conv_v, out_bias,
+        ffn_gain, down_bias, up_bias,
+    )
+    packs = call(
+        pack_k, [((24, 2176), BF16)] * 4, ids, *weights, hbm=13,
+        scratch=[((4, 24, 2176), BF16)] + [(w.shape, BF16) for w in weights] + [sem((13,))], name="pack",
+    )
+    packs = to_chips(packs)
+    x_peer = after(x_peer, *packs[1:])
+    (xw,) = call(place_k, [block], ids, x_peer, block_input, hbm=1, scratch=[sem(())], name="place_x")
+    xs = to_chips([xw] * 4)
+    a_own, b_own = call(split_k, [((4, 24, 640), BF16), ((8, 24, 768), BF16)], ids, *packs, name="split")
+    a_two, a_one = send_z(a_own, 2), send_z(a_own, 1)
+    a_three = send_z(a_two, 1)
+    (b_own,) = call(
+        with_down_k, [((12, 24, 768), BF16)], ids, after(b_own, a_two), down_weight, hbm=1, scratch=[sem((4,))],
+        name="with_down",
+    )
+
+    g_peer = send(after(out_grad, *packs[1:]), 1)
+    (gw,) = call(place_k, [block], ids, g_peer, out_grad, hbm=1, scratch=[sem(())], name="place_g")
+    (a_all,) = call(stack_k, [((4, 4, 24, 640), BF16)], ids, a_own, a_one, a_two, after(a_three, b_own, gw), name="stack_a")
+    a_peer = send(a_all, 1)
+    b_own = after(b_own, a_three)
+    b_one, b_two = send_z(b_own, 1), send_z(b_own, 2)
+    gw = after(gw, *xs[1:])
+    g_one, g_two = send(gw, 2), send(gw, 4)
+
+    w_a, up_bias_row, a1, lin, q, k, v, t0, t1, t2, t3, att, lse, small, kern = call(
+        attend_k,
+        [((768, 576), BF16), ((1, 768), F32), tall, ((1032, 576), F32)]
+        + [(heads, BF16)] * 3 + [((256, 192), BF16)] * 4
+        + [(heads, F32), ((3, 1024, 1), F32), ((16, 768), F32), ((3, 576), F32)],
+        ids, prefix_len, after(a_all, gw), a_peer, *xs,
+        smem=2, name="attend", us=0,
+        scratch=[((32, 24, 640), F32), ((4, 256, 192), BF16), ((256, 1024), F32), ((256, 576), BF16)],
+    )
+    atts = [t0, send(t1, 2), send(t2, 4)]
+    atts.append(send(after(t3, atts[1]), 6))
+    b_one, b_two, g_one, g_two = all_after([b_one, b_two, g_one, g_two], t1)
+    b_three = send_z(b_two, 1)
+    g_low, g_high = send(g_one[:128], 4), send(g_two[128:], 2)
+    (b_all,) = call(
+        stack_k, [((4, 12, 24, 768), BF16)], ids, b_own, *all_after([b_one, b_two, b_three], *atts[1:3], g_low, g_high), name="stack_b"
+    )
+    w_up, w_o, w_d = [
+        w.reshape(768, 768)
+        for w in call(gather_b_k, [((32, 24, 768), BF16)] * 3, ids, b_all, send(b_all, 1), name="gather_b")
+    ]
+    x1, a2 = call(resid_k, [((256, 768), F32), block], ids, *atts, w_o, xw, small, name="resid")
+    a2s = to_all_chips(a2)
+    dh, g_all = call(hidden_grad_k, [tall] * 2, ids, gw, g_one, g_two, g_low, g_high, w_d, name="hidden_grad")
+    hsq, du, a2_all, *da2 = call(
+        ffn_k, [tall] * 3 + blocks, ids, *a2s, dh, w_up, up_bias_row, scratch=[tall], name="ffn"
+    )
+    da2, da2_one, da2_two = to_owners(ids, *da2)
+    da2 = [da2, send(da2_one, 2), send(da2_two, 4)]
+    hsq, du = all_after([hsq, du], da2_one)
+    f_keep, f_away, up_bias_grad = call(
+        ffn_grads_k, [((32, 24, 768), BF16)] * 2 + [((1, 768), F32)], ids, a2_all, g_all, hsq, du,
+        scratch=[((2, 32, 24, 768), BF16)], name="ffn_grads", us=100,
+    )
+    f_keep, f_later, f_now = join_cores(ids, f_keep, f_away, "f")
+    f_now = send_z(f_now, 1)
+
+    outs = call(ffn_out_k, [block] * 4, ids, hsq, w_d, name="ffn_out", us=100)
+    dx, dz, out_bias_grad, *datt = call(
+        mid_grad_k, [((256, 768), F32), block, ((1, 768), F32)] + [((256, 192), BF16)] * 4,
+        ids, *da2, x1, after(gw, f_keep, outs[0]), small, w_o, name="mid_grad",
+    )
+    datt = to_chips(datt)
+    o_keep, o_away = call(
+        out_grads_k, [((16, 24, 768), BF16)] * 2, ids, *atts, dz,
+        scratch=[((2, 16, 24, 768), BF16)], name="out_grads", us=0,
+    )
+    out_one, out_two, out_three = all_after(outs[1:], *datt[1:])
+    out_one, out_two = send(out_one, 2), send(out_two, 4)
+    f_now = after(f_now, *datt[1:])
+    (f_later,) = call(pass_on_k, [(f_later.shape, BF16)], ids, f_later, f_now, name="pass_f")
+    f_sent = send_z(f_later, 2)
+    dlin, conv_grad, *da1 = call(
+        attend_grad_k, [((1024, 576), BF16), ((3, 576), F32)] + blocks,
+        ids, prefix_len, *datt, after(q, f_later), k, v, att, lse, lin, kern, w_a, smem=2, name="attend_grad", us=1000,
+        scratch=[(heads, BF16), ((1032, 576), F32), ((256, 1024), F32), (heads, F32)]
+        + [((3, 64, 1024), F32)] * 2 + [tall],
+    )
+    outs = [outs[0], out_one, out_two, send(after(out_three, dlin), 6)]
+    o_keep, o_later, o_now = join_cores(ids, o_keep, after(o_away, dlin), "o")
+    o_now = send_z(o_now, 1)
+    r_keep, r_away = call(
+        proj_grads_k, [((16, 24, 640), BF16)] * 2, ids, after(a1, out_one, out_two, f_sent), dlin, conv_grad, up_bias_grad, out_bias_grad, gw,
+        scratch=[((2, 16, 24, 640), F32)], name="proj_grads", us=0,
+    )
+    da1, da1_one, da1_two = to_owners(ids, *da1)
+    da1 = [da1, send(da1_one, 2), send(da1_two, 4)]
+    r_keep, r_later, r_now = join_cores(ids, r_keep, r_away, "r")
+    r_now = send_z(r_now, 1)
+    (o_later,) = call(pass_on_k, [(o_later.shape, BF16)], ids, after(o_later, r_keep), o_now, name="pass_o")
+    o_sent = send_z(o_later, 2)
+    (r_later,) = call(pass_on_k, [(r_later.shape, BF16)], ids, r_later, r_now, name="pass_r")
+    rows = (128, 768)
+    out_keep, out_away = call(output_k, [(rows, BF16)] * 2, ids, *outs, after(x1, r_later), small, name="output")
+    o_parts = [o_keep, o_now, o_sent]
+    f_parts = [f_keep, f_now, f_sent]
+    r_parts = [r_keep, r_now, send_z(r_later, 2)]
+    down_grad, *sums = call(
+        sum_planes_k, [((96, 768), F32)] + [((24, 2176), BF16)] * 4, ids, *f_parts, *o_parts, *r_parts,
+        name="sum_planes",
+    )
+    sums = to_chips(sums)
+
+    out_recv = send(out_away, 1)
+    in_keep, in_away = call(input_grad_k, [(rows, F32)] * 2, ids, *da1, xw, after(dx, out_keep), small, name="input_grad")
+    in_recv = send(in_away, 1)
+    block_output, input_grad = call(
+        deliver_k, [((2, 1, 128, 768), BF16), ((2, 1, 128, 768), F32)],
+        ids, out_keep, out_recv, in_keep, in_recv, name="deliver", us=100,
+    )
+    vec = ((24,), F32)
+    gq, gk, gv, cq, ck, cv, go, gu, ga, gf, bo, bd, bu = call(
+        owned_k,
+        [((24, 768), F32)] * 3 + [((3, 24), F32)] * 3 + [((24, 768), F32), ((24, 3072), F32)]
+        + [vec] * 4 + [((96,), F32)],
+        ids, *sums, q_weight, k_weight, v_weight, up_weight, attn_gain, ffn_gain,
+        scratch=[((4, 24, 640), F32), ((4, 24, 768), F32)], name="owned", us=100,
+    )
+    return (
+        block_output, input_grad, ga, gq, gk, gv, cq, ck, cv, go, bo, gf, gu, bu, down_grad, bd,
+    )
+
+
 def solution(mesh):
+    plan = plane_shards if plane_plan(mesh) else general_shards
     in_specs = (
         P(None, "dp", "ctx", None),
         P(None, "dp", "ctx", None),
@@ -455,4 +1142,4 @@
         P(("dp", "ctx"), None),
         P(("dp", "ctx")),
     )
-    return jax.shard_map(shards, mesh=mesh, in_specs=in_specs, out_specs=out_specs, check_vma=False)
+    return jax.shard_map(plan, mesh=mesh, in_specs=in_specs, out_specs=out_specs, check_vma=False)

time: 1530 us -> 201 us (0.13)
  waiting for transfers between devices: 1040 us -> 67 us
  blocking collectives: 198 us -> 0 us
  matrix products: 94.1 us -> 0 us
  local copies, waits for them, and re-layouts: 96.2 us -> 6.3 us
  Pallas kernels: 0 us -> 68.6 us
  other arithmetic: 55.6 us -> 0.08 us
  starting transfers between devices: 9.58 us -> 57.3 us
    reduce_scatter x10 -> x0, waiting for transfers between devices: 706 us -> none  [the longest x1 142 us: shards(): lax.psum_scatter(totals[12], ('dp', 'ctx'), scatter_dimension=0, tiled=True)]
    all_gather x10 -> x0, waiting for transfers between devices: 329 us -> none  [the longest x1 62 us: shards(): lax.all_gather(down_weight, ('dp', 'ctx'), axis=0, tiled=True)]
    all_gather x3 -> x0, blocking collectives: 113 us -> none  [the longest x1 38.3 us: shards(): lax.all_gather(conv_q, ('dp', 'ctx'), axis=1, tiled=True)]
    dot_general x52 -> x0, matrix products: 94.1 us -> none  [the longest x8 18.9 us: outer_sum(): lax.dot_general(left, right, (((0,), (0,)), ((), ())), preferred_element_...]
    unnamed x2 -> x0, blocking collectives: 84.7 us -> none
    pallas_call x0 -> x31, Pallas kernels: none -> 68.6 us  [call(): pl.pallas_call(body, out_shape=out_shape, compiler_params=pltpu.CompilerP...]
    ppermute x4 -> x55, waiting for transfers between devices: 0.32 us -> 67 us  [the longest x43 51.3 us: send(): return lax.ppermute(value, ('dp', 'ctx'), pairs)]
    ppermute x4 -> x55, starting transfers between devices: 8.11 us -> 57.3 us  [the longest x43 40.1 us: send(): return lax.ppermute(value, ('dp', 'ctx'), pairs)]
  transfers between devices with their start and end apart: 24 -> 55, of which waited for: 20 -> 23; matrix products, arithmetic and copies ran while one was open for 11% -> 0% of each run, Pallas kernels for 0% -> 28%
where the time goes in v1:
time: 201 us; the launch traced here: 200 us
  Pallas kernels  68.6 us (34%)
  waiting for transfers between devices  67 us (33%)
  starting transfers between devices  57.3 us (29%)
  local copies, waits for them, and re-layouts  6.3 us (3%)
    pallas_call x31, Pallas kernels, call(): pl.pallas_call(body, out_shape=out_shape, compiler_params=pltpu.CompilerP...  68.6 us
    ppermute x43, waiting for transfers between devices, send(): return lax.ppermute(value, ('dp', 'ctx'), pairs)  51.3 us
    ppermute x43, starting transfers between devices, send(): return lax.ppermute(value, ('dp', 'ctx'), pairs)  40.1 us
    ppermute x12, starting transfers between devices, send_z(): return lax.ppermute(value, ('dp', 'ctx'), pairs)  17.2 us
    ppermute x12, waiting for transfers between devices, send_z(): return lax.ppermute(value, ('dp', 'ctx'), pairs)  15.7 us
    unnamed x51, local copies, waits for them, and re-layouts  6.24 us
  transfers between devices with their start and end apart: 55, of which 23 were waited for; matrix products, arithmetic and copies ran while one was open for 0% of the time, Pallas kernels for 28%

profile of v1, /device:TPU:0, one launch (start us, length us, event | category | flops | bytes accessed | tf_op | source)
XLA Modules:
  0.0 200.4 jit_solution(450264062826331154)
XLA Ops:
  1.2 1.9 pack.1
  3.1 2.6 %collective-permute-start = (bf16[24,2176]{1,0:T(8,128)(2,1)S(1)}, bf16[24,2176]{1,0:T(8,128)(2,1)S(1)}, u32[]{:S(2)}, u32[]{:S(2)}) collective-permute-start(bf16[24,2176]{1,0:T(8,128)(2,1)S(1)} %get-tuple-element.148), channel_id=1, source_target_pairs={{0,2},{1,3},{2,0},{3,1},{4,6},{5,7},{6,4},{7,5},{8,10},{9,11},{10,... | collective-permute-start | bytes 313352 | tf_op jit(solution)/shard_map/ppermute | solution.py:469
  5.7 1.5 collective-permute-start.1
  7.3 2.0 %collective-permute-done.p1 = bf16[24,2176]{1,0:T(8,128)(2,1)S(1)} collective-permute-done((bf16[24,2176]{1,0:T(8,128)(2,1)S(1)}, bf16[24,2176]{1,0:T(8,128)(2,1)S(1)}, u32[]{:S(2)}, u32[]{:S(2)}) %collective-permute-start) | collective-permute-done | bytes 104480 | tf_op jit(solution)/shard_map/ppermute | solution.py:469
  9.3 2.7 %collective-permute-done.1.p2 = bf16[24,2176]{1,0:T(8,128)(2,1)S(1)} collective-permute-done((bf16[24,2176]{1,0:T(8,128)(2,1)S(1)}, bf16[24,2176]{1,0:T(8,128)(2,1)S(1)}, u32[]{:S(2)}, u32[]{:S(2)}) %collective-permute-start.1) | collective-permute-done | bytes 104480 | tf_op jit(solution)/shard_map/ppermute | solution.py:469
  13.0 1.5 place_x.1.refs_2_.xw
  14.5 1.6 collective-permute-start.10
  16.1 1.2 collective-permute-start.9
  18.6 2.7 %collective-permute-start.4 = (bf16[4,24,640]{2,1,0:T(8,128)(2,1)S(1)}, bf16[4,24,640]{2,1,0:T(8,128)(2,1)S(1)}, u32[]{:S(2)}, u32[]{:S(2)}) collective-permute-start(bf16[4,24,640]{2,1,0:T(8,128)(2,1)S(1)} %get-tuple-element.151.s0), channel_id=1, source_target_pairs={{0,16},{1,17},{2,18},{3,19},{4,20},{5,21},{6,22},{7,23},{8,24},{9,... | collective-permute-start | bytes 368648 | tf_op jit(solution)/shard_map/ppermute | solution.py:475
  21.3 5.8 %collective-permute-done.4.s2 = bf16[4,24,640]{2,1,0:T(8,128)(2,1)S(1)} collective-permute-done((bf16[4,24,640]{2,1,0:T(8,128)(2,1)S(1)}, bf16[4,24,640]{2,1,0:T(8,128)(2,1)S(1)}, u32[]{:S(2)}, u32[]{:S(2)}) %collective-permute-start.4) | collective-permute-done | bytes 122912 | tf_op jit(solution)/shard_map/ppermute | solution.py:475
  27.8 1.4 collective-permute-start.3
  29.2 1.4 with_down.1.s0
  30.6 1.5 place_g.1.g0.gw.g
  32.8 1.3 collective-permute-done.3.s1
  34.8 3.3 %collective-permute-start.16 = (bf16[12,24,768]{2,1,0:T(8,128)(2,1)S(1)}, bf16[12,24,768]{2,1,0:T(8,128)(2,1)S(1)}, u32[]{:S(2)}, u32[]{:S(2)}) collective-permute-start(bf16[12,24,768]{2,1,0:T(8,128)(2,1)S(1)} %with_down.1.s0), channel_id=1, source_target_pairs={{0,16},{1,17},{2,18},{3,19},{4,20},{5,21},{6,22},{7,23},{8,24},{9,... | collective-permute-start | bytes 1327112 | tf_op jit(solution)/shard_map/ppermute | solution.py:475
  38.8 1.7 collective-permute-start.15
  42.0 1.5 collective-permute-start.18
  47.2 13.4 %attend.1 = (bf16[768,576]{1,0:T(8,128)(2,1)S(1)}, f32[1,768]{1,0:T(1,128)S(1)}, bf16[1024,768]{1,0:T(8,128)(2,1)S(1)}, f32[1032,576]{1,0:T(8,128)S(1)}, bf16[3,...) custom-call(s32[3]{0:T(128)S(1)} %pad_add_fusion.ids, ...), custom_call_target="tpu_custom_call" | custom-call | flops 1 | bytes 1 | tf_op jit(solution)/shard_map/attend/pallas_call | solution.py:454
  61.0 1.6 collective-permute-start.21
  63.1 1.5 collective-permute-start.13
  65.2 5.8 %collective-permute-done.13.t2 = bf16[256,192]{1,0:T(8,128)(2,1)S(1)} collective-permute-done((bf16[256,192]{1,0:T(8,128)(2,1)S(1)}, bf16[256,192]{1,0:T(8,128)(2,1)S(1)}, u32[]{:S(2)}, u32[]{:S(2)}) %collective-permute-start.13) | collective-permute-done | bytes 98336 | tf_op jit(solution)/shard_map/ppermute | solution.py:469
  71.0 1.1 collective-permute-done.19.s3
  72.1 1.1 stack_b.1.mine
  73.3 1.5 collective-permute-start.14
  74.8 2.2 %collective-permute-done.22.other = bf16[4,12,24,768]{3,2,1,0:T(8,128)(2,1)S(1)} collective-permute-done((bf16[4,12,24,768]{3,2,1,0:T(8,128)(2,1)S(1)}, bf16[4,12,24,768]{3,2,1,0:T(8,128)(2,1)S(1)}, u32[]{:S(2)}, u32[]{:S(2)}) %collective-permute-start.22) | collective-permute-done | bytes 1769504 | tf_op jit(solution)/shard_map/ppermute | solution.py:469
  77.9 2.3 %collective-permute-done.14.t3 = bf16[256,192]{1,0:T(8,128)(2,1)S(1)} collective-permute-done((bf16[256,192]{1,0:T(8,128)(2,1)S(1)}, bf16[256,192]{1,0:T(8,128)(2,1)S(1)}, u32[]{:S(2)}, u32[]{:S(2)}) %collective-permute-start.14) | collective-permute-done | bytes 98336 | tf_op jit(solution)/shard_map/ppermute | solution.py:469
  80.2 1.2 resid.1
  81.4 1.3 collective-permute-start.24
  83.5 8.7 %collective-permute-done.24.a2 = bf16[256,768]{1,0:T(8,128)(2,1)S(1)} collective-permute-done((bf16[256,768]{1,0:T(8,128)(2,1)S(1)}, bf16[256,768]{1,0:T(8,128)(2,1)S(1)}, u32[]{:S(2)}, u32[]{:S(2)}) %collective-permute-start.24) | collective-permute-done | bytes 393248 | tf_op jit(solution)/shard_map/ppermute | solution.py:469
  92.2 1.6 collective-permute-start.26
  94.3 2.7 %hidden_grad.1 = (bf16[1024,768]{1,0:T(8,128)(2,1)S(1)}, bf16[1024,768]{1,0:T(8,128)(2,1)S(1)}) custom-call(s32[3]{0:T(128)S(1)} %pad_add_fusion.ids, bf16[256,768]{1,0:T(8,128)(2,1)S(1)} %place_g.1.g0.gw.g, bf16[256,768]{1,0:T(8,128)(2,1)S(1)} %collective-permute-done.17.g1, bf16[256,768]{1,0:T(8,128)(2,1)S(1)} %collective-permute-done.18.g2, ...), custom_call_target="tpu_custom_call" | custom-call | flops 1 | bytes 1 | tf_op jit(solution)/shard_map/hidden_grad/pallas_call | solution.py:454
  97.9 1.6 collective-permute-done.25.a3
  99.5 4.7 %ffn.1 = (bf16[1024,768]{1,0:T(8,128)(2,1)S(1)}, bf16[1024,768]{1,0:T(8,128)(2,1)S(1)}, bf16[1024,768]{1,0:T(8,128)(2,1)S(1)}, bf16[256,768]{1,0:T(8,128)(2,1)S(...) custom-call(s32[3]{0:T(128)S(1)} %pad_add_fusion.ids, ...), custom_call_target="tpu_custom_call" | custom-call | flops 1 | bytes 1 | tf_op jit(solution)/shard_map/ffn/pallas_call | solution.py:454
  104.8 1.2 collective-permute-start.28
  106.0 3.9 %collective-permute-done.27.low = bf16[128,768]{1,0:T(8,128)(2,1)S(1)} collective-permute-done((bf16[128,768]{1,0:T(8,128)(2,1)S(1)}, bf16[128,768]{1,0:T(8,128)(2,1)S(1)}, u32[]{:S(2)}, u32[]{:S(2)}) %collective-permute-start.27) | collective-permute-done | bytes 196640 | tf_op jit(solution)/shard_map/ppermute | solution.py:469
  111.1 3.4 %ffn_grads.1 = (bf16[32,24,768]{2,1,0:T(8,128)(2,1)S(1)}, bf16[32,24,768]{2,1,0:T(8,128)(2,1)S(1)}, f32[1,768]{1,0:T(1,128)S(1)}) custom-call(s32[3]{0:T(128)S(1)} %pad_add_fusion.ids, bf16[1024,768]{1,0:T(8,128)(2,1)S(1)} %get-tuple-element.196.a_all, bf16[1024,768]{1,0:T(8,128)(2,1)S(1)} %get-tuple-element.197.g_all, ...), custom_call_target="tpu_custom_call" | custom-call | flops 99999997952 | bytes 1 | tf_op jit(solution)/shard_map/ffn_grads/pallas_call | solution.py:454
  114.5 1.6 collective-permute-start.29
  118.9 2.6 %ffn_out.1 = (bf16[256,768]{1,0:T(8,128)(2,1)S(1)}, bf16[256,768]{1,0:T(8,128)(2,1)}, bf16[256,768]{1,0:T(8,128)(2,1)}, bf16[256,768]{1,0:T(8,128)(2,1)S(1)}) custom-call(s32[3]{0:T(128)S(1)} %pad_add_fusion.ids, bf16[1024,768]{1,0:T(8,128)(2,1)S(1)} %get-tuple-element.188.hsq, bf16[768,768]{1,0:T(8,128)(2,1)S(1)} %bitcast.10), custom_call_target="tpu_custom_call" | custom-call | flops 99999997952 | bytes 1 | tf_op jit(solution)/shard_map/ffn_out/pallas_call | solution.py:454
  121.5 5.8 %collective-permute-done.30.p2 = bf16[256,768]{1,0:T(8,128)(2,1)S(1)} collective-permute-done((bf16[256,768]{1,0:T(8,128)(2,1)S(1)}, bf16[256,768]{1,0:T(8,128)(2,1)S(1)}, u32[]{:S(2)}, u32[]{:S(2)}) %collective-permute-start.30) | collective-permute-done | bytes 393248 | tf_op jit(solution)/shard_map/ppermute | solution.py:469
  127.3 1.4 mid_grad.1
  129.4 1.2 collective-permute-start.33
  130.6 1.7 collective-permute-start.34
  132.3 1.1 out_grads.1
  133.5 1.6 collective-permute-done.32.d1
  135.1 2.0 collective-permute-done.33.d2
  137.1 1.2 collective-permute-start.35
  139.2 1.3 pass_f.1
  142.3 13.3 %attend_grad.1 = (bf16[1024,576]{1,0:T(8,128)(2,1)S(1)}, f32[3,576]{1,0:T(4,128)S(1)}, bf16[256,768]{1,0:T(8,128)(2,1)S(1)}, bf16[256,768]{1,0:T(8,128)(2,1)S(1)...) custom-call(s32[3]{0:T(128)S(1)} %pad_add_fusion.ids, ...), custom_call_target="tpu_custom_call" | custom-call | flops 999999995904 | bytes 1 | tf_op jit(solution)/shard_map/attend_grad/pallas_call | solution.py:454
  155.7 2.1 %proj_grads.1 = (bf16[16,24,640]{2,1,0:T(8,128)(2,1)S(1)}, bf16[16,24,640]{2,1,0:T(8,128)(2,1)S(1)}) custom-call(s32[3]{0:T(128)S(1)} %pad_add_fusion.ids, bf16[1024,768]{1,0:T(8,128)(2,1)S(1)} %get-tuple-element.225.a1, bf16[1024,576]{1,0:T(8,128)(2,1)S(1)} %get-tuple-element.222.dlin, f32[3,576]{1,0:T(4,128)S(1)} %get-tuple-element.226.conv, ...), custom_call_target="tpu_custom_call" | custom-call | flops 1 | bytes 1 | tf_op jit(solution)/shard_map/proj_grads/pallas_call | solution.py:454
  158.3 1.1 collective-permute-start.43
  161.0 1.7 collective-permute-start.49
  162.8 1.4 collective-permute-start.38
  165.4 8.0 %collective-permute-done.44.high = bf16[128,768]{1,0:T(8,128)(2,1)S(1)} collective-permute-done((bf16[128,768]{1,0:T(8,128)(2,1)S(1)}, bf16[128,768]{1,0:T(8,128)(2,1)S(1)}, u32[]{:S(2)}, u32[]{:S(2)}) %collective-permute-start.44) | collective-permute-done | bytes 196640 | tf_op jit(solution)/shard_map/ppermute | solution.py:469
  174.0 1.1 collective-permute-start.45
  175.1 1.0 collective-permute-start.46
  176.8 3.2 %collective-permute-start.50 = (bf16[4,24,768]{2,1,0:T(8,128)(2,1)S(1)}, bf16[4,24,768]{2,1,0:T(8,128)(2,1)S(1)}, u32[]{:S(2)}, u32[]{:S(2)}) collective-permute-start(bf16[4,24,768]{2,1,0:T(8,128)(2,1)S(1)} %pass_o.1), channel_id=1, source_target_pairs={{0,16},{1,17},{2,18},{3,19},{4,20},{5,21},{6,22},{7,23},{8,24},{9,... | collective-permute-start | bytes 442376 | tf_op jit(solution)/shard_map/ppermute | solution.py:475
  180.6 5.3 %collective-permute-done.50.refs_5_ = bf16[4,24,768]{2,1,0:T(8,128)(2,1)S(1)} collective-permute-done((bf16[4,24,768]{2,1,0:T(8,128)(2,1)S(1)}, bf16[4,24,768]{2,1,0:T(8,128)(2,1)S(1)}, u32[]{:S(2)}, u32[]{:S(2)}) %collective-permute-start.50) | collective-permute-done | bytes 147488 | tf_op jit(solution)/shard_map/ppermute | solution.py:475
  186.0 1.3 collective-permute-done.51.refs_8_
  187.3 1.7 sum_planes.1
  190.0 1.5 collective-permute-start.53
  192.5 1.4 output.1
  195.6 1.4 collective-permute-done.54.s3
  197.1 1.6 owned.1
  198.7 1.6 deliver.1
  (133 shorter events, 32.5 us)
Async XLA Ops:
  0.6 12.4 %collective-permute-start.7 = (bf16[2,1,128,768]{3,2,1,0:T(8,128)(2,1)}, bf16[2,1,128,768]{3,2,1,0:T(8,128)(2,1)S(1)}, u32[]{:S(2)}, u32[]{:S(2)}) collective-permute-start(bf16[2,1,128,768]{3,2,1,0:T(8,128)(2,1)} %mine.3), channel_id=1, source_target_pairs={{0,1},{1,0},{2,3},{3,2},{4,5},{5,4},{6,7},{7,6},{8,9},{9,8},{10,11... | collective-permute-start | bytes 1179656 | tf_op jit(solution)/shard_map/ppermute | solution.py:469
  3.1 6.2 %collective-permute-start = (bf16[24,2176]{1,0:T(8,128)(2,1)S(1)}, bf16[24,2176]{1,0:T(8,128)(2,1)S(1)}, u32[]{:S(2)}, u32[]{:S(2)}) collective-permute-start(bf16[24,2176]{1,0:T(8,128)(2,1)S(1)} %get-tuple-element.148), channel_id=1, source_target_pairs={{0,2},{1,3},{2,0},{3,1},{4,6},{5,7},{6,4},{7,5},{8,10},{9,11},{10,... | collective-permute-start | bytes 313352 | tf_op jit(solution)/shard_map/ppermute | solution.py:469
  5.7 6.3 %collective-permute-start.1 = (bf16[24,2176]{1,0:T(8,128)(2,1)S(1)}, bf16[24,2176]{1,0:T(8,128)(2,1)S(1)}, u32[]{:S(2)}, u32[]{:S(2)}) collective-permute-start(bf16[24,2176]{1,0:T(8,128)(2,1)S(1)} %get-tuple-element.149), channel_id=1, source_target_pairs={{0,4},{1,5},{2,6},{3,7},{4,0},{5,1},{6,2},{7,3},{8,12},{9,13},{10,... | collective-permute-start | bytes 313352 | tf_op jit(solution)/shard_map/ppermute | solution.py:469
  7.3 5.7 %collective-permute-start.2 = (bf16[24,2176]{1,0:T(8,128)(2,1)S(1)}, bf16[24,2176]{1,0:T(8,128)(2,1)S(1)}, u32[]{:S(2)}, u32[]{:S(2)}) collective-permute-start(bf16[24,2176]{1,0:T(8,128)(2,1)S(1)} %get-tuple-element.150), channel_id=1, source_target_pairs={{0,6},{1,7},{2,4},{3,5},{4,2},{5,3},{6,0},{7,1},{8,14},{9,15},{10,... | collective-permute-start | bytes 313352 | tf_op jit(solution)/shard_map/ppermute | solution.py:469
  13.0 14.8 %collective-permute-start.6 = (bf16[2,1,128,768]{3,2,1,0:T(8,128)(2,1)}, bf16[2,1,128,768]{3,2,1,0:T(8,128)(2,1)S(1)}, u32[]{:S(2)}, u32[]{:S(2)}) collective-permute-start(bf16[2,1,128,768]{3,2,1,0:T(8,128)(2,1)} %mine.2), channel_id=1, source_target_pairs={{0,1},{1,0},{2,3},{3,2},{4,5},{5,4},{6,7},{7,6},{8,9},{9,8},{10,11... | collective-permute-start | bytes 1179656 | tf_op jit(solution)/shard_map/ppermute | solution.py:469
  14.5 23.6 %collective-permute-start.10 = (bf16[256,768]{1,0:T(8,128)(2,1)S(1)}, bf16[256,768]{1,0:T(8,128)(2,1)S(1)}, u32[]{:S(2)}, u32[]{:S(2)}) collective-permute-start(bf16[256,768]{1,0:T(8,128)(2,1)S(1)} %place_x.1.refs_2_.xw), channel_id=1, source_target_pairs={{0,6},{1,7},{2,4},{3,5},{4,2},{5,3},{6,0},{7,1},{8,14},{9,15},{10,... | collective-permute-start | bytes 1179656 | tf_op jit(solution)/shard_map/ppermute | solution.py:469
  16.1 24.5 %collective-permute-start.9 = (bf16[256,768]{1,0:T(8,128)(2,1)S(1)}, bf16[256,768]{1,0:T(8,128)(2,1)S(1)}, u32[]{:S(2)}, u32[]{:S(2)}) collective-permute-start(bf16[256,768]{1,0:T(8,128)(2,1)S(1)} %place_x.1.refs_2_.xw), channel_id=1, source_target_pairs={{0,4},{1,5},{2,6},{3,7},{4,0},{5,1},{6,2},{7,3},{8,12},{9,13},{10,... | collective-permute-start | bytes 1179656 | tf_op jit(solution)/shard_map/ppermute | solution.py:469
  17.3 24.0 %collective-permute-start.8 = (bf16[256,768]{1,0:T(8,128)(2,1)S(1)}, bf16[256,768]{1,0:T(8,128)(2,1)S(1)}, u32[]{:S(2)}, u32[]{:S(2)}) collective-permute-start(bf16[256,768]{1,0:T(8,128)(2,1)S(1)} %place_x.1.refs_2_.xw), channel_id=1, source_target_pairs={{0,2},{1,3},{2,0},{3,1},{4,6},{5,7},{6,4},{7,5},{8,10},{9,11},{10,... | collective-permute-start | bytes 1179656 | tf_op jit(solution)/shard_map/ppermute | solution.py:469
  18.6 25.5 %copy-start.24 = (s32[2,1]{0,1:T(1,128)S(1)}, s32[2,1]{0,1:T(1,128)}, u32[]{:S(2)}) copy-start(s32[2,1]{0,1:T(1,128)} %param.19) | copy-start | bytes 28
  18.6 8.5 %collective-permute-start.4 = (bf16[4,24,640]{2,1,0:T(8,128)(2,1)S(1)}, bf16[4,24,640]{2,1,0:T(8,128)(2,1)S(1)}, u32[]{:S(2)}, u32[]{:S(2)}) collective-permute-start(bf16[4,24,640]{2,1,0:T(8,128)(2,1)S(1)} %get-tuple-element.151.s0), channel_id=1, source_target_pairs={{0,16},{1,17},{2,18},{3,19},{4,20},{5,21},{6,22},{7,23},{8,24},{9,... | collective-permute-start | bytes 368648 | tf_op jit(solution)/shard_map/ppermute | solution.py:475
  27.1 5.7 %collective-permute-start.5 = (bf16[4,24,640]{2,1,0:T(8,128)(2,1)S(1)}, bf16[4,24,640]{2,1,0:T(8,128)(2,1)S(1)}, u32[]{:S(2)}, u32[]{:S(2)}) collective-permute-start(bf16[4,24,640]{2,1,0:T(8,128)(2,1)S(1)} %collective-permute-done.4.s2), channel_id=1, source_target_pairs={{0,8},{1,9},{2,10},{3,11},{4,12},{5,13},{6,14},{7,15},{8,0},{9,1},... | collective-permute-start | bytes 368648 | tf_op jit(solution)/shard_map/ppermute | solution.py:475
  27.8 6.3 %collective-permute-start.3 = (bf16[4,24,640]{2,1,0:T(8,128)(2,1)S(1)}, bf16[4,24,640]{2,1,0:T(8,128)(2,1)S(1)}, u32[]{:S(2)}, u32[]{:S(2)}) collective-permute-start(bf16[4,24,640]{2,1,0:T(8,128)(2,1)S(1)} %get-tuple-element.151.s0), channel_id=1, source_target_pairs={{0,8},{1,9},{2,10},{3,11},{4,12},{5,13},{6,14},{7,15},{8,0},{9,1},... | collective-permute-start | bytes 368648 | tf_op jit(solution)/shard_map/ppermute | solution.py:475
  34.7 9.5 %collective-permute-start.11 = (bf16[4,4,24,640]{3,2,1,0:T(8,128)(2,1)S(1)}, bf16[4,4,24,640]{3,2,1,0:T(8,128)(2,1)S(1)}, u32[]{:S(2)}, u32[]{:S(2)}) collective-permute-start(bf16[4,4,24,640]{3,2,1,0:T(8,128)(2,1)S(1)} %stack_a.1.refs_0_), channel_id=1, source_target_pairs={{0,1},{1,0},{2,3},{3,2},{4,5},{5,4},{6,7},{7,6},{8,9},{9,8},{10,11... | collective-permute-start | bytes 1474568 | tf_op jit(solution)/shard_map/ppermute | solution.py:469
  34.8 25.9 %collective-permute-start.16 = (bf16[12,24,768]{2,1,0:T(8,128)(2,1)S(1)}, bf16[12,24,768]{2,1,0:T(8,128)(2,1)S(1)}, u32[]{:S(2)}, u32[]{:S(2)}) collective-permute-start(bf16[12,24,768]{2,1,0:T(8,128)(2,1)S(1)} %with_down.1.s0), channel_id=1, source_target_pairs={{0,16},{1,17},{2,18},{3,19},{4,20},{5,21},{6,22},{7,23},{8,24},{9,... | collective-permute-start | bytes 1327112 | tf_op jit(solution)/shard_map/ppermute | solution.py:475
  38.8 21.8 %collective-permute-start.15 = (bf16[12,24,768]{2,1,0:T(8,128)(2,1)S(1)}, bf16[12,24,768]{2,1,0:T(8,128)(2,1)}, u32[]{:S(2)}, u32[]{:S(2)}) collective-permute-start(bf16[12,24,768]{2,1,0:T(8,128)(2,1)S(1)} %with_down.1.s0), channel_id=1, source_target_pairs={{0,8},{1,9},{2,10},{3,11},{4,12},{5,13},{6,14},{7,15},{8,0},{9,1},... | collective-permute-start | bytes 1327112 | tf_op jit(solution)/shard_map/ppermute | solution.py:475
  42.0 18.6 %collective-permute-start.18 = (bf16[256,768]{1,0:T(8,128)(2,1)S(1)}, bf16[256,768]{1,0:T(8,128)(2,1)S(1)}, u32[]{:S(2)}, u32[]{:S(2)}) collective-permute-start(bf16[256,768]{1,0:T(8,128)(2,1)S(1)} %place_g.1.g0.gw.g), channel_id=1, source_target_pairs={{0,4},{1,5},{2,6},{3,7},{4,0},{5,1},{6,2},{7,3},{8,12},{9,13},{10,... | collective-permute-start | bytes 1179656 | tf_op jit(solution)/shard_map/ppermute | solution.py:469
  43.6 17.1 %collective-permute-start.17 = (bf16[256,768]{1,0:T(8,128)(2,1)S(1)}, bf16[256,768]{1,0:T(8,128)(2,1)S(1)}, u32[]{:S(2)}, u32[]{:S(2)}) collective-permute-start(bf16[256,768]{1,0:T(8,128)(2,1)S(1)} %place_g.1.g0.gw.g), channel_id=1, source_target_pairs={{0,2},{1,3},{2,0},{3,1},{4,6},{5,7},{6,4},{7,5},{8,10},{9,11},{10,... | collective-permute-start | bytes 1179656 | tf_op jit(solution)/shard_map/ppermute | solution.py:469
  60.6 19.6 %copy-start.8 = (bf16[256,192]{1,0:T(8,128)(2,1)}, bf16[256,192]{1,0:T(8,128)(2,1)S(1)}, u32[]{:S(2)}) copy-start(bf16[256,192]{1,0:T(8,128)(2,1)S(1)} %get-tuple-element.159.t0) | copy-start | bytes 294916
  60.6 66.7 %copy-start.6 = (f32[16,768]{1,0:T(8,128)}, f32[16,768]{1,0:T(8,128)S(1)}, u32[]{:S(2)}) copy-start(f32[16,768]{1,0:T(8,128)S(1)} %get-tuple-element.173.small) | copy-start | bytes 147460
  60.7 11.5 %collective-permute-start.19 = (bf16[12,24,768]{2,1,0:T(8,128)(2,1)S(1)}, bf16[12,24,768]{2,1,0:T(8,128)(2,1)S(1)}, u32[]{:S(2)}, u32[]{:S(2)}) collective-permute-start(bf16[12,24,768]{2,1,0:T(8,128)(2,1)S(1)} %collective-permute-done.16.s2), channel_id=1, source_target_pairs={{0,8},{1,9},{2,10},{3,11},{4,12},{5,13},{6,14},{7,15},{8,0},{9,1},... | collective-permute-start | bytes 1327112 | tf_op jit(solution)/shard_map/ppermute | solution.py:475
  61.0 10.0 %collective-permute-start.21 = (bf16[128,768]{1,0:T(8,128)(2,1)S(1)}, bf16[128,768]{1,0:T(8,128)(2,1)S(1)}, u32[]{:S(2)}, u32[]{:S(2)}) collective-permute-start(bf16[128,768]{1,0:T(8,128)(2,1)S(1)} %slice.13), channel_id=1, source_target_pairs={{0,2},{1,3},{2,0},{3,1},{4,6},{5,7},{6,4},{7,5},{8,10},{9,11},{10,... | collective-permute-start | bytes 589832 | tf_op jit(solution)/shard_map/ppermute | solution.py:469
  62.6 8.4 %collective-permute-start.20 = (bf16[128,768]{1,0:T(8,128)(2,1)S(1)}, bf16[128,768]{1,0:T(8,128)(2,1)S(1)}, u32[]{:S(2)}, u32[]{:S(2)}) collective-permute-start(bf16[128,768]{1,0:T(8,128)(2,1)S(1)} %slice.12), channel_id=1, source_target_pairs={{0,4},{1,5},{2,6},{3,7},{4,0},{5,1},{6,2},{7,3},{8,12},{9,13},{10,... | collective-permute-start | bytes 589832 | tf_op jit(solution)/shard_map/ppermute | solution.py:469
  63.1 7.9 %collective-permute-start.13 = (bf16[256,192]{1,0:T(8,128)(2,1)S(1)}, bf16[256,192]{1,0:T(8,128)(2,1)S(1)}, u32[]{:S(2)}, u32[]{:S(2)}) collective-permute-start(bf16[256,192]{1,0:T(8,128)(2,1)S(1)} %get-tuple-element.161), channel_id=1, source_target_pairs={{0,4},{1,5},{2,6},{3,7},{4,0},{5,1},{6,2},{7,3},{8,12},{9,13},{10,... | collective-permute-start | bytes 294920 | tf_op jit(solution)/shard_map/ppermute | solution.py:469
  64.6 6.4 %collective-permute-start.12 = (bf16[256,192]{1,0:T(8,128)(2,1)S(1)}, bf16[256,192]{1,0:T(8,128)(2,1)S(1)}, u32[]{:S(2)}, u32[]{:S(2)}) collective-permute-start(bf16[256,192]{1,0:T(8,128)(2,1)S(1)} %get-tuple-element.160), channel_id=1, source_target_pairs={{0,2},{1,3},{2,0},{3,1},{4,6},{5,7},{6,4},{7,5},{8,10},{9,11},{10,... | collective-permute-start | bytes 294920 | tf_op jit(solution)/shard_map/ppermute | solution.py:469
  73.3 3.8 %collective-permute-start.22 = (bf16[4,12,24,768]{3,2,1,0:T(8,128)(2,1)S(1)}, bf16[4,12,24,768]{3,2,1,0:T(8,128)(2,1)S(1)}, u32[]{:S(2)}, u32[]{:S(2)}) collective-permute-start(bf16[4,12,24,768]{3,2,1,0:T(8,128)(2,1)S(1)} %stack_b.1.mine), channel_id=1, source_target_pairs={{0,1},{1,0},{2,3},{3,2},{4,5},{5,4},{6,7},{7,6},{8,9},{9,8},{10,11... | collective-permute-start | bytes 5308424 | tf_op jit(solution)/shard_map/ppermute | solution.py:469
  73.3 6.8 %collective-permute-start.14 = (bf16[256,192]{1,0:T(8,128)(2,1)S(1)}, bf16[256,192]{1,0:T(8,128)(2,1)S(1)}, u32[]{:S(2)}, u32[]{:S(2)}) collective-permute-start(bf16[256,192]{1,0:T(8,128)(2,1)S(1)} %get-tuple-element.163), channel_id=1, source_target_pairs={{0,6},{1,7},{2,4},{3,5},{4,2},{5,3},{6,0},{7,1},{8,14},{9,15},{10,... | collective-permute-start | bytes 294920 | tf_op jit(solution)/shard_map/ppermute | solution.py:469
  77.9 19.2 %copy-start = (bf16[32,24,768]{2,1,0:T(8,128)(2,1)}, bf16[32,24,768]{2,1,0:T(8,128)(2,1)S(1)}, u32[]{:S(2)}) copy-start(bf16[32,24,768]{2,1,0:T(8,128)(2,1)S(1)} %get-tuple-element.172) | copy-start | bytes 3538948
  80.2 14.2 %copy-start.10 = (bf16[256,192]{1,0:T(8,128)(2,1)}, bf16[256,192]{1,0:T(8,128)(2,1)S(1)}, u32[]{:S(2)}) copy-start(bf16[256,192]{1,0:T(8,128)(2,1)S(1)} %collective-permute-done.14.t3) | copy-start | bytes 294916
  81.4 45.9 %copy-start.2 = (f32[256,768]{1,0:T(8,128)}, f32[256,768]{1,0:T(8,128)S(1)}, u32[]{:S(2)}) copy-start(f32[256,768]{1,0:T(8,128)S(1)} %get-tuple-element.233.x1) | copy-start | bytes 2359300
  81.4 10.7 %collective-permute-start.24 = (bf16[256,768]{1,0:T(8,128)(2,1)S(1)}, bf16[256,768]{1,0:T(8,128)(2,1)S(1)}, u32[]{:S(2)}, u32[]{:S(2)}) collective-permute-start(bf16[256,768]{1,0:T(8,128)(2,1)S(1)} %get-tuple-element.174.a0), channel_id=1, source_target_pairs={{0,4},{1,5},{2,6},{3,7},{4,0},{5,1},{6,2},{7,3},{8,12},{9,13},{10,... | collective-permute-start | bytes 1179656 | tf_op jit(solution)/shard_map/ppermute | solution.py:469
  82.7 11.0 %collective-permute-start.23 = (bf16[256,768]{1,0:T(8,128)(2,1)S(1)}, bf16[256,768]{1,0:T(8,128)(2,1)S(1)}, u32[]{:S(2)}, u32[]{:S(2)}) collective-permute-start(bf16[256,768]{1,0:T(8,128)(2,1)S(1)} %get-tuple-element.174.a0), channel_id=1, source_target_pairs={{0,2},{1,3},{2,0},{3,1},{4,6},{5,7},{6,4},{7,5},{8,10},{9,11},{10,... | collective-permute-start | bytes 1179656 | tf_op jit(solution)/shard_map/ppermute | solution.py:469
  92.2 5.7 %collective-permute-start.26 = (bf16[128,768]{1,0:T(8,128)(2,1)S(1)}, bf16[128,768]{1,0:T(8,128)(2,1)S(1)}, u32[]{:S(2)}, u32[]{:S(2)}) collective-permute-start(bf16[128,768]{1,0:T(8,128)(2,1)S(1)} %slice.17), channel_id=1, source_target_pairs={{0,2},{1,3},{2,0},{3,1},{4,6},{5,7},{6,4},{7,5},{8,10},{9,11},{10,... | collective-permute-start | bytes 589832 | tf_op jit(solution)/shard_map/ppermute | solution.py:469
  93.8 5.7 %collective-permute-start.25 = (bf16[128,768]{1,0:T(8,128)(2,1)S(1)}, bf16[128,768]{1,0:T(8,128)(2,1)S(1)}, u32[]{:S(2)}, u32[]{:S(2)}) collective-permute-start(bf16[128,768]{1,0:T(8,128)(2,1)S(1)} %slice.16), channel_id=1, source_target_pairs={{0,4},{1,5},{2,6},{3,7},{4,0},{5,1},{6,2},{7,3},{8,12},{9,13},{10,... | collective-permute-start | bytes 589832 | tf_op jit(solution)/shard_map/ppermute | solution.py:469
  104.2 5.7 %collective-permute-start.27 = (bf16[128,768]{1,0:T(8,128)(2,1)S(1)}, bf16[128,768]{1,0:T(8,128)(2,1)S(1)}, u32[]{:S(2)}, u32[]{:S(2)}) collective-permute-start(bf16[128,768]{1,0:T(8,128)(2,1)S(1)} %get-tuple-element.183), channel_id=1, source_target_pairs={{0,2},{1,3},{2,0},{3,1},{4,6},{5,7},{6,4},{7,5},{8,10},{9,11},{10,... | collective-permute-start | bytes 589832 | tf_op jit(solution)/shard_map/ppermute | solution.py:469
  104.8 5.7 %collective-permute-start.28 = (bf16[128,768]{1,0:T(8,128)(2,1)S(1)}, bf16[128,768]{1,0:T(8,128)(2,1)S(1)}, u32[]{:S(2)}, u32[]{:S(2)}) collective-permute-start(bf16[128,768]{1,0:T(8,128)(2,1)S(1)} %get-tuple-element.184), channel_id=1, source_target_pairs={{0,4},{1,5},{2,6},{3,7},{4,0},{5,1},{6,2},{7,3},{8,12},{9,13},{10,... | collective-permute-start | bytes 589832 | tf_op jit(solution)/shard_map/ppermute | solution.py:469
  114.5 2.9 %collective-permute-start.31 = (bf16[32,24,768]{2,1,0:T(8,128)(2,1)S(1)}, bf16[32,24,768]{2,1,0:T(8,128)(2,1)S(1)}, u32[]{:S(2)}, u32[]{:S(2)}) collective-permute-start(bf16[32,24,768]{2,1,0:T(8,128)(2,1)S(1)} %get-tuple-element.200), channel_id=1, source_target_pairs={{0,1},{1,0},{2,3},{3,2},{4,5},{5,4},{6,7},{7,6},{8,9},{9,8},{10,11... | collective-permute-start | bytes 3538952 | tf_op jit(solution)/shard_map/ppermute | solution.py:469
  114.5 12.7 %collective-permute-start.29 = (bf16[256,768]{1,0:T(8,128)(2,1)S(1)}, bf16[256,768]{1,0:T(8,128)(2,1)S(1)}, u32[]{:S(2)}, u32[]{:S(2)}) collective-permute-start(bf16[256,768]{1,0:T(8,128)(2,1)S(1)} %get-tuple-element.187), channel_id=1, source_target_pairs={{0,2},{1,3},{2,0},{3,1},{4,6},{5,7},{6,4},{7,5},{8,10},{9,11},{10,... | collective-permute-start | bytes 1179656 | tf_op jit(solution)/shard_map/ppermute | solution.py:469
  116.1 11.2 %collective-permute-start.30 = (bf16[256,768]{1,0:T(8,128)(2,1)S(1)}, bf16[256,768]{1,0:T(8,128)(2,1)S(1)}, u32[]{:S(2)}, u32[]{:S(2)}) collective-permute-start(bf16[256,768]{1,0:T(8,128)(2,1)S(1)} %get-tuple-element.194), channel_id=1, source_target_pairs={{0,4},{1,5},{2,6},{3,7},{4,0},{5,1},{6,2},{7,3},{8,12},{9,13},{10,... | collective-permute-start | bytes 1179656 | tf_op jit(solution)/shard_map/ppermute | solution.py:469
  118.2 21.0 %collective-permute-start.37 = (bf16[2,8,24,768]{3,2,1,0:T(8,128)(2,1)S(1)}, bf16[2,8,24,768]{3,2,1,0:T(8,128)(2,1)S(1)}, u32[]{:S(2)}, u32[]{:S(2)}) collective-permute-start(bf16[2,8,24,768]{3,2,1,0:T(8,128)(2,1)S(1)} %get-tuple-element.212), channel_id=1, source_target_pairs={{0,8},{1,9},{2,10},{3,11},{4,12},{5,13},{6,14},{7,15},{8,0},{9,1},... | collective-permute-start | bytes 1769480 | tf_op jit(solution)/shard_map/ppermute | solution.py:475
  128.8 6.3 %collective-permute-start.32 = (bf16[256,192]{1,0:T(8,128)(2,1)S(1)}, bf16[256,192]{1,0:T(8,128)(2,1)S(1)}, u32[]{:S(2)}, u32[]{:S(2)}) collective-permute-start(bf16[256,192]{1,0:T(8,128)(2,1)S(1)} %get-tuple-element.203), channel_id=1, source_target_pairs={{0,2},{1,3},{2,0},{3,1},{4,6},{5,7},{6,4},{7,5},{8,10},{9,11},{10,... | collective-permute-start | bytes 294920 | tf_op jit(solution)/shard_map/ppermute | solution.py:469
  129.4 7.7 %collective-permute-start.33 = (bf16[256,192]{1,0:T(8,128)(2,1)S(1)}, bf16[256,192]{1,0:T(8,128)(2,1)S(1)}, u32[]{:S(2)}, u32[]{:S(2)}) collective-permute-start(bf16[256,192]{1,0:T(8,128)(2,1)S(1)} %get-tuple-element.204), channel_id=1, source_target_pairs={{0,4},{1,5},{2,6},{3,7},{4,0},{5,1},{6,2},{7,3},{8,12},{9,13},{10,... | collective-permute-start | bytes 294920 | tf_op jit(solution)/shard_map/ppermute | solution.py:469
  130.6 6.5 %collective-permute-start.34 = (bf16[256,192]{1,0:T(8,128)(2,1)S(1)}, bf16[256,192]{1,0:T(8,128)(2,1)S(1)}, u32[]{:S(2)}, u32[]{:S(2)}) collective-permute-start(bf16[256,192]{1,0:T(8,128)(2,1)S(1)} %get-tuple-element.205), channel_id=1, source_target_pairs={{0,6},{1,7},{2,4},{3,5},{4,2},{5,3},{6,0},{7,1},{8,14},{9,15},{10,... | collective-permute-start | bytes 294920 | tf_op jit(solution)/shard_map/ppermute | solution.py:469
  137.1 18.6 %collective-permute-start.35 = (bf16[256,768]{1,0:T(8,128)(2,1)}, bf16[256,768]{1,0:T(8,128)(2,1)}, u32[]{:S(2)}, u32[]{:S(2)}) collective-permute-start(bf16[256,768]{1,0:T(8,128)(2,1)} %get-tuple-element.206), channel_id=1, source_target_pairs={{0,2},{1,3},{2,0},{3,1},{4,6},{5,7},{6,4},{7,5},{8,10},{9,11},{10,... | collective-permute-start | bytes 1179656 | tf_op jit(solution)/shard_map/ppermute | solution.py:469
  138.2 17.4 %collective-permute-start.36 = (bf16[256,768]{1,0:T(8,128)(2,1)}, bf16[256,768]{1,0:T(8,128)(2,1)}, u32[]{:S(2)}, u32[]{:S(2)}) collective-permute-start(bf16[256,768]{1,0:T(8,128)(2,1)} %get-tuple-element.207), channel_id=1, source_target_pairs={{0,4},{1,5},{2,6},{3,7},{4,0},{5,1},{6,2},{7,3},{8,12},{9,13},{10,... | collective-permute-start | bytes 1179656 | tf_op jit(solution)/shard_map/ppermute | solution.py:469
  141.3 14.4 %collective-permute-start.39 = (bf16[8,24,768]{2,1,0:T(8,128)(2,1)}, bf16[8,24,768]{2,1,0:T(8,128)(2,1)}, u32[]{:S(2)}, u32[]{:S(2)}) collective-permute-start(bf16[8,24,768]{2,1,0:T(8,128)(2,1)} %pass_f.1), channel_id=1, source_target_pairs={{0,16},{1,17},{2,18},{3,19},{4,20},{5,21},{6,22},{7,23},{8,24},{9,... | collective-permute-start | bytes 884744 | tf_op jit(solution)/shard_map/ppermute | solution.py:475
  155.6 4.8 %collective-permute-start.48 = (bf16[16,24,768]{2,1,0:T(8,128)(2,1)S(1)}, bf16[16,24,768]{2,1,0:T(8,128)(2,1)S(1)}, u32[]{:S(2)}, u32[]{:S(2)}) collective-permute-start(bf16[16,24,768]{2,1,0:T(8,128)(2,1)S(1)} %get-tuple-element.254), channel_id=1, source_target_pairs={{0,1},{1,0},{2,3},{3,2},{4,5},{5,4},{6,7},{7,6},{8,9},{9,8},{10,11... | collective-permute-start | bytes 1769480 | tf_op jit(solution)/shard_map/ppermute | solution.py:469
  157.8 6.4 %collective-permute-start.40 = (bf16[16,24,640]{2,1,0:T(8,128)(2,1)S(1)}, bf16[16,24,640]{2,1,0:T(8,128)(2,1)S(1)}, u32[]{:S(2)}, u32[]{:S(2)}) collective-permute-start(bf16[16,24,640]{2,1,0:T(8,128)(2,1)S(1)} %get-tuple-element.230), channel_id=1, source_target_pairs={{0,1},{1,0},{2,3},{3,2},{4,5},{5,4},{6,7},{7,6},{8,9},{9,8},{10,11... | collective-permute-start | bytes 1474568 | tf_op jit(solution)/shard_map/ppermute | solution.py:469
  158.3 7.0 %collective-permute-start.43 = (bf16[128,768]{1,0:T(8,128)(2,1)S(1)}, bf16[128,768]{1,0:T(8,128)(2,1)S(1)}, u32[]{:S(2)}, u32[]{:S(2)}) collective-permute-start(bf16[128,768]{1,0:T(8,128)(2,1)S(1)} %get-tuple-element.239), channel_id=1, source_target_pairs={{0,2},{1,3},{2,0},{3,1},{4,6},{5,7},{6,4},{7,5},{8,10},{9,11},{10,... | collective-permute-start | bytes 589832 | tf_op jit(solution)/shard_map/ppermute | solution.py:469
  159.4 14.0 %collective-permute-start.44 = (bf16[128,768]{1,0:T(8,128)(2,1)S(1)}, bf16[128,768]{1,0:T(8,128)(2,1)S(1)}, u32[]{:S(2)}, u32[]{:S(2)}) collective-permute-start(bf16[128,768]{1,0:T(8,128)(2,1)S(1)} %get-tuple-element.240), channel_id=1, source_target_pairs={{0,4},{1,5},{2,6},{3,7},{4,0},{5,1},{6,2},{7,3},{8,12},{9,13},{10,... | collective-permute-start | bytes 589832 | tf_op jit(solution)/shard_map/ppermute | solution.py:469
  161.0 15.2 %collective-permute-start.49 = (bf16[2,4,24,768]{3,2,1,0:T(8,128)(2,1)S(1)}, bf16[2,4,24,768]{3,2,1,0:T(8,128)(2,1)S(1)}, u32[]{:S(2)}, u32[]{:S(2)}) collective-permute-start(bf16[2,4,24,768]{3,2,1,0:T(8,128)(2,1)S(1)} %get-tuple-element.256), channel_id=1, source_target_pairs={{0,8},{1,9},{2,10},{3,11},{4,12},{5,13},{6,14},{7,15},{8,0},{9,1},... | collective-permute-start | bytes 884744 | tf_op jit(solution)/shard_map/ppermute | solution.py:475
  162.8 28.7 %collective-permute-start.38 = (bf16[256,768]{1,0:T(8,128)(2,1)S(1)}, bf16[256,768]{1,0:T(8,128)(2,1)S(1)}, u32[]{:S(2)}, u32[]{:S(2)}) collective-permute-start(bf16[256,768]{1,0:T(8,128)(2,1)S(1)} %get-tuple-element.223), channel_id=1, source_target_pairs={{0,6},{1,7},{2,4},{3,5},{4,2},{5,3},{6,0},{7,1},{8,14},{9,15},{10,... | collective-permute-start | bytes 1179656 | tf_op jit(solution)/shard_map/ppermute | solution.py:469
  164.2 23.1 %copy-start.5 = (bf16[2,8,24,768]{3,2,1,0:T(8,128)(2,1)S(1)}, bf16[2,8,24,768]{3,2,1,0:T(8,128)(2,1)}, u32[]{:S(2)}) copy-start(bf16[2,8,24,768]{3,2,1,0:T(8,128)(2,1)} %copy-done.4) | copy-start | bytes 1769476
  164.8 15.1 %collective-permute-start.41 = (bf16[2,4,24,640]{3,2,1,0:T(8,128)(2,1)S(1)}, bf16[2,4,24,640]{3,2,1,0:T(8,128)(2,1)S(1)}, u32[]{:S(2)}, u32[]{:S(2)}) collective-permute-start(bf16[2,4,24,640]{3,2,1,0:T(8,128)(2,1)S(1)} %get-tuple-element.232), channel_id=1, source_target_pairs={{0,8},{1,9},{2,10},{3,11},{4,12},{5,13},{6,14},{7,15},{8,0},{9,1},... | collective-permute-start | bytes 737288 | tf_op jit(solution)/shard_map/ppermute | solution.py:475
  174.0 20.0 %collective-permute-start.45 = (bf16[256,768]{1,0:T(8,128)(2,1)S(1)}, bf16[256,768]{1,0:T(8,128)(2,1)S(1)}, u32[]{:S(2)}, u32[]{:S(2)}) collective-permute-start(bf16[256,768]{1,0:T(8,128)(2,1)S(1)} %get-tuple-element.243), channel_id=1, source_target_pairs={{0,2},{1,3},{2,0},{3,1},{4,6},{5,7},{6,4},{7,5},{8,10},{9,11},{10,... | collective-permute-start | bytes 1179656 | tf_op jit(solution)/shard_map/ppermute | solution.py:469
  175.1 18.9 %collective-permute-start.46 = (bf16[256,768]{1,0:T(8,128)(2,1)S(1)}, bf16[256,768]{1,0:T(8,128)(2,1)S(1)}, u32[]{:S(2)}, u32[]{:S(2)}) collective-permute-start(bf16[256,768]{1,0:T(8,128)(2,1)S(1)} %get-tuple-element.244), channel_id=1, source_target_pairs={{0,4},{1,5},{2,6},{3,7},{4,0},{5,1},{6,2},{7,3},{8,12},{9,13},{10,... | collective-permute-start | bytes 1179656 | tf_op jit(solution)/shard_map/ppermute | solution.py:469
  176.2 16.3 %copy-start.3 = (f32[256,768]{1,0:T(8,128)S(1)}, f32[256,768]{1,0:T(8,128)}, u32[]{:S(2)}) copy-start(f32[256,768]{1,0:T(8,128)} %copy-done.2) | copy-start | bytes 2359300
  176.2 16.3 %copy-start.7 = (f32[16,768]{1,0:T(8,128)S(1)}, f32[16,768]{1,0:T(8,128)}, u32[]{:S(2)}) copy-start(f32[16,768]{1,0:T(8,128)} %copy-done.6) | copy-start | bytes 147460
  176.8 9.2 %collective-permute-start.50 = (bf16[4,24,768]{2,1,0:T(8,128)(2,1)S(1)}, bf16[4,24,768]{2,1,0:T(8,128)(2,1)S(1)}, u32[]{:S(2)}, u32[]{:S(2)}) collective-permute-start(bf16[4,24,768]{2,1,0:T(8,128)(2,1)S(1)} %pass_o.1), channel_id=1, source_target_pairs={{0,16},{1,17},{2,18},{3,19},{4,20},{5,21},{6,22},{7,23},{8,24},{9,... | collective-permute-start | bytes 442376 | tf_op jit(solution)/shard_map/ppermute | solution.py:475
  180.5 6.8 %collective-permute-start.51 = (bf16[4,24,640]{2,1,0:T(8,128)(2,1)S(1)}, bf16[4,24,640]{2,1,0:T(8,128)(2,1)S(1)}, u32[]{:S(2)}, u32[]{:S(2)}) collective-permute-start(bf16[4,24,640]{2,1,0:T(8,128)(2,1)S(1)} %pass_r.1), channel_id=1, source_target_pairs={{0,16},{1,17},{2,18},{3,19},{4,20},{5,21},{6,22},{7,23},{8,24},{9,... | collective-permute-start | bytes 368648 | tf_op jit(solution)/shard_map/ppermute | solution.py:475
  189.0 6.6 %collective-permute-start.52 = (bf16[24,2176]{1,0:T(8,128)(2,1)S(1)}, bf16[24,2176]{1,0:T(8,128)(2,1)S(1)}, u32[]{:S(2)}, u32[]{:S(2)}) collective-permute-start(bf16[24,2176]{1,0:T(8,128)(2,1)S(1)} %get-tuple-element.261), channel_id=1, source_target_pairs={{0,2},{1,3},{2,0},{3,1},{4,6},{5,7},{6,4},{7,5},{8,10},{9,11},{10,... | collective-permute-start | bytes 313352 | tf_op jit(solution)/shard_map/ppermute | solution.py:469
  190.0 5.6 %collective-permute-start.53 = (bf16[24,2176]{1,0:T(8,128)(2,1)S(1)}, bf16[24,2176]{1,0:T(8,128)(2,1)S(1)}, u32[]{:S(2)}, u32[]{:S(2)}) collective-permute-start(bf16[24,2176]{1,0:T(8,128)(2,1)S(1)} %get-tuple-element.262), channel_id=1, source_target_pairs={{0,4},{1,5},{2,6},{3,7},{4,0},{5,1},{6,2},{7,3},{8,12},{9,13},{10,... | collective-permute-start | bytes 313352 | tf_op jit(solution)/shard_map/ppermute | solution.py:469
  191.5 5.6 %collective-permute-start.54 = (bf16[24,2176]{1,0:T(8,128)(2,1)S(1)}, bf16[24,2176]{1,0:T(8,128)(2,1)S(1)}, u32[]{:S(2)}, u32[]{:S(2)}) collective-permute-start(bf16[24,2176]{1,0:T(8,128)(2,1)S(1)} %get-tuple-element.263), channel_id=1, source_target_pairs={{0,6},{1,7},{2,4},{3,5},{4,2},{5,3},{6,0},{7,1},{8,14},{9,15},{10,... | collective-permute-start | bytes 313352 | tf_op jit(solution)/shard_map/ppermute | solution.py:469
  194.0 4.7 %collective-permute-start.42 = (bf16[128,768]{1,0:T(8,128)(2,1)S(1)}, bf16[128,768]{1,0:T(8,128)(2,1)S(1)}, u32[]{:S(2)}, u32[]{:S(2)}) collective-permute-start(bf16[128,768]{1,0:T(8,128)(2,1)S(1)} %get-tuple-element.235), channel_id=1, source_target_pairs={{0,1},{1,0},{2,3},{3,2},{4,5},{5,4},{6,7},{7,6},{8,9},{9,8},{10,11... | collective-permute-start | bytes 589832 | tf_op jit(solution)/shard_map/ppermute | solution.py:469
  195.1 3.6 %collective-permute-start.47 = (f32[128,768]{1,0:T(8,128)S(1)}, f32[128,768]{1,0:T(8,128)S(1)}, u32[]{:S(2)}, u32[]{:S(2)}) collective-permute-start(f32[128,768]{1,0:T(8,128)S(1)} %get-tuple-element.248), channel_id=1, source_target_pairs={{0,1},{1,0},{2,3},{3,2},{4,5},{5,4},{6,7},{7,6},{8,9},{9,8},{10,11... | collective-permute-start | bytes 1179656 | tf_op jit(solution)/shard_map/ppermute | solution.py:469
  (16 other events, 44.1 us)

commit v2 on v1

--- a/solution.py
+++ b/solution.py
@@ -487,12 +487,6 @@
     return [blocks[0]] + [send(blocks[j], 2 * j) for j in range(1, CHIPS)]
 
 
-def to_all_planes(ids, block, *first, direct=False):
-    two, one = send_z(block, 2), send_z(block, 1)
-    three = send_z(block, 3) if direct else send_z(after(two, *first), 1)
-    return call(stack_k, [((4, *block.shape), block.dtype)], ids, block, one, two, three, name="stack")[0]
-
-
 def stack_k(ids, s0, s1, s2, s3, out):
     for r, ref in enumerate((s0, s1, s2, s3)):
         out[r] = ref[...]
@@ -512,7 +506,7 @@
 def join_cores(ids, keep, away, name):
     size = (keep.shape[0] // 4, *keep.shape[1:])
     return call(
-        join_k, [(size, BF16)] * 2 + [((2, *size), BF16)], ids, keep, send(away, 1), name="join_" + name
+        join_k, [(size, BF16)] * 2 + [((2, *size), BF16)], ids, keep, away, name="join_" + name
     )
 
 
@@ -585,12 +579,13 @@
 
 
 def with_down_k(ids, b, wd, b_out, sems):
+    n = b.shape[0]
     copies = [
-        pltpu.make_async_copy(wd.at[24 * j : 24 * j + 24, :], b_out.at[8 + j], sems.at[j]) for j in range(CHIPS)
+        pltpu.make_async_copy(wd.at[24 * j : 24 * j + 24, :], b_out.at[n + j], sems.at[j]) for j in range(CHIPS)
     ]
     for copy in copies:
         copy.start()
-    b_out[0:8] = b[...]
+    b_out[0:n] = b[...]
     for copy in copies:
         copy.wait()
 
@@ -610,12 +605,7 @@
     for ref, (lo, hi) in zip((g0, g1, g2, g3, g4), ROWS):
         g_all[lo:hi, :] = ref[...]
 
-    def block(j, carry):
-        at = pl.ds(pl.multiple_of(256 * j, 256), 256)
-        dh[at, :] = dot_nt(g_all[at, :], wd[...]).astype(BF16)
-        return carry
-
-    lax.fori_loop(0, 4, block, 0)
+    dh[...] = dot_nt(g_all[...], wd[...]).astype(BF16)
 
 
 def mask_rows(b, prefix, out):
@@ -629,9 +619,10 @@
 def attend_k(
     ids, pre, *refs,
 ):
-    pieces, xs = refs[:2], refs[2:6]
-    w_out, bias_out, a_out, lin, q_out, k_out, v_out, o0, o1, o2, o3, att, lse, small_out, kern_out = refs[6:21]
-    w_scr, stage, mask, mixed = refs[21:]
+    n_x = len(refs) - 21
+    pieces, xs, refs = refs[:2], refs[2 : 2 + n_x], refs[2 + n_x :]
+    w_out, bias_out, a_out, lin, q_out, k_out, v_out, o0, o1, o2, o3, att, lse, small_out, kern_out = refs[:15]
+    w_scr, stage, mask, mixed = refs[15:]
     z, k, c = ids[0], ids[1], ids[2]
     prefix = pre[c, 0]
     for core in range(2):
@@ -655,18 +646,13 @@
     kern = jnp.concatenate([own[0:3], own[3:6], own[6:9]], axis=1)
     kern_out[...] = kern
     lin[0:8, :] = jnp.zeros((8, lin.shape[1]), F32)
-    for j, ref in enumerate(xs):
-        at = pl.multiple_of((k ^ j) * 256, 256)
+    for ref, (lo, hi) in zip(xs, ROWS if n_x == 5 else ROWS[:3] + ((768, 1024),)):
+        at = pl.multiple_of((k ^ (lo // 256)) * 256 + lo % 256, 128)
         x = ref[...].astype(F32)
         factor = lax.rsqrt(jnp.mean(x * x, axis=-1, keepdims=True) + EPS)
-        a_out[pl.ds(at, 256), :] = (x * factor * gain).astype(BF16)
-
-    def project(b, carry):
-        at = pl.multiple_of(256 * b, 256)
-        lin[pl.ds(pl.multiple_of(at + 8, 8), 256), :] = dot_nn(a_out[pl.ds(at, 256), :], w_out[...])
-        return carry
-
-    lax.fori_loop(0, 4, project, 0)
+        a_out[pl.ds(at, hi - lo), :] = (x * factor * gain).astype(BF16)
+
+    lin[8:1032, :] = dot_nn(a_out[...], w_out[...])
     for b in range(4):
         t = 256 * b
         mixed[...] = (
@@ -683,17 +669,13 @@
         t = 256 * b
         cols = mask_rows(b, prefix, mask)
 
-        def one_head(h, carry, t=t, cols=cols):
+        for h in range(3):
             scores = dot_nt(q_out[h, t : t + 256, :], k_out[h, 0:cols, :]) + mask[:, :cols]
             top = jnp.max(scores, axis=-1, keepdims=True)
             weight = jnp.exp(scores - top)
             total = jnp.sum(weight, axis=-1, keepdims=True)
-            probs = (weight * (1.0 / total)).astype(BF16)
-            att[h, t : t + 256, :] = dot_nn(probs, v_out[h, 0:cols, :])
+            att[h, t : t + 256, :] = dot_nn(weight.astype(BF16), v_out[h, 0:cols, :]) * (1.0 / total)
             lse[h, t : t + 256, :] = top + jnp.log(total)
-            return carry
-
-        lax.fori_loop(0, 3, one_head, 0)
         stage[b] = jnp.concatenate([att[h, t : t + 256, :] for h in range(3)], axis=1).astype(BF16)
     for j, out in enumerate((o0, o1, o2, o3)):
         out[...] = stage[k ^ j]
@@ -710,20 +692,17 @@
     a2_out[...] = (total * factor * small[11:12]).astype(BF16)
 
 
-def ffn_k(ids, a0, a1, a2, a3, a4, dh, up, bias, hsq, du, a_all, p0, p1, p2, p3, p4, stage):
-    for ref, (lo, hi) in zip((a0, a1, a2, a3, a4), ROWS):
+def ffn_k(ids, *refs):
+    n_a = len(refs) - 12
+    blocks, refs = refs[:n_a], refs[n_a:]
+    dh, up, bias, hsq, du, a_all, p0, p1, p2, p3, p4, stage = refs
+    for ref, (lo, hi) in zip(blocks, ROWS if n_a == 5 else ROWS[:3] + ((768, 1024),)):
         a_all[lo:hi, :] = ref[...]
 
-    def block(j, carry):
-        at = pl.ds(pl.multiple_of(256 * j, 256), 256)
-        act = jax.nn.relu(dot_nn(a_all[at, :], up[...]) + bias[...])
-        hsq[at, :] = (act * act).astype(BF16)
-        low = (dh[at, :].astype(F32) * 2.0 * act).astype(BF16)
-        du[at, :] = low
-        stage[at, :] = dot_nt(low, up[...]).astype(BF16)
-        return carry
-
-    lax.fori_loop(0, 4, block, 0)
+    act = jax.nn.relu(dot_nn(a_all[...], up[...]) + bias[...])
+    hsq[...] = (act * act).astype(BF16)
+    du[...] = (dh[...].astype(F32) * 2.0 * act).astype(BF16)
+    stage[...] = dot_nt(du[...], up[...]).astype(BF16)
     for ref, (lo, hi) in zip((p0, p1, p2, p3, p4), ROWS):
         ref[...] = stage[lo:hi, :]
 
@@ -813,7 +792,7 @@
         t = 256 * b
         cols = mask_rows(b, prefix, mask)
 
-        def one_head(h, carry, b=b, t=t, cols=cols):
+        for h in range(3):
             q_rows, do_rows = q_in[h, t : t + 256, :], do_scr[h, t : t + 256, :]
             scores = dot_nt(q_rows, k_in[h, 0:cols, :]) + mask[:, :cols]
             probs = jnp.exp(scores - lse[h, t : t + 256, :])
@@ -829,9 +808,6 @@
             else:
                 dk[h, :, 0:cols] = dk[h, :, 0:cols] + dk_part
                 dv[h, :, 0:cols] = dv[h, :, 0:cols] + dv_part
-            return carry
-
-        lax.fori_loop(0, 3, one_head, 0)
     for h in range(3):
         dm[0:1024, 64 * h : 64 * h + 64] = dq[h]
         dm[0:1024, 192 + 64 * h : 256 + 64 * h] = dk[h].T
@@ -850,14 +826,10 @@
             )
     conv_out[...] = jnp.concatenate(sums, axis=0)
 
-    def block(j, carry):
-        rows = dlin_out[pl.ds(pl.multiple_of((k ^ j) * 256, 256), 256), :]
-        stage[pl.ds(pl.multiple_of(256 * j, 256), 256), :] = dot_nt(rows, w[...]).astype(BF16)
-        return carry
-
-    lax.fori_loop(0, 4, block, 0)
+    stage[...] = dot_nt(dlin_out[...], w[...]).astype(BF16)
     for ref, (lo, hi) in zip((p0, p1, p2, p3, p4), ROWS):
-        ref[...] = stage[lo:hi, :]
+        at = pl.multiple_of((k ^ (lo // 256)) * 256 + lo % 256, 128)
+        ref[...] = stage[pl.ds(at, hi - lo), :]
 
 
 def proj_grads_k(ids, a1, dlin, conv, up_bias, out_bias, g, keep, away, stage):
@@ -959,148 +931,108 @@
     bu[...] = jnp.concatenate([extra[i : i + 1, 80:104] for i in range(4)], axis=1).reshape(96)
 
 
-def plane_shards(
-    block_input, out_grad, prefix_len, attn_gain, q_weight, k_weight, v_weight, conv_q, conv_k, conv_v,
-    out_weight, out_bias, ffn_gain, up_weight, up_bias, down_weight, down_bias,
-):
-    z, place = lax.axis_index("dp"), lax.axis_index("ctx")
+def plane_shards(block_input, out_grad, prefix_len, attn_gain, q_weight, k_weight, v_weight, conv_q, conv_k, conv_v, out_weight, out_bias, ffn_gain, up_weight, up_bias, down_weight, down_bias):
+    z, place = (lax.axis_index('dp'), lax.axis_index('ctx'))
     ids = jnp.stack([z, place // 2, place % 2]).astype(jnp.int32)
-    block, half = ((256, 768), BF16), ((128, 768), BF16)
+    block, half = (((256, 768), BF16), ((128, 768), BF16))
     blocks = [block] * 3 + [half] * 2
-    tall, heads = ((1024, 768), BF16), (3, 1024, 64)
-
+    tall, heads = (((1024, 768), BF16), (3, 1024, 64))
+    rows = (128, 768)
     sem = pltpu.SemaphoreType.DMA
     x_peer = send(block_input, 1)
-    weights = (
-        q_weight, k_weight, v_weight, up_weight, out_weight, attn_gain, conv_q, conv_k, conv_v, out_bias,
-        ffn_gain, down_bias, up_bias,
-    )
-    packs = call(
-        pack_k, [((24, 2176), BF16)] * 4, ids, *weights, hbm=13,
-        scratch=[((4, 24, 2176), BF16)] + [(w.shape, BF16) for w in weights] + [sem((13,))], name="pack",
-    )
+    weights = (q_weight, k_weight, v_weight, up_weight, out_weight, attn_gain, conv_q, conv_k, conv_v, out_bias, ffn_gain, down_bias, up_bias)
+    packs = call(pack_k, [((24, 2176), BF16)] * 4, ids, *weights, hbm=13, scratch=[((4, 24, 2176), BF16)] + [(w.shape, BF16) for w in weights] + [sem((13,))], name='pack')
     packs = to_chips(packs)
-    x_peer = after(x_peer, *packs[1:])
-    (xw,) = call(place_k, [block], ids, x_peer, block_input, hbm=1, scratch=[sem(())], name="place_x")
-    xs = to_chips([xw] * 4)
-    a_own, b_own = call(split_k, [((4, 24, 640), BF16), ((8, 24, 768), BF16)], ids, *packs, name="split")
-    a_two, a_one = send_z(a_own, 2), send_z(a_own, 1)
-    a_three = send_z(a_two, 1)
-    (b_own,) = call(
-        with_down_k, [((12, 24, 768), BF16)], ids, after(b_own, a_two), down_weight, hbm=1, scratch=[sem((4,))],
-        name="with_down",
-    )
-
+    x_peer = after(x_peer, *packs[1:2])
+    xw, = call(place_k, [block], ids, x_peer, block_input, hbm=1, scratch=[sem(())], name='place_x')
+    x_one, x_two = (send(xw, 2), send(xw, 4))
+    a_own, b_own = call(split_k, [((4, 24, 640), BF16), ((8, 24, 768), BF16)], ids, *packs, name='split')
+    a_two, a_one = (send_z(a_own, 2), send_z(a_own, 1))
+    a_three = send_z(a_own, 3)
+    x_low, x_high = (send(part, bits) for part, bits in zip(all_after([x_one[:128], x_two[128:]], a_two), (4, 2)))
+    xs = [xw, x_one, x_two, x_low, x_high]
+    bdep = ()
+    b_own, = call(with_down_k, [((12, 24, 768), BF16)], ids, after(b_own, *bdep), down_weight, hbm=1, scratch=[sem((4,))], name='with_down')
+    wd_dep = b_own
     g_peer = send(after(out_grad, *packs[1:]), 1)
-    (gw,) = call(place_k, [block], ids, g_peer, out_grad, hbm=1, scratch=[sem(())], name="place_g")
-    (a_all,) = call(stack_k, [((4, 4, 24, 640), BF16)], ids, a_own, a_one, a_two, after(a_three, b_own, gw), name="stack_a")
+    gw, = call(place_k, [block], ids, g_peer, out_grad, hbm=1, scratch=[sem(())], name='place_g')
+    a_last = after(a_three, wd_dep)
+    a_all, = call(stack_k, [((4, 4, 24, 640), BF16)], ids, a_own, a_one, a_two, a_last, name='stack_a')
     a_peer = send(a_all, 1)
     b_own = after(b_own, a_three)
-    b_one, b_two = send_z(b_own, 1), send_z(b_own, 2)
-    gw = after(gw, *xs[1:])
-    g_one, g_two = send(gw, 2), send(gw, 4)
-
-    w_a, up_bias_row, a1, lin, q, k, v, t0, t1, t2, t3, att, lse, small, kern = call(
-        attend_k,
-        [((768, 576), BF16), ((1, 768), F32), tall, ((1032, 576), F32)]
-        + [(heads, BF16)] * 3 + [((256, 192), BF16)] * 4
-        + [(heads, F32), ((3, 1024, 1), F32), ((16, 768), F32), ((3, 576), F32)],
-        ids, prefix_len, after(a_all, gw), a_peer, *xs,
-        smem=2, name="attend", us=0,
-        scratch=[((32, 24, 640), F32), ((4, 256, 192), BF16), ((256, 1024), F32), ((256, 576), BF16)],
-    )
+    b_one, b_two = (send_z(b_own, 1), send_z(b_own, 2))
+    gsrc = after(gw, *xs[1:3])
+    g_one, g_two = (send(gsrc, 2), send(gsrc, 4))
+    w_a, up_bias_row, a1, lin, q, k, v, t0, t1, t2, t3, att, lse, small, kern = call(attend_k, [((768, 576), BF16), ((1, 768), F32), tall, ((1032, 576), F32)] + [(heads, BF16)] * 3 + [((256, 192), BF16)] * 4 + [(heads, F32), ((3, 1024, 1), F32), ((16, 768), F32), ((3, 576), F32)], ids, prefix_len, after(a_all, gw), a_peer, *xs, smem=2, name='attend', scratch=[((32, 24, 640), F32), ((4, 256, 192), BF16), ((256, 1024), F32), ((256, 576), BF16)])
     atts = [t0, send(t1, 2), send(t2, 4)]
-    atts.append(send(after(t3, atts[1]), 6))
-    b_one, b_two, g_one, g_two = all_after([b_one, b_two, g_one, g_two], t1)
+    atts.append(send(after(t3, *atts[1:2]), 6))
+    g_one, g_two = all_after([g_one, g_two], t1)
+    g_low, g_high = (send(part, bits) for part, bits in zip([g_one[:128], g_two[128:]], (4, 2)))
+    sdep = [*atts[1:3], *(g_low, g_high)]
+    b_one, b_two = all_after([b_one, b_two], t1)
     b_three = send_z(b_two, 1)
-    g_low, g_high = send(g_one[:128], 4), send(g_two[128:], 2)
-    (b_all,) = call(
-        stack_k, [((4, 12, 24, 768), BF16)], ids, b_own, *all_after([b_one, b_two, b_three], *atts[1:3], g_low, g_high), name="stack_b"
-    )
-    w_up, w_o, w_d = [
-        w.reshape(768, 768)
-        for w in call(gather_b_k, [((32, 24, 768), BF16)] * 3, ids, b_all, send(b_all, 1), name="gather_b")
-    ]
-    x1, a2 = call(resid_k, [((256, 768), F32), block], ids, *atts, w_o, xw, small, name="resid")
+    b_all, = call(stack_k, [((4, 12, 24, 768), BF16)], ids, b_own, *all_after([b_one, b_two, b_three], *sdep), name='stack_b')
+    w_up, w_o, w_d = [w.reshape(768, 768) for w in call(gather_b_k, [((32, 24, 768), BF16)] * 3, ids, b_all, send(b_all, 1), name='gather_b')]
+    x1, a2 = call(resid_k, [((256, 768), F32), block], ids, *atts, w_o, xw, small, name='resid')
     a2s = to_all_chips(a2)
-    dh, g_all = call(hidden_grad_k, [tall] * 2, ids, gw, g_one, g_two, g_low, g_high, w_d, name="hidden_grad")
-    hsq, du, a2_all, *da2 = call(
-        ffn_k, [tall] * 3 + blocks, ids, *a2s, dh, w_up, up_bias_row, scratch=[tall], name="ffn"
-    )
-    da2, da2_one, da2_two = to_owners(ids, *da2)
+    dh, g_all = call(hidden_grad_k, [tall] * 2, ids, gw, g_one, g_two, g_low, g_high, w_d, name='hidden_grad')
+    hsq, du, a2_all, *da2 = call(ffn_k, [tall] * 3 + blocks, ids, *a2s, dh, w_up, up_bias_row, scratch=[tall], name='ffn')
+    da2_parts = da2
+    f_keep, f_away, up_bias_grad = call(ffn_grads_k, [((32, 24, 768), BF16)] * 2 + [((1, 768), F32)], ids, a2_all, g_all, hsq, du, scratch=[((2, 32, 24, 768), BF16)], name='ffn_grads', us=1000)
+    d_first = []
+    d_first.append(up_bias_grad)
+    da2, da2_one, da2_two = to_owners(ids, *da2_parts, *d_first)
     da2 = [da2, send(da2_one, 2), send(da2_two, 4)]
-    hsq, du = all_after([hsq, du], da2_one)
-    f_keep, f_away, up_bias_grad = call(
-        ffn_grads_k, [((32, 24, 768), BF16)] * 2 + [((1, 768), F32)], ids, a2_all, g_all, hsq, du,
-        scratch=[((2, 32, 24, 768), BF16)], name="ffn_grads", us=100,
-    )
-    f_keep, f_later, f_now = join_cores(ids, f_keep, f_away, "f")
+    mid_first = []
+    outs = list(call(ffn_out_k, [block] * 4, ids, hsq, after(w_d, da2_one), name='ffn_out'))
+    mid_first.append(outs[0])
+    f_peer = send(after(f_away, da2_one), 1)
+    f_keep, f_later, f_now = join_cores(ids, f_keep, f_peer, 'f')
     f_now = send_z(f_now, 1)
-
-    outs = call(ffn_out_k, [block] * 4, ids, hsq, w_d, name="ffn_out", us=100)
-    dx, dz, out_bias_grad, *datt = call(
-        mid_grad_k, [((256, 768), F32), block, ((1, 768), F32)] + [((256, 192), BF16)] * 4,
-        ids, *da2, x1, after(gw, f_keep, outs[0]), small, w_o, name="mid_grad",
-    )
+    mid_first.append(f_keep)
+    dx, dz, out_bias_grad, *datt = call(mid_grad_k, [((256, 768), F32), block, ((1, 768), F32)] + [((256, 192), BF16)] * 4, ids, *da2, x1, after(gw, *mid_first), small, w_o, name='mid_grad')
     datt = to_chips(datt)
-    o_keep, o_away = call(
-        out_grads_k, [((16, 24, 768), BF16)] * 2, ids, *atts, dz,
-        scratch=[((2, 16, 24, 768), BF16)], name="out_grads", us=0,
-    )
-    out_one, out_two, out_three = all_after(outs[1:], *datt[1:])
-    out_one, out_two = send(out_one, 2), send(out_two, 4)
+    ag_first = []
+    o_keep, o_away = call(out_grads_k, [((16, 24, 768), BF16)] * 2, ids, *atts, dz, scratch=[((2, 16, 24, 768), BF16)], name='out_grads')
+    ag_first.append(o_keep)
+    pj_first = []
     f_now = after(f_now, *datt[1:])
-    (f_later,) = call(pass_on_k, [(f_later.shape, BF16)], ids, f_later, f_now, name="pass_f")
+    f_later, = call(pass_on_k, [(f_later.shape, BF16)], ids, f_later, f_now, name='pass_f')
     f_sent = send_z(f_later, 2)
-    dlin, conv_grad, *da1 = call(
-        attend_grad_k, [((1024, 576), BF16), ((3, 576), F32)] + blocks,
-        ids, prefix_len, *datt, after(q, f_later), k, v, att, lse, lin, kern, w_a, smem=2, name="attend_grad", us=1000,
-        scratch=[(heads, BF16), ((1032, 576), F32), ((256, 1024), F32), (heads, F32)]
-        + [((3, 64, 1024), F32)] * 2 + [tall],
-    )
-    outs = [outs[0], out_one, out_two, send(after(out_three, dlin), 6)]
-    o_keep, o_later, o_now = join_cores(ids, o_keep, after(o_away, dlin), "o")
+    ag_first.append(f_later)
+    pj_first.append(f_sent)
+    outs[1:] = all_after(outs[1:], *datt[1:])
+    outs[1], outs[2] = (send(outs[1], 2), send(outs[2], 4))
+    pj_first += outs[1:3]
+    dlin, conv_grad, *da1 = call(attend_grad_k, [((1024, 576), BF16), ((3, 576), F32)] + blocks, ids, prefix_len, *datt, after(q, *ag_first), k, v, att, lse, lin, kern, w_a, smem=2, name='attend_grad', scratch=[(heads, BF16), ((1032, 576), F32), ((256, 1024), F32), (heads, F32)] + [((3, 64, 1024), F32)] * 2 + [tall])
+    o_peer = send(after(o_away, dlin), 1)
+    r_keep, r_away = call(proj_grads_k, [((16, 24, 640), BF16)] * 2, ids, after(a1, *pj_first), dlin, conv_grad, up_bias_grad, out_bias_grad, gw, scratch=[((2, 16, 24, 640), F32)], name='proj_grads')
+    r_peer = send(r_away, 1)
+    r_keep, r_later, r_now = join_cores(ids, r_keep, r_peer, 'r')
+    r_now = send_z(r_now, 1)
+    o_keep, o_later, o_now = join_cores(ids, o_keep, o_peer, 'o')
     o_now = send_z(o_now, 1)
-    r_keep, r_away = call(
-        proj_grads_k, [((16, 24, 640), BF16)] * 2, ids, after(a1, out_one, out_two, f_sent), dlin, conv_grad, up_bias_grad, out_bias_grad, gw,
-        scratch=[((2, 16, 24, 640), F32)], name="proj_grads", us=0,
-    )
+    o_now = after(o_now, r_keep)
+    o_later, = call(pass_on_k, [(o_later.shape, BF16)], ids, o_later, o_now, name='pass_o')
+    o_sent = send_z(o_later, 2)
     da1, da1_one, da1_two = to_owners(ids, *da1)
+    r_later, = call(pass_on_k, [(r_later.shape, BF16)], ids, r_later, r_now, name='pass_r')
     da1 = [da1, send(da1_one, 2), send(da1_two, 4)]
-    r_keep, r_later, r_now = join_cores(ids, r_keep, r_away, "r")
-    r_now = send_z(r_now, 1)
-    (o_later,) = call(pass_on_k, [(o_later.shape, BF16)], ids, after(o_later, r_keep), o_now, name="pass_o")
-    o_sent = send_z(o_later, 2)
-    (r_later,) = call(pass_on_k, [(r_later.shape, BF16)], ids, r_later, r_now, name="pass_r")
-    rows = (128, 768)
-    out_keep, out_away = call(output_k, [(rows, BF16)] * 2, ids, *outs, after(x1, r_later), small, name="output")
+    r_sent = send_z(r_later, 2)
+    outs[3] = send(after(outs[3], r_keep), 6)
+    out_keep, out_away = call(output_k, [(rows, BF16)] * 2, ids, *outs, after(x1, r_later), small, name='output')
+    out_recv = send(out_away, 1)
+    in_keep, in_away = call(input_grad_k, [(rows, F32)] * 2, ids, *da1, xw, dx, small, name='input_grad')
+    in_recv = send(in_away, 1)
     o_parts = [o_keep, o_now, o_sent]
     f_parts = [f_keep, f_now, f_sent]
-    r_parts = [r_keep, r_now, send_z(r_later, 2)]
-    down_grad, *sums = call(
-        sum_planes_k, [((96, 768), F32)] + [((24, 2176), BF16)] * 4, ids, *f_parts, *o_parts, *r_parts,
-        name="sum_planes",
-    )
+    r_parts = [r_keep, r_now, r_sent]
+    down_grad, *sums = call(sum_planes_k, [((96, 768), F32)] + [((24, 2176), BF16)] * 4, ids, *f_parts, *o_parts, *r_parts, name='sum_planes')
     sums = to_chips(sums)
-
-    out_recv = send(out_away, 1)
-    in_keep, in_away = call(input_grad_k, [(rows, F32)] * 2, ids, *da1, xw, after(dx, out_keep), small, name="input_grad")
-    in_recv = send(in_away, 1)
-    block_output, input_grad = call(
-        deliver_k, [((2, 1, 128, 768), BF16), ((2, 1, 128, 768), F32)],
-        ids, out_keep, out_recv, in_keep, in_recv, name="deliver", us=100,
-    )
+    block_output, input_grad = call(deliver_k, [((2, 1, 128, 768), BF16), ((2, 1, 128, 768), F32)], ids, out_keep, out_recv, in_keep, in_recv, name='deliver', us=100)
     vec = ((24,), F32)
-    gq, gk, gv, cq, ck, cv, go, gu, ga, gf, bo, bd, bu = call(
-        owned_k,
-        [((24, 768), F32)] * 3 + [((3, 24), F32)] * 3 + [((24, 768), F32), ((24, 3072), F32)]
-        + [vec] * 4 + [((96,), F32)],
-        ids, *sums, q_weight, k_weight, v_weight, up_weight, attn_gain, ffn_gain,
-        scratch=[((4, 24, 640), F32), ((4, 24, 768), F32)], name="owned", us=100,
-    )
-    return (
-        block_output, input_grad, ga, gq, gk, gv, cq, ck, cv, go, bo, gf, gu, bu, down_grad, bd,
-    )
+    gq, gk, gv, cq, ck, cv, go, gu, ga, gf, bo, bd, bu = call(owned_k, [((24, 768), F32)] * 3 + [((3, 24), F32)] * 3 + [((24, 768), F32), ((24, 3072), F32)] + [vec] * 4 + [((96,), F32)], ids, sums[0], *sums[1:], q_weight, k_weight, v_weight, up_weight, attn_gain, ffn_gain, scratch=[((4, 24, 640), F32), ((4, 24, 768), F32)], name='owned', us=100)
+    return (block_output, input_grad, ga, gq, gk, gv, cq, ck, cv, go, bo, gf, gu, bu, down_grad, bd)
 
 
 def solution(mesh):

time: 201 us -> 184 us (0.915)
  Pallas kernels: 68.6 us -> 59.1 us
  waiting for transfers between devices: 67 us -> 62.9 us
  local copies, waits for them, and re-layouts: 6.3 us -> 2.74 us
    pallas_call x31, Pallas kernels: 68.6 us -> 59.1 us  [call(): pl.pallas_call(body, out_shape=out_shape, compiler_params=pltpu.CompilerP...]
    ppermute x43 -> x44, waiting for transfers between devices: 51.3 us -> 43.6 us  [send(): return lax.ppermute(value, ('dp', 'ctx'), pairs)]
    ppermute x43 -> x44, starting transfers between devices: 40.1 us -> 45.6 us  [send(): return lax.ppermute(value, ('dp', 'ctx'), pairs)]
    ppermute x12, starting transfers between devices: 17.2 us -> 12.1 us  [send_z(): return lax.ppermute(value, ('dp', 'ctx'), pairs)]
    unnamed x51 -> x37, local copies, waits for them, and re-layouts: 6.24 us -> 1.98 us
    ppermute x12, waiting for transfers between devices: 15.7 us -> 19.3 us  [send_z(): return lax.ppermute(value, ('dp', 'ctx'), pairs)]
  transfers between devices with their start and end apart: 55 -> 56, of which waited for: 23 -> 27; matrix products, arithmetic and copies ran while one was open for 0% -> 1% of each run, Pallas kernels for 28% -> 27%
where the time goes in v2:
time: 184 us
  waiting for transfers between devices  62.9 us (34%)
  Pallas kernels  59.1 us (32%)
  starting transfers between devices  57.7 us (31%)
  local copies, waits for them, and re-layouts  2.74 us (1%)
    pallas_call x31, Pallas kernels, call(): pl.pallas_call(body, out_shape=out_shape, compiler_params=pltpu.CompilerP...  59.1 us
    ppermute x44, starting transfers between devices, send(): return lax.ppermute(value, ('dp', 'ctx'), pairs)  45.6 us
    ppermute x44, waiting for transfers between devices, send(): return lax.ppermute(value, ('dp', 'ctx'), pairs)  43.6 us
    ppermute x12, waiting for transfers between devices, send_z(): return lax.ppermute(value, ('dp', 'ctx'), pairs)  19.3 us
    ppermute x12, starting transfers between devices, send_z(): return lax.ppermute(value, ('dp', 'ctx'), pairs)  12.1 us
  transfers between devices with their start and end apart: 56, of which 27 were waited for; matrix products, arithmetic and copies ran while one was open for 1% of the time, Pallas kernels for 27%

profile of v2, /device:TPU:0, one launch (start us, length us, event | category | flops | bytes accessed | tf_op | source)
XLA Modules:
  0.0 183.7 jit_solution(11965562797728569948)
XLA Ops:
  1.2 1.9 %pack.1 = (bf16[24,2176]{1,0:T(8,128)(2,1)S(1)}, bf16[24,2176]{1,0:T(8,128)(2,1)S(1)}, bf16[24,2176]{1,0:T(8,128)(2,1)S(1)}, bf16[24,2176]{1,0:T(8,128)(2,1)S(1)}) custom-call(s32[3]{0:T(128)S(1)} %pad_add_fusion.ids, bf16[24,768]{1,0:T(8,128)(2,1)} %wq.1, bf16[24,768]{1,0:T(8,128)(2,1)} %wk.1, bf16[24,768]{1,0:T(8,128)(2,1)} %wv.1, bf16[24,3072]{1,0:T(8,128)(2,1)} %up.1, ...), custom_call_target="tpu_custom_call" | custom-call | flops 1 | bytes 1 | tf_op jit(solution)/shard_map/pack/pallas_call | solution.py:454
  3.1 2.6 %collective-permute-start = (bf16[24,2176]{1,0:T(8,128)(2,1)S(1)}, bf16[24,2176]{1,0:T(8,128)(2,1)S(1)}, u32[]{:S(2)}, u32[]{:S(2)}) collective-permute-start(bf16[24,2176]{1,0:T(8,128)(2,1)S(1)} %get-tuple-element.148), channel_id=1, source_target_pairs={{0,2},{1,3},{2,0},{3,1},{4,6},{5,7},{6,4},{7,5},{8,10},{9,11},{10,... | collective-permute-start | bytes 313352 | tf_op jit(solution)/shard_map/ppermute | solution.py:469
  5.7 1.5 collective-permute-start.1
  7.3 2.0 %collective-permute-done.p1 = bf16[24,2176]{1,0:T(8,128)(2,1)S(1)} collective-permute-done((bf16[24,2176]{1,0:T(8,128)(2,1)S(1)}, bf16[24,2176]{1,0:T(8,128)(2,1)S(1)}, u32[]{:S(2)}, u32[]{:S(2)}) %collective-permute-start) | collective-permute-done | bytes 104480 | tf_op jit(solution)/shard_map/ppermute | solution.py:469
  9.3 1.5 place_x.1.refs_2_.xw
  10.8 1.8 collective-permute-start.10
  13.6 3.7 %collective-permute-start.5 = (bf16[4,24,640]{2,1,0:T(8,128)(2,1)S(1)}, bf16[4,24,640]{2,1,0:T(8,128)(2,1)S(1)}, u32[]{:S(2)}, u32[]{:S(2)}) collective-permute-start(bf16[4,24,640]{2,1,0:T(8,128)(2,1)S(1)} %get-tuple-element.151.s0), channel_id=1, source_target_pairs={{0,24},{1,25},{2,26},{3,27},{4,28},{5,29},{6,30},{7,31},{8,16},{9,... | collective-permute-start | bytes 368648 | tf_op jit(solution)/shard_map/ppermute | solution.py:475
  18.0 1.6 collective-permute-start.9
  19.6 1.4 with_down.1.s0
  21.5 5.3 %collective-permute-done.4.s2 = bf16[4,24,640]{2,1,0:T(8,128)(2,1)S(1)} collective-permute-done((bf16[4,24,640]{2,1,0:T(8,128)(2,1)S(1)}, bf16[4,24,640]{2,1,0:T(8,128)(2,1)S(1)}, u32[]{:S(2)}, u32[]{:S(2)}) %collective-permute-start.4) | collective-permute-done | bytes 122912 | tf_op jit(solution)/shard_map/ppermute | solution.py:475
  28.3 2.8 %collective-permute-start.16 = (bf16[12,24,768]{2,1,0:T(8,128)(2,1)S(1)}, bf16[12,24,768]{2,1,0:T(8,128)(2,1)}, u32[]{:S(2)}, u32[]{:S(2)}) collective-permute-start(bf16[12,24,768]{2,1,0:T(8,128)(2,1)S(1)} %with_down.1.s0), channel_id=1, source_target_pairs={{0,8},{1,9},{2,10},{3,11},{4,12},{5,13},{6,14},{7,15},{8,0},{9,1},... | collective-permute-start | bytes 1327112 | tf_op jit(solution)/shard_map/ppermute | solution.py:475
  31.8 1.9 %collective-permute-start.11 = (bf16[128,768]{1,0:T(8,128)(2,1)S(1)}, bf16[128,768]{1,0:T(8,128)(2,1)S(1)}, u32[]{:S(2)}, u32[]{:S(2)}) collective-permute-start(bf16[128,768]{1,0:T(8,128)(2,1)S(1)} %slice.24), channel_id=1, source_target_pairs={{0,4},{1,5},{2,6},{3,7},{4,0},{5,1},{6,2},{7,3},{8,12},{9,13},{10,... | collective-permute-start | bytes 589832 | tf_op jit(solution)/shard_map/ppermute | solution.py:469
  34.3 1.5 place_g.1.g0.gw.g
  36.5 1.5 collective-permute-start.20
  38.4 2.1 %collective-permute-start.19 = (bf16[256,768]{1,0:T(8,128)(2,1)S(1)}, bf16[256,768]{1,0:T(8,128)(2,1)S(1)}, u32[]{:S(2)}, u32[]{:S(2)}) collective-permute-start(bf16[256,768]{1,0:T(8,128)(2,1)S(1)} %place_g.1.g0.gw.g), channel_id=1, source_target_pairs={{0,2},{1,3},{2,0},{3,1},{4,6},{5,7},{6,4},{7,5},{8,10},{9,11},{10,... | collective-permute-start | bytes 1179656 | tf_op jit(solution)/shard_map/ppermute | solution.py:469
  40.6 1.0 copy-done.9
  41.6 9.2 %attend.1 = (bf16[768,576]{1,0:T(8,128)(2,1)S(1)}, f32[1,768]{1,0:T(1,128)S(1)}, bf16[1024,768]{1,0:T(8,128)(2,1)S(1)}, f32[1032,576]{1,0:T(8,128)S(1)}, bf16[3,...) custom-call(s32[3]{0:T(128)S(1)} %pad_add_fusion.ids, ...), custom_call_target="tpu_custom_call" | custom-call | flops 1 | bytes 1 | tf_op jit(solution)/shard_map/attend/pallas_call | solution.py:454
  51.2 1.6 collective-permute-start.22
  53.3 1.5 collective-permute-start.14
  55.3 6.6 %collective-permute-done.14.t2 = bf16[256,192]{1,0:T(8,128)(2,1)S(1)} collective-permute-done((bf16[256,192]{1,0:T(8,128)(2,1)S(1)}, bf16[256,192]{1,0:T(8,128)(2,1)S(1)}, u32[]{:S(2)}, u32[]{:S(2)}) %collective-permute-start.14) | collective-permute-done | bytes 98336 | tf_op jit(solution)/shard_map/ppermute | solution.py:469
  62.8 1.3 stack_b.1.mine
  64.2 1.9 %collective-permute-start.15 = (bf16[256,192]{1,0:T(8,128)(2,1)S(1)}, bf16[256,192]{1,0:T(8,128)(2,1)S(1)}, u32[]{:S(2)}, u32[]{:S(2)}) collective-permute-start(bf16[256,192]{1,0:T(8,128)(2,1)S(1)} %get-tuple-element.163), channel_id=1, source_target_pairs={{0,6},{1,7},{2,4},{3,5},{4,2},{5,3},{6,0},{7,1},{8,14},{9,15},{10,... | collective-permute-start | bytes 294920 | tf_op jit(solution)/shard_map/ppermute | solution.py:469
  66.1 1.7 collective-permute-done.23.other
  68.7 2.3 %collective-permute-done.15.t3 = bf16[256,192]{1,0:T(8,128)(2,1)S(1)} collective-permute-done((bf16[256,192]{1,0:T(8,128)(2,1)S(1)}, bf16[256,192]{1,0:T(8,128)(2,1)S(1)}, u32[]{:S(2)}, u32[]{:S(2)}) %collective-permute-start.15) | collective-permute-done | bytes 98336 | tf_op jit(solution)/shard_map/ppermute | solution.py:469
  71.0 1.2 resid.1
  72.3 1.9 %collective-permute-start.25 = (bf16[256,768]{1,0:T(8,128)(2,1)S(1)}, bf16[256,768]{1,0:T(8,128)(2,1)S(1)}, u32[]{:S(2)}, u32[]{:S(2)}) collective-permute-start(bf16[256,768]{1,0:T(8,128)(2,1)S(1)} %get-tuple-element.175.refs_0_), channel_id=1, source_target_pairs={{0,4},{1,5},{2,6},{3,7},{4,0},{5,1},{6,2},{7,3},{8,12},{9,13},{10,... | collective-permute-start | bytes 1179656 | tf_op jit(solution)/shard_map/ppermute | solution.py:469
  74.7 8.4 %collective-permute-done.25.refs_2_ = bf16[256,768]{1,0:T(8,128)(2,1)S(1)} collective-permute-done((bf16[256,768]{1,0:T(8,128)(2,1)S(1)}, bf16[256,768]{1,0:T(8,128)(2,1)S(1)}, u32[]{:S(2)}, u32[]{:S(2)}) %collective-permute-start.25) | collective-permute-done | bytes 393248 | tf_op jit(solution)/shard_map/ppermute | solution.py:469
  83.1 1.8 collective-permute-start.27
  85.6 2.2 %hidden_grad.1 = (bf16[1024,768]{1,0:T(8,128)(2,1)S(1)}, bf16[1024,768]{1,0:T(8,128)(2,1)S(1)}) custom-call(s32[3]{0:T(128)S(1)} %pad_add_fusion.ids, bf16[256,768]{1,0:T(8,128)(2,1)S(1)} %place_g.1.g0.gw.g, bf16[256,768]{1,0:T(8,128)(2,1)S(1)} %collective-permute-done.19.g1, bf16[256,768]{1,0:T(8,128)(2,1)S(1)} %collective-permute-done.20.g2, ...), custom_call_target="tpu_custom_call" | custom-call | flops 1 | bytes 1 | tf_op jit(solution)/shard_map/hidden_grad/pallas_call | solution.py:454
  87.8 1.1 collective-permute-done.27.refs_4_
  88.9 1.8 %collective-permute-done.26.refs_3_ = bf16[128,768]{1,0:T(8,128)(2,1)S(1)} collective-permute-done((bf16[128,768]{1,0:T(8,128)(2,1)S(1)}, bf16[128,768]{1,0:T(8,128)(2,1)S(1)}, u32[]{:S(2)}, u32[]{:S(2)}) %collective-permute-start.26) | collective-permute-done | bytes 196640 | tf_op jit(solution)/shard_map/ppermute | solution.py:469
  90.7 4.2 %ffn.1 = (bf16[1024,768]{1,0:T(8,128)(2,1)S(1)}, bf16[1024,768]{1,0:T(8,128)(2,1)S(1)}, bf16[1024,768]{1,0:T(8,128)(2,1)S(1)}, bf16[256,768]{1,0:T(8,128)(2,1)S(...) custom-call(s32[3]{0:T(128)S(1)} %pad_add_fusion.ids, ...), custom_call_target="tpu_custom_call" | custom-call | flops 1 | bytes 1 | tf_op jit(solution)/shard_map/ffn/pallas_call | solution.py:454
  95.1 1.7 collective-permute-start.29
  96.9 3.4 %ffn_grads.1 = (bf16[32,24,768]{2,1,0:T(8,128)(2,1)S(1)}, bf16[32,24,768]{2,1,0:T(8,128)(2,1)S(1)}, f32[1,768]{1,0:T(1,128)S(1)}) custom-call(s32[3]{0:T(128)S(1)} %pad_add_fusion.ids, bf16[1024,768]{1,0:T(8,128)(2,1)S(1)} %get-tuple-element.185.a_all, bf16[1024,768]{1,0:T(8,128)(2,1)S(1)} %get-tuple-element.186.g_all, ...), custom_call_target="tpu_custom_call" | custom-call | flops 999999995904 | bytes 1 | tf_op jit(solution)/shard_map/ffn_grads/pallas_call | solution.py:454
  101.1 1.3 add_half.2
  102.5 1.8 collective-permute-start.31
  106.9 1.9 %ffn_out.1 = (bf16[256,768]{1,0:T(8,128)(2,1)S(1)}, bf16[256,768]{1,0:T(8,128)(2,1)S(1)}, bf16[256,768]{1,0:T(8,128)(2,1)S(1)}, bf16[256,768]{1,0:T(8,128)(2,1)S(1)}) custom-call(s32[3]{0:T(128)S(1)} %pad_add_fusion.ids, bf16[1024,768]{1,0:T(8,128)(2,1)S(1)} %get-tuple-element.180.hsq, bf16[768,768]{1,0:T(8,128)(2,1)S(1)} %bitcast.7), custom_call_target="tpu_custom_call" | custom-call | flops 1 | bytes 1 | tf_op jit(solution)/shard_map/ffn_out/pallas_call | solution.py:454
  108.8 5.1 %collective-permute-done.31.p2 = bf16[256,768]{1,0:T(8,128)(2,1)S(1)} collective-permute-done((bf16[256,768]{1,0:T(8,128)(2,1)S(1)}, bf16[256,768]{1,0:T(8,128)(2,1)S(1)}, u32[]{:S(2)}, u32[]{:S(2)}) %collective-permute-start.31) | collective-permute-done | bytes 393248 | tf_op jit(solution)/shard_map/ppermute | solution.py:469
  114.0 1.5 collective-permute-done.30.p1
  115.5 1.5 mid_grad.1
  117.6 1.5 collective-permute-start.34
  119.0 1.4 collective-permute-start.35
  120.5 2.8 %collective-permute-done.33.d1 = bf16[256,192]{1,0:T(8,128)(2,1)S(1)} collective-permute-done((bf16[256,192]{1,0:T(8,128)(2,1)S(1)}, bf16[256,192]{1,0:T(8,128)(2,1)S(1)}, u32[]{:S(2)}, u32[]{:S(2)}) %collective-permute-start.33) | collective-permute-done | bytes 98336 | tf_op jit(solution)/shard_map/ppermute | solution.py:469
  123.3 2.1 %collective-permute-done.34.d2 = bf16[256,192]{1,0:T(8,128)(2,1)S(1)} collective-permute-done((bf16[256,192]{1,0:T(8,128)(2,1)S(1)}, bf16[256,192]{1,0:T(8,128)(2,1)S(1)}, u32[]{:S(2)}, u32[]{:S(2)}) %collective-permute-start.34) | collective-permute-done | bytes 98336 | tf_op jit(solution)/shard_map/ppermute | solution.py:469
  125.4 1.0 collective-permute-start.36
  128.4 1.1 out_grads.1
  129.5 10.5 %attend_grad.1 = (bf16[1024,576]{1,0:T(8,128)(2,1)S(1)}, f32[3,576]{1,0:T(4,128)S(1)}, bf16[256,768]{1,0:T(8,128)(2,1)S(1)}, bf16[256,768]{1,0:T(8,128)(2,1)S(1)...) custom-call(s32[3]{0:T(128)S(1)} %pad_add_fusion.ids, ...), custom_call_target="tpu_custom_call" | custom-call | flops 1 | bytes 1 | tf_op jit(solution)/shard_map/attend_grad/pallas_call | solution.py:454
  140.1 1.2 collective-permute-done.39.refs_2_
  141.3 2.1 %proj_grads.1 = (bf16[16,24,640]{2,1,0:T(8,128)(2,1)S(1)}, bf16[16,24,640]{2,1,0:T(8,128)(2,1)S(1)}) custom-call(s32[3]{0:T(128)S(1)} %pad_add_fusion.ids, bf16[1024,768]{1,0:T(8,128)(2,1)S(1)} %get-tuple-element.215.a1, bf16[1024,576]{1,0:T(8,128)(2,1)S(1)} %get-tuple-element.228.dlin, f32[3,576]{1,0:T(4,128)S(1)} %get-tuple-element.229.conv, ...), custom_call_target="tpu_custom_call" | custom-call | flops 1 | bytes 1 | tf_op jit(solution)/shard_map/proj_grads/pallas_call | solution.py:454
  143.5 1.3 collective-permute-start.44
  147.2 3.6 %collective-permute-done.44.low = bf16[128,768]{1,0:T(8,128)(2,1)S(1)} collective-permute-done((bf16[128,768]{1,0:T(8,128)(2,1)S(1)}, bf16[128,768]{1,0:T(8,128)(2,1)S(1)}, u32[]{:S(2)}, u32[]{:S(2)}) %collective-permute-start.44) | collective-permute-done | bytes 196640 | tf_op jit(solution)/shard_map/ppermute | solution.py:469
  154.2 1.3 collective-permute-start.47
  155.5 1.5 collective-permute-start.41
  157.6 1.7 collective-permute-start.51
  159.3 3.3 %collective-permute-done.42.got.refs_7_ = bf16[2,4,24,640]{3,2,1,0:T(8,128)(2,1)S(1)} collective-permute-done((bf16[2,4,24,640]{3,2,1,0:T(8,128)(2,1)S(1)}, bf16[2,4,24,640]{3,2,1,0:T(8,128)(2,1)S(1)}, u32[]{:S(2)}, u32[]{:S(2)}) %collective-permute-start.42) | collective-permute-done | bytes 245792 | tf_op jit(solution)/shard_map/ppermute | solution.py:475
  163.3 6.8 %collective-permute-done.51.refs_5_ = bf16[4,24,768]{2,1,0:T(8,128)(2,1)S(1)} collective-permute-done((bf16[4,24,768]{2,1,0:T(8,128)(2,1)S(1)}, bf16[4,24,768]{2,1,0:T(8,128)(2,1)S(1)}, u32[]{:S(2)}, u32[]{:S(2)}) %collective-permute-start.51) | collective-permute-done | bytes 147488 | tf_op jit(solution)/shard_map/ppermute | solution.py:475
  170.0 1.3 collective-permute-done.52.refs_8_
  171.3 1.4 sum_planes.1
  173.5 1.3 collective-permute-start.54
  174.8 1.4 collective-permute-start.55
  176.2 1.0 input_grad.1
  178.9 1.5 collective-permute-done.55.s3
  180.4 1.6 owned.1
  182.1 1.6 deliver.1
  (123 shorter events, 27.4 us)
Async XLA Ops:
  0.6 8.7 %collective-permute-start.8 = (bf16[2,1,128,768]{3,2,1,0:T(8,128)(2,1)}, bf16[2,1,128,768]{3,2,1,0:T(8,128)(2,1)S(1)}, u32[]{:S(2)}, u32[]{:S(2)}) collective-permute-start(bf16[2,1,128,768]{3,2,1,0:T(8,128)(2,1)} %mine.3), channel_id=1, source_target_pairs={{0,1},{1,0},{2,3},{3,2},{4,5},{5,4},{6,7},{7,6},{8,9},{9,8},{10,11... | collective-permute-start | bytes 1179656 | tf_op jit(solution)/shard_map/ppermute | solution.py:469
  3.1 6.2 %collective-permute-start = (bf16[24,2176]{1,0:T(8,128)(2,1)S(1)}, bf16[24,2176]{1,0:T(8,128)(2,1)S(1)}, u32[]{:S(2)}, u32[]{:S(2)}) collective-permute-start(bf16[24,2176]{1,0:T(8,128)(2,1)S(1)} %get-tuple-element.148), channel_id=1, source_target_pairs={{0,2},{1,3},{2,0},{3,1},{4,6},{5,7},{6,4},{7,5},{8,10},{9,11},{10,... | collective-permute-start | bytes 313352 | tf_op jit(solution)/shard_map/ppermute | solution.py:469
  5.7 6.9 %collective-permute-start.1 = (bf16[24,2176]{1,0:T(8,128)(2,1)S(1)}, bf16[24,2176]{1,0:T(8,128)(2,1)S(1)}, u32[]{:S(2)}, u32[]{:S(2)}) collective-permute-start(bf16[24,2176]{1,0:T(8,128)(2,1)S(1)} %get-tuple-element.149), channel_id=1, source_target_pairs={{0,4},{1,5},{2,6},{3,7},{4,0},{5,1},{6,2},{7,3},{8,12},{9,13},{10,... | collective-permute-start | bytes 313352 | tf_op jit(solution)/shard_map/ppermute | solution.py:469
  7.3 20.2 %copy-start.16 = (bf16[2,1,128,768]{3,2,1,0:T(8,128)(2,1)S(1)}, bf16[2,1,128,768]{3,2,1,0:T(8,128)(2,1)}, u32[]{:S(2)}) copy-start(bf16[2,1,128,768]{3,2,1,0:T(8,128)(2,1)} %mine.2) | copy-start | bytes 1179652
  7.3 5.7 %collective-permute-start.2 = (bf16[24,2176]{1,0:T(8,128)(2,1)S(1)}, bf16[24,2176]{1,0:T(8,128)(2,1)S(1)}, u32[]{:S(2)}, u32[]{:S(2)}) collective-permute-start(bf16[24,2176]{1,0:T(8,128)(2,1)S(1)} %get-tuple-element.150), channel_id=1, source_target_pairs={{0,6},{1,7},{2,4},{3,5},{4,2},{5,3},{6,0},{7,1},{8,14},{9,15},{10,... | collective-permute-start | bytes 313352 | tf_op jit(solution)/shard_map/ppermute | solution.py:469
  10.8 17.5 %collective-permute-start.10 = (bf16[256,768]{1,0:T(8,128)(2,1)S(1)}, bf16[256,768]{1,0:T(8,128)(2,1)S(1)}, u32[]{:S(2)}, u32[]{:S(2)}) collective-permute-start(bf16[256,768]{1,0:T(8,128)(2,1)S(1)} %place_x.1.refs_2_.xw), channel_id=1, source_target_pairs={{0,4},{1,5},{2,6},{3,7},{4,0},{5,1},{6,2},{7,3},{8,12},{9,13},{10,... | collective-permute-start | bytes 1179656 | tf_op jit(solution)/shard_map/ppermute | solution.py:469
  13.6 7.9 %collective-permute-start.5 = (bf16[4,24,640]{2,1,0:T(8,128)(2,1)S(1)}, bf16[4,24,640]{2,1,0:T(8,128)(2,1)S(1)}, u32[]{:S(2)}, u32[]{:S(2)}) collective-permute-start(bf16[4,24,640]{2,1,0:T(8,128)(2,1)S(1)} %get-tuple-element.151.s0), channel_id=1, source_target_pairs={{0,24},{1,25},{2,26},{3,27},{4,28},{5,29},{6,30},{7,31},{8,16},{9,... | collective-permute-start | bytes 368648 | tf_op jit(solution)/shard_map/ppermute | solution.py:475
  17.2 9.6 %collective-permute-start.4 = (bf16[4,24,640]{2,1,0:T(8,128)(2,1)S(1)}, bf16[4,24,640]{2,1,0:T(8,128)(2,1)S(1)}, u32[]{:S(2)}, u32[]{:S(2)}) collective-permute-start(bf16[4,24,640]{2,1,0:T(8,128)(2,1)S(1)} %get-tuple-element.151.s0), channel_id=1, source_target_pairs={{0,16},{1,17},{2,18},{3,19},{4,20},{5,21},{6,22},{7,23},{8,24},{9,... | collective-permute-start | bytes 368648 | tf_op jit(solution)/shard_map/ppermute | solution.py:475
  17.2 9.6 %collective-permute-start.3 = (bf16[4,24,640]{2,1,0:T(8,128)(2,1)S(1)}, bf16[4,24,640]{2,1,0:T(8,128)(2,1)S(1)}, u32[]{:S(2)}, u32[]{:S(2)}) collective-permute-start(bf16[4,24,640]{2,1,0:T(8,128)(2,1)S(1)} %get-tuple-element.151.s0), channel_id=1, source_target_pairs={{0,8},{1,9},{2,10},{3,11},{4,12},{5,13},{6,14},{7,15},{8,0},{9,1},... | collective-permute-start | bytes 368648 | tf_op jit(solution)/shard_map/ppermute | solution.py:475
  18.0 13.7 %collective-permute-start.9 = (bf16[256,768]{1,0:T(8,128)(2,1)S(1)}, bf16[256,768]{1,0:T(8,128)(2,1)S(1)}, u32[]{:S(2)}, u32[]{:S(2)}) collective-permute-start(bf16[256,768]{1,0:T(8,128)(2,1)S(1)} %place_x.1.refs_2_.xw), channel_id=1, source_target_pairs={{0,2},{1,3},{2,0},{3,1},{4,6},{5,7},{6,4},{7,5},{8,10},{9,11},{10,... | collective-permute-start | bytes 1179656 | tf_op jit(solution)/shard_map/ppermute | solution.py:469
  21.0 19.5 %copy-start.17 = (s32[2,1]{0,1:T(1,128)S(1)}, s32[2,1]{0,1:T(1,128)}, u32[]{:S(2)}) copy-start(s32[2,1]{0,1:T(1,128)} %param.19) | copy-start | bytes 28
  27.4 8.3 %collective-permute-start.7 = (bf16[4,4,24,640]{3,2,1,0:T(8,128)(2,1)S(1)}, bf16[4,4,24,640]{3,2,1,0:T(8,128)(2,1)S(1)}, u32[]{:S(2)}, u32[]{:S(2)}) collective-permute-start(bf16[4,4,24,640]{3,2,1,0:T(8,128)(2,1)S(1)} %stack_a.1.refs_0_), channel_id=1, source_target_pairs={{0,1},{1,0},{2,3},{3,2},{4,5},{5,4},{6,7},{7,6},{8,9},{9,8},{10,11... | collective-permute-start | bytes 1474568 | tf_op jit(solution)/shard_map/ppermute | solution.py:469
  27.5 6.2 %collective-permute-start.6 = (bf16[2,1,128,768]{3,2,1,0:T(8,128)(2,1)S(1)}, bf16[2,1,128,768]{3,2,1,0:T(8,128)(2,1)S(1)}, u32[]{:S(2)}, u32[]{:S(2)}) collective-permute-start(bf16[2,1,128,768]{3,2,1,0:T(8,128)(2,1)S(1)} %copy-done.16), channel_id=1, source_target_pairs={{0,1},{1,0},{2,3},{3,2},{4,5},{5,4},{6,7},{7,6},{8,9},{9,8},{10,11... | collective-permute-start | bytes 1179656 | tf_op jit(solution)/shard_map/ppermute | solution.py:469
  28.0 22.8 %collective-permute-start.17 = (bf16[12,24,768]{2,1,0:T(8,128)(2,1)S(1)}, bf16[12,24,768]{2,1,0:T(8,128)(2,1)}, u32[]{:S(2)}, u32[]{:S(2)}) collective-permute-start(bf16[12,24,768]{2,1,0:T(8,128)(2,1)S(1)} %with_down.1.s0), channel_id=1, source_target_pairs={{0,16},{1,17},{2,18},{3,19},{4,20},{5,21},{6,22},{7,23},{8,24},{9,... | collective-permute-start | bytes 1327112 | tf_op jit(solution)/shard_map/ppermute | solution.py:475
  28.3 22.5 %collective-permute-start.16 = (bf16[12,24,768]{2,1,0:T(8,128)(2,1)S(1)}, bf16[12,24,768]{2,1,0:T(8,128)(2,1)}, u32[]{:S(2)}, u32[]{:S(2)}) collective-permute-start(bf16[12,24,768]{2,1,0:T(8,128)(2,1)S(1)} %with_down.1.s0), channel_id=1, source_target_pairs={{0,8},{1,9},{2,10},{3,11},{4,12},{5,13},{6,14},{7,15},{8,0},{9,1},... | collective-permute-start | bytes 1327112 | tf_op jit(solution)/shard_map/ppermute | solution.py:475
  31.8 6.6 %collective-permute-start.11 = (bf16[128,768]{1,0:T(8,128)(2,1)S(1)}, bf16[128,768]{1,0:T(8,128)(2,1)S(1)}, u32[]{:S(2)}, u32[]{:S(2)}) collective-permute-start(bf16[128,768]{1,0:T(8,128)(2,1)S(1)} %slice.24), channel_id=1, source_target_pairs={{0,4},{1,5},{2,6},{3,7},{4,0},{5,1},{6,2},{7,3},{8,12},{9,13},{10,... | collective-permute-start | bytes 589832 | tf_op jit(solution)/shard_map/ppermute | solution.py:469
  33.7 6.9 %collective-permute-start.12 = (bf16[128,768]{1,0:T(8,128)(2,1)}, bf16[128,768]{1,0:T(8,128)(2,1)}, u32[]{:S(2)}, u32[]{:S(2)}) collective-permute-start(bf16[128,768]{1,0:T(8,128)(2,1)} %slice.25), channel_id=1, source_target_pairs={{0,2},{1,3},{2,0},{3,1},{4,6},{5,7},{6,4},{7,5},{8,10},{9,11},{10,... | collective-permute-start | bytes 589832 | tf_op jit(solution)/shard_map/ppermute | solution.py:469
  36.5 14.6 %collective-permute-start.20 = (bf16[256,768]{1,0:T(8,128)(2,1)S(1)}, bf16[256,768]{1,0:T(8,128)(2,1)S(1)}, u32[]{:S(2)}, u32[]{:S(2)}) collective-permute-start(bf16[256,768]{1,0:T(8,128)(2,1)S(1)} %place_g.1.g0.gw.g), channel_id=1, source_target_pairs={{0,4},{1,5},{2,6},{3,7},{4,0},{5,1},{6,2},{7,3},{8,12},{9,13},{10,... | collective-permute-start | bytes 1179656 | tf_op jit(solution)/shard_map/ppermute | solution.py:469
  38.4 12.8 %collective-permute-start.19 = (bf16[256,768]{1,0:T(8,128)(2,1)S(1)}, bf16[256,768]{1,0:T(8,128)(2,1)S(1)}, u32[]{:S(2)}, u32[]{:S(2)}) collective-permute-start(bf16[256,768]{1,0:T(8,128)(2,1)S(1)} %place_g.1.g0.gw.g), channel_id=1, source_target_pairs={{0,2},{1,3},{2,0},{3,1},{4,6},{5,7},{6,4},{7,5},{8,10},{9,11},{10,... | collective-permute-start | bytes 1179656 | tf_op jit(solution)/shard_map/ppermute | solution.py:469
  50.8 20.2 %copy-start.4 = (f32[16,768]{1,0:T(8,128)}, f32[16,768]{1,0:T(8,128)S(1)}, u32[]{:S(2)}) copy-start(f32[16,768]{1,0:T(8,128)S(1)} %get-tuple-element.174.small) | copy-start | bytes 147460
  50.8 20.2 %copy-start.6 = (bf16[256,192]{1,0:T(8,128)(2,1)}, bf16[256,192]{1,0:T(8,128)(2,1)S(1)}, u32[]{:S(2)}) copy-start(bf16[256,192]{1,0:T(8,128)(2,1)S(1)} %get-tuple-element.159.t0) | copy-start | bytes 294916
  50.8 12.0 %collective-permute-start.18 = (bf16[12,24,768]{2,1,0:T(8,128)(2,1)}, bf16[12,24,768]{2,1,0:T(8,128)(2,1)S(1)}, u32[]{:S(2)}, u32[]{:S(2)}) collective-permute-start(bf16[12,24,768]{2,1,0:T(8,128)(2,1)} %collective-permute-done.17.s2), channel_id=1, source_target_pairs={{0,8},{1,9},{2,10},{3,11},{4,12},{5,13},{6,14},{7,15},{8,0},{9,1},... | collective-permute-start | bytes 1327112 | tf_op jit(solution)/shard_map/ppermute | solution.py:475
  51.2 10.7 %collective-permute-start.22 = (bf16[128,768]{1,0:T(8,128)(2,1)S(1)}, bf16[128,768]{1,0:T(8,128)(2,1)S(1)}, u32[]{:S(2)}, u32[]{:S(2)}) collective-permute-start(bf16[128,768]{1,0:T(8,128)(2,1)S(1)} %slice.21), channel_id=1, source_target_pairs={{0,2},{1,3},{2,0},{3,1},{4,6},{5,7},{6,4},{7,5},{8,10},{9,11},{10,... | collective-permute-start | bytes 589832 | tf_op jit(solution)/shard_map/ppermute | solution.py:469
  52.8 9.2 %collective-permute-start.21 = (bf16[128,768]{1,0:T(8,128)(2,1)S(1)}, bf16[128,768]{1,0:T(8,128)(2,1)S(1)}, u32[]{:S(2)}, u32[]{:S(2)}) collective-permute-start(bf16[128,768]{1,0:T(8,128)(2,1)S(1)} %slice.20), channel_id=1, source_target_pairs={{0,4},{1,5},{2,6},{3,7},{4,0},{5,1},{6,2},{7,3},{8,12},{9,13},{10,... | collective-permute-start | bytes 589832 | tf_op jit(solution)/shard_map/ppermute | solution.py:469
  53.3 8.6 %collective-permute-start.14 = (bf16[256,192]{1,0:T(8,128)(2,1)S(1)}, bf16[256,192]{1,0:T(8,128)(2,1)S(1)}, u32[]{:S(2)}, u32[]{:S(2)}) collective-permute-start(bf16[256,192]{1,0:T(8,128)(2,1)S(1)} %get-tuple-element.161), channel_id=1, source_target_pairs={{0,4},{1,5},{2,6},{3,7},{4,0},{5,1},{6,2},{7,3},{8,12},{9,13},{10,... | collective-permute-start | bytes 294920 | tf_op jit(solution)/shard_map/ppermute | solution.py:469
  54.8 7.1 %collective-permute-start.13 = (bf16[256,192]{1,0:T(8,128)(2,1)S(1)}, bf16[256,192]{1,0:T(8,128)(2,1)S(1)}, u32[]{:S(2)}, u32[]{:S(2)}) collective-permute-start(bf16[256,192]{1,0:T(8,128)(2,1)S(1)} %get-tuple-element.160), channel_id=1, source_target_pairs={{0,2},{1,3},{2,0},{3,1},{4,6},{5,7},{6,4},{7,5},{8,10},{9,11},{10,... | collective-permute-start | bytes 294920 | tf_op jit(solution)/shard_map/ppermute | solution.py:469
  64.1 3.8 %collective-permute-start.23 = (bf16[4,12,24,768]{3,2,1,0:T(8,128)(2,1)S(1)}, bf16[4,12,24,768]{3,2,1,0:T(8,128)(2,1)S(1)}, u32[]{:S(2)}, u32[]{:S(2)}) collective-permute-start(bf16[4,12,24,768]{3,2,1,0:T(8,128)(2,1)S(1)} %stack_b.1.mine), channel_id=1, source_target_pairs={{0,1},{1,0},{2,3},{3,2},{4,5},{5,4},{6,7},{7,6},{8,9},{9,8},{10,11... | collective-permute-start | bytes 5308424 | tf_op jit(solution)/shard_map/ppermute | solution.py:469
  64.2 6.8 %collective-permute-start.15 = (bf16[256,192]{1,0:T(8,128)(2,1)S(1)}, bf16[256,192]{1,0:T(8,128)(2,1)S(1)}, u32[]{:S(2)}, u32[]{:S(2)}) collective-permute-start(bf16[256,192]{1,0:T(8,128)(2,1)S(1)} %get-tuple-element.163), channel_id=1, source_target_pairs={{0,6},{1,7},{2,4},{3,5},{4,2},{5,3},{6,0},{7,1},{8,14},{9,15},{10,... | collective-permute-start | bytes 294920 | tf_op jit(solution)/shard_map/ppermute | solution.py:469
  68.7 19.1 %copy-start = (bf16[32,24,768]{2,1,0:T(8,128)(2,1)}, bf16[32,24,768]{2,1,0:T(8,128)(2,1)S(1)}, u32[]{:S(2)}) copy-start(bf16[32,24,768]{2,1,0:T(8,128)(2,1)S(1)} %get-tuple-element.176) | copy-start | bytes 3538948
  68.7 19.1 %copy-start.2 = (bf16[32,24,768]{2,1,0:T(8,128)(2,1)}, bf16[32,24,768]{2,1,0:T(8,128)(2,1)S(1)}, u32[]{:S(2)}) copy-start(bf16[32,24,768]{2,1,0:T(8,128)(2,1)S(1)} %get-tuple-element.173) | copy-start | bytes 3538948
  72.3 10.9 %collective-permute-start.25 = (bf16[256,768]{1,0:T(8,128)(2,1)S(1)}, bf16[256,768]{1,0:T(8,128)(2,1)S(1)}, u32[]{:S(2)}, u32[]{:S(2)}) collective-permute-start(bf16[256,768]{1,0:T(8,128)(2,1)S(1)} %get-tuple-element.175.refs_0_), channel_id=1, source_target_pairs={{0,4},{1,5},{2,6},{3,7},{4,0},{5,1},{6,2},{7,3},{8,12},{9,13},{10,... | collective-permute-start | bytes 1179656 | tf_op jit(solution)/shard_map/ppermute | solution.py:469
  74.2 10.8 %collective-permute-start.24 = (bf16[256,768]{1,0:T(8,128)(2,1)S(1)}, bf16[256,768]{1,0:T(8,128)(2,1)S(1)}, u32[]{:S(2)}, u32[]{:S(2)}) collective-permute-start(bf16[256,768]{1,0:T(8,128)(2,1)S(1)} %get-tuple-element.175.refs_0_), channel_id=1, source_target_pairs={{0,2},{1,3},{2,0},{3,1},{4,6},{5,7},{6,4},{7,5},{8,10},{9,11},{10,... | collective-permute-start | bytes 1179656 | tf_op jit(solution)/shard_map/ppermute | solution.py:469
  83.1 5.8 %collective-permute-start.27 = (bf16[128,768]{1,0:T(8,128)(2,1)S(1)}, bf16[128,768]{1,0:T(8,128)(2,1)S(1)}, u32[]{:S(2)}, u32[]{:S(2)}) collective-permute-start(bf16[128,768]{1,0:T(8,128)(2,1)S(1)} %slice.27), channel_id=1, source_target_pairs={{0,2},{1,3},{2,0},{3,1},{4,6},{5,7},{6,4},{7,5},{8,10},{9,11},{10,... | collective-permute-start | bytes 589832 | tf_op jit(solution)/shard_map/ppermute | solution.py:469
  85.0 5.7 %collective-permute-start.26 = (bf16[128,768]{1,0:T(8,128)(2,1)S(1)}, bf16[128,768]{1,0:T(8,128)(2,1)S(1)}, u32[]{:S(2)}, u32[]{:S(2)}) collective-permute-start(bf16[128,768]{1,0:T(8,128)(2,1)S(1)} %slice.26), channel_id=1, source_target_pairs={{0,4},{1,5},{2,6},{3,7},{4,0},{5,1},{6,2},{7,3},{8,12},{9,13},{10,... | collective-permute-start | bytes 589832 | tf_op jit(solution)/shard_map/ppermute | solution.py:469
  94.9 6.0 %collective-permute-start.28 = (bf16[128,768]{1,0:T(8,128)(2,1)}, bf16[128,768]{1,0:T(8,128)(2,1)}, u32[]{:S(2)}, u32[]{:S(2)}) collective-permute-start(bf16[128,768]{1,0:T(8,128)(2,1)} %get-tuple-element.183), channel_id=1, source_target_pairs={{0,2},{1,3},{2,0},{3,1},{4,6},{5,7},{6,4},{7,5},{8,10},{9,11},{10,... | collective-permute-start | bytes 589832 | tf_op jit(solution)/shard_map/ppermute | solution.py:469
  95.1 6.0 %collective-permute-start.29 = (bf16[128,768]{1,0:T(8,128)(2,1)}, bf16[128,768]{1,0:T(8,128)(2,1)}, u32[]{:S(2)}, u32[]{:S(2)}) collective-permute-start(bf16[128,768]{1,0:T(8,128)(2,1)} %get-tuple-element.184), channel_id=1, source_target_pairs={{0,4},{1,5},{2,6},{3,7},{4,0},{5,1},{6,2},{7,3},{8,12},{9,13},{10,... | collective-permute-start | bytes 589832 | tf_op jit(solution)/shard_map/ppermute | solution.py:469
  102.4 2.9 %collective-permute-start.32 = (bf16[32,24,768]{2,1,0:T(8,128)(2,1)S(1)}, bf16[32,24,768]{2,1,0:T(8,128)(2,1)S(1)}, u32[]{:S(2)}, u32[]{:S(2)}) collective-permute-start(bf16[32,24,768]{2,1,0:T(8,128)(2,1)S(1)} %get-tuple-element.202), channel_id=1, source_target_pairs={{0,1},{1,0},{2,3},{3,2},{4,5},{5,4},{6,7},{7,6},{8,9},{9,8},{10,11... | collective-permute-start | bytes 3538952 | tf_op jit(solution)/shard_map/ppermute | solution.py:469
  102.5 11.5 %collective-permute-start.31 = (bf16[256,768]{1,0:T(8,128)(2,1)S(1)}, bf16[256,768]{1,0:T(8,128)(2,1)S(1)}, u32[]{:S(2)}, u32[]{:S(2)}) collective-permute-start(bf16[256,768]{1,0:T(8,128)(2,1)S(1)} %get-tuple-element.198), channel_id=1, source_target_pairs={{0,4},{1,5},{2,6},{3,7},{4,0},{5,1},{6,2},{7,3},{8,12},{9,13},{10,... | collective-permute-start | bytes 1179656 | tf_op jit(solution)/shard_map/ppermute | solution.py:469
  104.3 11.2 %collective-permute-start.30 = (bf16[256,768]{1,0:T(8,128)(2,1)S(1)}, bf16[256,768]{1,0:T(8,128)(2,1)S(1)}, u32[]{:S(2)}, u32[]{:S(2)}) collective-permute-start(bf16[256,768]{1,0:T(8,128)(2,1)S(1)} %get-tuple-element.191), channel_id=1, source_target_pairs={{0,2},{1,3},{2,0},{3,1},{4,6},{5,7},{6,4},{7,5},{8,10},{9,11},{10,... | collective-permute-start | bytes 1179656 | tf_op jit(solution)/shard_map/ppermute | solution.py:469
  106.1 9.3 %copy-start.3 = (bf16[32,24,768]{2,1,0:T(8,128)(2,1)S(1)}, bf16[32,24,768]{2,1,0:T(8,128)(2,1)}, u32[]{:S(2)}) copy-start(bf16[32,24,768]{2,1,0:T(8,128)(2,1)} %copy-done.2) | copy-start | bytes 3538948
  106.1 21.0 %collective-permute-start.38 = (bf16[2,8,24,768]{3,2,1,0:T(8,128)(2,1)S(1)}, bf16[2,8,24,768]{3,2,1,0:T(8,128)(2,1)S(1)}, u32[]{:S(2)}, u32[]{:S(2)}) collective-permute-start(bf16[2,8,24,768]{3,2,1,0:T(8,128)(2,1)S(1)} %get-tuple-element.213), channel_id=1, source_target_pairs={{0,8},{1,9},{2,10},{3,11},{4,12},{5,13},{6,14},{7,15},{8,0},{9,1},... | collective-permute-start | bytes 1769480 | tf_op jit(solution)/shard_map/ppermute | solution.py:475
  115.5 12.9 %copy-start.7 = (bf16[256,192]{1,0:T(8,128)(2,1)S(1)}, bf16[256,192]{1,0:T(8,128)(2,1)}, u32[]{:S(2)}) copy-start(bf16[256,192]{1,0:T(8,128)(2,1)} %copy-done.6) | copy-start | bytes 294916
  116.9 6.4 %collective-permute-start.33 = (bf16[256,192]{1,0:T(8,128)(2,1)S(1)}, bf16[256,192]{1,0:T(8,128)(2,1)S(1)}, u32[]{:S(2)}, u32[]{:S(2)}) collective-permute-start(bf16[256,192]{1,0:T(8,128)(2,1)S(1)} %get-tuple-element.205), channel_id=1, source_target_pairs={{0,2},{1,3},{2,0},{3,1},{4,6},{5,7},{6,4},{7,5},{8,10},{9,11},{10,... | collective-permute-start | bytes 294920 | tf_op jit(solution)/shard_map/ppermute | solution.py:469
  117.6 7.8 %collective-permute-start.34 = (bf16[256,192]{1,0:T(8,128)(2,1)S(1)}, bf16[256,192]{1,0:T(8,128)(2,1)S(1)}, u32[]{:S(2)}, u32[]{:S(2)}) collective-permute-start(bf16[256,192]{1,0:T(8,128)(2,1)S(1)} %get-tuple-element.206), channel_id=1, source_target_pairs={{0,4},{1,5},{2,6},{3,7},{4,0},{5,1},{6,2},{7,3},{8,12},{9,13},{10,... | collective-permute-start | bytes 294920 | tf_op jit(solution)/shard_map/ppermute | solution.py:469
  119.0 6.3 %collective-permute-start.35 = (bf16[256,192]{1,0:T(8,128)(2,1)S(1)}, bf16[256,192]{1,0:T(8,128)(2,1)S(1)}, u32[]{:S(2)}, u32[]{:S(2)}) collective-permute-start(bf16[256,192]{1,0:T(8,128)(2,1)S(1)} %get-tuple-element.207), channel_id=1, source_target_pairs={{0,6},{1,7},{2,4},{3,5},{4,2},{5,3},{6,0},{7,1},{8,14},{9,15},{10,... | collective-permute-start | bytes 294920 | tf_op jit(solution)/shard_map/ppermute | solution.py:469
  125.4 14.8 %collective-permute-start.36 = (bf16[256,768]{1,0:T(8,128)(2,1)S(1)}, bf16[256,768]{1,0:T(8,128)(2,1)S(1)}, u32[]{:S(2)}, u32[]{:S(2)}) collective-permute-start(bf16[256,768]{1,0:T(8,128)(2,1)S(1)} %get-tuple-element.208), channel_id=1, source_target_pairs={{0,2},{1,3},{2,0},{3,1},{4,6},{5,7},{6,4},{7,5},{8,10},{9,11},{10,... | collective-permute-start | bytes 1179656 | tf_op jit(solution)/shard_map/ppermute | solution.py:469
  126.4 13.7 %collective-permute-start.37 = (bf16[256,768]{1,0:T(8,128)(2,1)S(1)}, bf16[256,768]{1,0:T(8,128)(2,1)S(1)}, u32[]{:S(2)}, u32[]{:S(2)}) collective-permute-start(bf16[256,768]{1,0:T(8,128)(2,1)S(1)} %get-tuple-element.209), channel_id=1, source_target_pairs={{0,4},{1,5},{2,6},{3,7},{4,0},{5,1},{6,2},{7,3},{8,12},{9,13},{10,... | collective-permute-start | bytes 1179656 | tf_op jit(solution)/shard_map/ppermute | solution.py:469
  127.7 13.6 %collective-permute-start.39 = (bf16[8,24,768]{2,1,0:T(8,128)(2,1)S(1)}, bf16[8,24,768]{2,1,0:T(8,128)(2,1)S(1)}, u32[]{:S(2)}, u32[]{:S(2)}) collective-permute-start(bf16[8,24,768]{2,1,0:T(8,128)(2,1)S(1)} %pass_f.1), channel_id=1, source_target_pairs={{0,16},{1,17},{2,18},{3,19},{4,20},{5,21},{6,22},{7,23},{8,24},{9,... | collective-permute-start | bytes 884744 | tf_op jit(solution)/shard_map/ppermute | solution.py:475
  140.0 5.6 %collective-permute-start.49 = (bf16[16,24,768]{2,1,0:T(8,128)(2,1)S(1)}, bf16[16,24,768]{2,1,0:T(8,128)(2,1)S(1)}, u32[]{:S(2)}, u32[]{:S(2)}) collective-permute-start(bf16[16,24,768]{2,1,0:T(8,128)(2,1)S(1)} %get-tuple-element.255), channel_id=1, source_target_pairs={{0,1},{1,0},{2,3},{3,2},{4,5},{5,4},{6,7},{7,6},{8,9},{9,8},{10,11... | collective-permute-start | bytes 1769480 | tf_op jit(solution)/shard_map/ppermute | solution.py:469
  143.4 9.9 %collective-permute-start.40 = (bf16[16,24,640]{2,1,0:T(8,128)(2,1)S(1)}, bf16[16,24,640]{2,1,0:T(8,128)(2,1)S(1)}, u32[]{:S(2)}, u32[]{:S(2)}) collective-permute-start(bf16[16,24,640]{2,1,0:T(8,128)(2,1)S(1)} %get-tuple-element.232), channel_id=1, source_target_pairs={{0,1},{1,0},{2,3},{3,2},{4,5},{5,4},{6,7},{7,6},{8,9},{9,8},{10,11... | collective-permute-start | bytes 1474568 | tf_op jit(solution)/shard_map/ppermute | solution.py:469
  143.5 7.3 %collective-permute-start.44 = (bf16[128,768]{1,0:T(8,128)(2,1)S(1)}, bf16[128,768]{1,0:T(8,128)(2,1)S(1)}, u32[]{:S(2)}, u32[]{:S(2)}) collective-permute-start(bf16[128,768]{1,0:T(8,128)(2,1)S(1)} %get-tuple-element.243), channel_id=1, source_target_pairs={{0,2},{1,3},{2,0},{3,1},{4,6},{5,7},{6,4},{7,5},{8,10},{9,11},{10,... | collective-permute-start | bytes 589832 | tf_op jit(solution)/shard_map/ppermute | solution.py:469
  144.8 7.0 %collective-permute-start.45 = (bf16[128,768]{1,0:T(8,128)(2,1)S(1)}, bf16[128,768]{1,0:T(8,128)(2,1)S(1)}, u32[]{:S(2)}, u32[]{:S(2)}) collective-permute-start(bf16[128,768]{1,0:T(8,128)(2,1)S(1)} %get-tuple-element.244), channel_id=1, source_target_pairs={{0,4},{1,5},{2,6},{3,7},{4,0},{5,1},{6,2},{7,3},{8,12},{9,13},{10,... | collective-permute-start | bytes 589832 | tf_op jit(solution)/shard_map/ppermute | solution.py:469
  146.3 10.7 %collective-permute-start.50 = (bf16[2,4,24,768]{3,2,1,0:T(8,128)(2,1)S(1)}, bf16[2,4,24,768]{3,2,1,0:T(8,128)(2,1)S(1)}, u32[]{:S(2)}, u32[]{:S(2)}) collective-permute-start(bf16[2,4,24,768]{3,2,1,0:T(8,128)(2,1)S(1)} %get-tuple-element.257), channel_id=1, source_target_pairs={{0,8},{1,9},{2,10},{3,11},{4,12},{5,13},{6,14},{7,15},{8,0},{9,1},... | collective-permute-start | bytes 884744 | tf_op jit(solution)/shard_map/ppermute | solution.py:475
  152.4 22.4 %collective-permute-start.46 = (bf16[256,768]{1,0:T(8,128)(2,1)S(1)}, bf16[256,768]{1,0:T(8,128)(2,1)S(1)}, u32[]{:S(2)}, u32[]{:S(2)}) collective-permute-start(bf16[256,768]{1,0:T(8,128)(2,1)S(1)} %get-tuple-element.247), channel_id=1, source_target_pairs={{0,2},{1,3},{2,0},{3,1},{4,6},{5,7},{6,4},{7,5},{8,10},{9,11},{10,... | collective-permute-start | bytes 1179656 | tf_op jit(solution)/shard_map/ppermute | solution.py:469
  154.0 8.6 %collective-permute-start.42 = (bf16[2,4,24,640]{3,2,1,0:T(8,128)(2,1)S(1)}, bf16[2,4,24,640]{3,2,1,0:T(8,128)(2,1)S(1)}, u32[]{:S(2)}, u32[]{:S(2)}) collective-permute-start(bf16[2,4,24,640]{3,2,1,0:T(8,128)(2,1)S(1)} %get-tuple-element.236), channel_id=1, source_target_pairs={{0,8},{1,9},{2,10},{3,11},{4,12},{5,13},{6,14},{7,15},{8,0},{9,1},... | collective-permute-start | bytes 737288 | tf_op jit(solution)/shard_map/ppermute | solution.py:475
  154.2 22.0 %collective-permute-start.47 = (bf16[256,768]{1,0:T(8,128)(2,1)S(1)}, bf16[256,768]{1,0:T(8,128)(2,1)S(1)}, u32[]{:S(2)}, u32[]{:S(2)}) collective-permute-start(bf16[256,768]{1,0:T(8,128)(2,1)S(1)} %get-tuple-element.248), channel_id=1, source_target_pairs={{0,4},{1,5},{2,6},{3,7},{4,0},{5,1},{6,2},{7,3},{8,12},{9,13},{10,... | collective-permute-start | bytes 1179656 | tf_op jit(solution)/shard_map/ppermute | solution.py:469
  155.5 21.9 %collective-permute-start.41 = (bf16[256,768]{1,0:T(8,128)(2,1)S(1)}, bf16[256,768]{1,0:T(8,128)(2,1)S(1)}, u32[]{:S(2)}, u32[]{:S(2)}) collective-permute-start(bf16[256,768]{1,0:T(8,128)(2,1)S(1)} %get-tuple-element.234), channel_id=1, source_target_pairs={{0,6},{1,7},{2,4},{3,5},{4,2},{5,3},{6,0},{7,1},{8,14},{9,15},{10,... | collective-permute-start | bytes 1179656 | tf_op jit(solution)/shard_map/ppermute | solution.py:469
  157.6 12.4 %collective-permute-start.51 = (bf16[4,24,768]{2,1,0:T(8,128)(2,1)S(1)}, bf16[4,24,768]{2,1,0:T(8,128)(2,1)S(1)}, u32[]{:S(2)}, u32[]{:S(2)}) collective-permute-start(bf16[4,24,768]{2,1,0:T(8,128)(2,1)S(1)} %pass_o.1), channel_id=1, source_target_pairs={{0,16},{1,17},{2,18},{3,19},{4,20},{5,21},{6,22},{7,23},{8,24},{9,... | collective-permute-start | bytes 442376 | tf_op jit(solution)/shard_map/ppermute | solution.py:475
  163.2 8.2 %collective-permute-start.52 = (bf16[4,24,640]{2,1,0:T(8,128)(2,1)S(1)}, bf16[4,24,640]{2,1,0:T(8,128)(2,1)S(1)}, u32[]{:S(2)}, u32[]{:S(2)}) collective-permute-start(bf16[4,24,640]{2,1,0:T(8,128)(2,1)S(1)} %pass_r.1), channel_id=1, source_target_pairs={{0,16},{1,17},{2,18},{3,19},{4,20},{5,21},{6,22},{7,23},{8,24},{9,... | collective-permute-start | bytes 368648 | tf_op jit(solution)/shard_map/ppermute | solution.py:475
  172.7 6.0 %collective-permute-start.53 = (bf16[24,2176]{1,0:T(8,128)(2,1)S(1)}, bf16[24,2176]{1,0:T(8,128)(2,1)S(1)}, u32[]{:S(2)}, u32[]{:S(2)}) collective-permute-start(bf16[24,2176]{1,0:T(8,128)(2,1)S(1)} %get-tuple-element.261), channel_id=1, source_target_pairs={{0,2},{1,3},{2,0},{3,1},{4,6},{5,7},{6,4},{7,5},{8,10},{9,11},{10,... | collective-permute-start | bytes 313352 | tf_op jit(solution)/shard_map/ppermute | solution.py:469
  173.5 5.4 %collective-permute-start.54 = (bf16[24,2176]{1,0:T(8,128)(2,1)S(1)}, bf16[24,2176]{1,0:T(8,128)(2,1)S(1)}, u32[]{:S(2)}, u32[]{:S(2)}) collective-permute-start(bf16[24,2176]{1,0:T(8,128)(2,1)S(1)} %get-tuple-element.262), channel_id=1, source_target_pairs={{0,4},{1,5},{2,6},{3,7},{4,0},{5,1},{6,2},{7,3},{8,12},{9,13},{10,... | collective-permute-start | bytes 313352 | tf_op jit(solution)/shard_map/ppermute | solution.py:469
  174.8 5.6 %collective-permute-start.55 = (bf16[24,2176]{1,0:T(8,128)(2,1)S(1)}, bf16[24,2176]{1,0:T(8,128)(2,1)S(1)}, u32[]{:S(2)}, u32[]{:S(2)}) collective-permute-start(bf16[24,2176]{1,0:T(8,128)(2,1)S(1)} %get-tuple-element.263), channel_id=1, source_target_pairs={{0,6},{1,7},{2,4},{3,5},{4,2},{5,3},{6,0},{7,1},{8,14},{9,15},{10,... | collective-permute-start | bytes 313352 | tf_op jit(solution)/shard_map/ppermute | solution.py:469
  177.3 4.7 %collective-permute-start.48 = (f32[128,768]{1,0:T(8,128)S(1)}, f32[128,768]{1,0:T(8,128)S(1)}, u32[]{:S(2)}, u32[]{:S(2)}) collective-permute-start(f32[128,768]{1,0:T(8,128)S(1)} %get-tuple-element.251), channel_id=1, source_target_pairs={{0,1},{1,0},{2,3},{3,2},{4,5},{5,4},{6,7},{7,6},{8,9},{9,8},{10,11... | collective-permute-start | bytes 1179656 | tf_op jit(solution)/shard_map/ppermute | solution.py:469
  178.2 3.8 %collective-permute-start.43 = (bf16[128,768]{1,0:T(8,128)(2,1)S(1)}, bf16[128,768]{1,0:T(8,128)(2,1)S(1)}, u32[]{:S(2)}, u32[]{:S(2)}) collective-permute-start(bf16[128,768]{1,0:T(8,128)(2,1)S(1)} %get-tuple-element.239), channel_id=1, source_target_pairs={{0,1},{1,0},{2,3},{3,2},{4,5},{5,4},{6,7},{7,6},{8,9},{9,8},{10,11... | collective-permute-start | bytes 589832 | tf_op jit(solution)/shard_map/ppermute | solution.py:469
  (10 other events, 35.7 us)

commit v3 on v2

--- a/solution.py
+++ b/solution.py
@@ -652,7 +652,9 @@
         factor = lax.rsqrt(jnp.mean(x * x, axis=-1, keepdims=True) + EPS)
         a_out[pl.ds(at, hi - lo), :] = (x * factor * gain).astype(BF16)
 
-    lin[8:1032, :] = dot_nn(a_out[...], w_out[...])
+    for b in range(4):
+        at = 256 * b
+        lin[at + 8 : at + 264, :] = dot_nn(a_out[at : at + 256, :], w_out[...])
     for b in range(4):
         t = 256 * b
         mixed[...] = (

time: 184 us -> 184 us (level)
  no operation moved by 1% of the time
where the time goes in v3:
time: 184 us
  waiting for transfers between devices  62.8 us (34%)
  Pallas kernels  59.1 us (32%)
  starting transfers between devices  57.8 us (31%)
  local copies, waits for them, and re-layouts  2.74 us (1%)
    pallas_call x31, Pallas kernels, call(): pl.pallas_call(body, out_shape=out_shape, compiler_params=pltpu.CompilerP...  59.1 us
    ppermute x44, starting transfers between devices, send(): return lax.ppermute(value, ('dp', 'ctx'), pairs)  45.6 us
    ppermute x44, waiting for transfers between devices, send(): return lax.ppermute(value, ('dp', 'ctx'), pairs)  43.5 us
    ppermute x12, waiting for transfers between devices, send_z(): return lax.ppermute(value, ('dp', 'ctx'), pairs)  19.3 us
    ppermute x12, starting transfers between devices, send_z(): return lax.ppermute(value, ('dp', 'ctx'), pairs)  12.2 us
  transfers between devices with their start and end apart: 56, of which 27 were waited for; matrix products, arithmetic and copies ran while one was open for 1% of the time, Pallas kernels for 27%

profile of v3, /device:TPU:0, one launch (start us, length us, event | category | flops | bytes accessed | tf_op | source)
XLA Modules:
  0.0 183.7 jit_solution(17640003010556937711)
XLA Ops:
  1.2 1.9 %pack.1 = (bf16[24,2176]{1,0:T(8,128)(2,1)S(1)}, bf16[24,2176]{1,0:T(8,128)(2,1)S(1)}, bf16[24,2176]{1,0:T(8,128)(2,1)S(1)}, bf16[24,2176]{1,0:T(8,128)(2,1)S(1)}) custom-call(s32[3]{0:T(128)S(1)} %pad_add_fusion.ids, bf16[24,768]{1,0:T(8,128)(2,1)} %wq.1, bf16[24,768]{1,0:T(8,128)(2,1)} %wk.1, bf16[24,768]{1,0:T(8,128)(2,1)} %wv.1, bf16[24,3072]{1,0:T(8,128)(2,1)} %up.1, ...), custom_call_target="tpu_custom_call" | custom-call | flops 1 | bytes 1 | tf_op jit(solution)/shard_map/pack/pallas_call | solution.py:454
  3.1 2.6 %collective-permute-start = (bf16[24,2176]{1,0:T(8,128)(2,1)S(1)}, bf16[24,2176]{1,0:T(8,128)(2,1)S(1)}, u32[]{:S(2)}, u32[]{:S(2)}) collective-permute-start(bf16[24,2176]{1,0:T(8,128)(2,1)S(1)} %get-tuple-element.148), channel_id=1, source_target_pairs={{0,2},{1,3},{2,0},{3,1},{4,6},{5,7},{6,4},{7,5},{8,10},{9,11},{10,... | collective-permute-start | bytes 313352 | tf_op jit(solution)/shard_map/ppermute | solution.py:469
  5.7 1.5 collective-permute-start.1
  7.3 2.0 %collective-permute-done.p1 = bf16[24,2176]{1,0:T(8,128)(2,1)S(1)} collective-permute-done((bf16[24,2176]{1,0:T(8,128)(2,1)S(1)}, bf16[24,2176]{1,0:T(8,128)(2,1)S(1)}, u32[]{:S(2)}, u32[]{:S(2)}) %collective-permute-start) | collective-permute-done | bytes 104480 | tf_op jit(solution)/shard_map/ppermute | solution.py:469
  9.3 1.5 place_x.1.refs_2_.xw
  10.8 1.8 collective-permute-start.10
  13.6 3.7 %collective-permute-start.5 = (bf16[4,24,640]{2,1,0:T(8,128)(2,1)S(1)}, bf16[4,24,640]{2,1,0:T(8,128)(2,1)S(1)}, u32[]{:S(2)}, u32[]{:S(2)}) collective-permute-start(bf16[4,24,640]{2,1,0:T(8,128)(2,1)S(1)} %get-tuple-element.151.s0), channel_id=1, source_target_pairs={{0,24},{1,25},{2,26},{3,27},{4,28},{5,29},{6,30},{7,31},{8,16},{9,... | collective-permute-start | bytes 368648 | tf_op jit(solution)/shard_map/ppermute | solution.py:475
  18.0 1.6 collective-permute-start.9
  19.6 1.4 with_down.1.s0
  21.5 5.3 %collective-permute-done.4.s2 = bf16[4,24,640]{2,1,0:T(8,128)(2,1)S(1)} collective-permute-done((bf16[4,24,640]{2,1,0:T(8,128)(2,1)S(1)}, bf16[4,24,640]{2,1,0:T(8,128)(2,1)S(1)}, u32[]{:S(2)}, u32[]{:S(2)}) %collective-permute-start.4) | collective-permute-done | bytes 122912 | tf_op jit(solution)/shard_map/ppermute | solution.py:475
  28.3 2.8 %collective-permute-start.16 = (bf16[12,24,768]{2,1,0:T(8,128)(2,1)S(1)}, bf16[12,24,768]{2,1,0:T(8,128)(2,1)}, u32[]{:S(2)}, u32[]{:S(2)}) collective-permute-start(bf16[12,24,768]{2,1,0:T(8,128)(2,1)S(1)} %with_down.1.s0), channel_id=1, source_target_pairs={{0,8},{1,9},{2,10},{3,11},{4,12},{5,13},{6,14},{7,15},{8,0},{9,1},... | collective-permute-start | bytes 1327112 | tf_op jit(solution)/shard_map/ppermute | solution.py:475
  31.8 1.9 %collective-permute-start.11 = (bf16[128,768]{1,0:T(8,128)(2,1)S(1)}, bf16[128,768]{1,0:T(8,128)(2,1)S(1)}, u32[]{:S(2)}, u32[]{:S(2)}) collective-permute-start(bf16[128,768]{1,0:T(8,128)(2,1)S(1)} %slice.24), channel_id=1, source_target_pairs={{0,4},{1,5},{2,6},{3,7},{4,0},{5,1},{6,2},{7,3},{8,12},{9,13},{10,... | collective-permute-start | bytes 589832 | tf_op jit(solution)/shard_map/ppermute | solution.py:469
  34.3 1.5 place_g.1.g0.gw.g
  36.5 1.5 collective-permute-start.20
  38.4 2.1 %collective-permute-start.19 = (bf16[256,768]{1,0:T(8,128)(2,1)S(1)}, bf16[256,768]{1,0:T(8,128)(2,1)S(1)}, u32[]{:S(2)}, u32[]{:S(2)}) collective-permute-start(bf16[256,768]{1,0:T(8,128)(2,1)S(1)} %place_g.1.g0.gw.g), channel_id=1, source_target_pairs={{0,2},{1,3},{2,0},{3,1},{4,6},{5,7},{6,4},{7,5},{8,10},{9,11},{10,... | collective-permute-start | bytes 1179656 | tf_op jit(solution)/shard_map/ppermute | solution.py:469
  40.6 1.0 copy-done.9
  41.6 9.2 %attend.1 = (bf16[768,576]{1,0:T(8,128)(2,1)S(1)}, f32[1,768]{1,0:T(1,128)S(1)}, bf16[1024,768]{1,0:T(8,128)(2,1)S(1)}, f32[1032,576]{1,0:T(8,128)S(1)}, bf16[3,...) custom-call(s32[3]{0:T(128)S(1)} %pad_add_fusion.ids, ...), custom_call_target="tpu_custom_call" | custom-call | flops 1 | bytes 1 | tf_op jit(solution)/shard_map/attend/pallas_call | solution.py:454
  51.3 1.5 collective-permute-start.22
  53.3 1.5 collective-permute-start.14
  55.4 6.5 %collective-permute-done.14.t2 = bf16[256,192]{1,0:T(8,128)(2,1)S(1)} collective-permute-done((bf16[256,192]{1,0:T(8,128)(2,1)S(1)}, bf16[256,192]{1,0:T(8,128)(2,1)S(1)}, u32[]{:S(2)}, u32[]{:S(2)}) %collective-permute-start.14) | collective-permute-done | bytes 98336 | tf_op jit(solution)/shard_map/ppermute | solution.py:469
  62.8 1.3 stack_b.1.mine
  64.2 1.9 %collective-permute-start.15 = (bf16[256,192]{1,0:T(8,128)(2,1)S(1)}, bf16[256,192]{1,0:T(8,128)(2,1)S(1)}, u32[]{:S(2)}, u32[]{:S(2)}) collective-permute-start(bf16[256,192]{1,0:T(8,128)(2,1)S(1)} %get-tuple-element.163), channel_id=1, source_target_pairs={{0,6},{1,7},{2,4},{3,5},{4,2},{5,3},{6,0},{7,1},{8,14},{9,15},{10,... | collective-permute-start | bytes 294920 | tf_op jit(solution)/shard_map/ppermute | solution.py:469
  66.1 1.7 collective-permute-done.23.other
  68.7 2.3 %collective-permute-done.15.t3 = bf16[256,192]{1,0:T(8,128)(2,1)S(1)} collective-permute-done((bf16[256,192]{1,0:T(8,128)(2,1)S(1)}, bf16[256,192]{1,0:T(8,128)(2,1)S(1)}, u32[]{:S(2)}, u32[]{:S(2)}) %collective-permute-start.15) | collective-permute-done | bytes 98336 | tf_op jit(solution)/shard_map/ppermute | solution.py:469
  71.0 1.2 resid.1
  72.3 1.9 %collective-permute-start.25 = (bf16[256,768]{1,0:T(8,128)(2,1)S(1)}, bf16[256,768]{1,0:T(8,128)(2,1)S(1)}, u32[]{:S(2)}, u32[]{:S(2)}) collective-permute-start(bf16[256,768]{1,0:T(8,128)(2,1)S(1)} %get-tuple-element.175.refs_0_), channel_id=1, source_target_pairs={{0,4},{1,5},{2,6},{3,7},{4,0},{5,1},{6,2},{7,3},{8,12},{9,13},{10,... | collective-permute-start | bytes 1179656 | tf_op jit(solution)/shard_map/ppermute | solution.py:469
  74.7 8.4 %collective-permute-done.25.refs_2_ = bf16[256,768]{1,0:T(8,128)(2,1)S(1)} collective-permute-done((bf16[256,768]{1,0:T(8,128)(2,1)S(1)}, bf16[256,768]{1,0:T(8,128)(2,1)S(1)}, u32[]{:S(2)}, u32[]{:S(2)}) %collective-permute-start.25) | collective-permute-done | bytes 393248 | tf_op jit(solution)/shard_map/ppermute | solution.py:469
  83.1 1.8 collective-permute-start.27
  85.6 2.2 %hidden_grad.1 = (bf16[1024,768]{1,0:T(8,128)(2,1)S(1)}, bf16[1024,768]{1,0:T(8,128)(2,1)S(1)}) custom-call(s32[3]{0:T(128)S(1)} %pad_add_fusion.ids, bf16[256,768]{1,0:T(8,128)(2,1)S(1)} %place_g.1.g0.gw.g, bf16[256,768]{1,0:T(8,128)(2,1)S(1)} %collective-permute-done.19.g1, bf16[256,768]{1,0:T(8,128)(2,1)S(1)} %collective-permute-done.20.g2, ...), custom_call_target="tpu_custom_call" | custom-call | flops 1 | bytes 1 | tf_op jit(solution)/shard_map/hidden_grad/pallas_call | solution.py:454
  87.8 1.1 collective-permute-done.27.refs_4_
  88.9 1.8 %collective-permute-done.26.refs_3_ = bf16[128,768]{1,0:T(8,128)(2,1)S(1)} collective-permute-done((bf16[128,768]{1,0:T(8,128)(2,1)S(1)}, bf16[128,768]{1,0:T(8,128)(2,1)S(1)}, u32[]{:S(2)}, u32[]{:S(2)}) %collective-permute-start.26) | collective-permute-done | bytes 196640 | tf_op jit(solution)/shard_map/ppermute | solution.py:469
  90.7 4.2 %ffn.1 = (bf16[1024,768]{1,0:T(8,128)(2,1)S(1)}, bf16[1024,768]{1,0:T(8,128)(2,1)S(1)}, bf16[1024,768]{1,0:T(8,128)(2,1)S(1)}, bf16[256,768]{1,0:T(8,128)(2,1)S(...) custom-call(s32[3]{0:T(128)S(1)} %pad_add_fusion.ids, ...), custom_call_target="tpu_custom_call" | custom-call | flops 1 | bytes 1 | tf_op jit(solution)/shard_map/ffn/pallas_call | solution.py:454
  95.1 1.7 collective-permute-start.29
  96.9 3.4 %ffn_grads.1 = (bf16[32,24,768]{2,1,0:T(8,128)(2,1)S(1)}, bf16[32,24,768]{2,1,0:T(8,128)(2,1)S(1)}, f32[1,768]{1,0:T(1,128)S(1)}) custom-call(s32[3]{0:T(128)S(1)} %pad_add_fusion.ids, bf16[1024,768]{1,0:T(8,128)(2,1)S(1)} %get-tuple-element.185.a_all, bf16[1024,768]{1,0:T(8,128)(2,1)S(1)} %get-tuple-element.186.g_all, ...), custom_call_target="tpu_custom_call" | custom-call | flops 999999995904 | bytes 1 | tf_op jit(solution)/shard_map/ffn_grads/pallas_call | solution.py:454
  101.1 1.3 add_half.2
  102.5 1.8 collective-permute-start.31
  106.9 1.9 %ffn_out.1 = (bf16[256,768]{1,0:T(8,128)(2,1)S(1)}, bf16[256,768]{1,0:T(8,128)(2,1)S(1)}, bf16[256,768]{1,0:T(8,128)(2,1)S(1)}, bf16[256,768]{1,0:T(8,128)(2,1)S(1)}) custom-call(s32[3]{0:T(128)S(1)} %pad_add_fusion.ids, bf16[1024,768]{1,0:T(8,128)(2,1)S(1)} %get-tuple-element.180.hsq, bf16[768,768]{1,0:T(8,128)(2,1)S(1)} %bitcast.7), custom_call_target="tpu_custom_call" | custom-call | flops 1 | bytes 1 | tf_op jit(solution)/shard_map/ffn_out/pallas_call | solution.py:454
  108.8 5.1 %collective-permute-done.31.p2 = bf16[256,768]{1,0:T(8,128)(2,1)S(1)} collective-permute-done((bf16[256,768]{1,0:T(8,128)(2,1)S(1)}, bf16[256,768]{1,0:T(8,128)(2,1)S(1)}, u32[]{:S(2)}, u32[]{:S(2)}) %collective-permute-start.31) | collective-permute-done | bytes 393248 | tf_op jit(solution)/shard_map/ppermute | solution.py:469
  114.0 1.5 collective-permute-done.30.p1
  115.5 1.5 mid_grad.1
  117.6 1.5 collective-permute-start.34
  119.0 1.4 collective-permute-start.35
  120.5 2.8 %collective-permute-done.33.d1 = bf16[256,192]{1,0:T(8,128)(2,1)S(1)} collective-permute-done((bf16[256,192]{1,0:T(8,128)(2,1)S(1)}, bf16[256,192]{1,0:T(8,128)(2,1)S(1)}, u32[]{:S(2)}, u32[]{:S(2)}) %collective-permute-start.33) | collective-permute-done | bytes 98336 | tf_op jit(solution)/shard_map/ppermute | solution.py:469
  123.3 2.1 %collective-permute-done.34.d2 = bf16[256,192]{1,0:T(8,128)(2,1)S(1)} collective-permute-done((bf16[256,192]{1,0:T(8,128)(2,1)S(1)}, bf16[256,192]{1,0:T(8,128)(2,1)S(1)}, u32[]{:S(2)}, u32[]{:S(2)}) %collective-permute-start.34) | collective-permute-done | bytes 98336 | tf_op jit(solution)/shard_map/ppermute | solution.py:469
  125.4 1.0 collective-permute-start.36
  128.4 1.1 out_grads.1
  129.5 10.5 %attend_grad.1 = (bf16[1024,576]{1,0:T(8,128)(2,1)S(1)}, f32[3,576]{1,0:T(4,128)S(1)}, bf16[256,768]{1,0:T(8,128)(2,1)S(1)}, bf16[256,768]{1,0:T(8,128)(2,1)S(1)...) custom-call(s32[3]{0:T(128)S(1)} %pad_add_fusion.ids, ...), custom_call_target="tpu_custom_call" | custom-call | flops 1 | bytes 1 | tf_op jit(solution)/shard_map/attend_grad/pallas_call | solution.py:454
  140.2 1.2 collective-permute-done.39.refs_2_
  141.3 2.1 %proj_grads.1 = (bf16[16,24,640]{2,1,0:T(8,128)(2,1)S(1)}, bf16[16,24,640]{2,1,0:T(8,128)(2,1)S(1)}) custom-call(s32[3]{0:T(128)S(1)} %pad_add_fusion.ids, bf16[1024,768]{1,0:T(8,128)(2,1)S(1)} %get-tuple-element.215.a1, bf16[1024,576]{1,0:T(8,128)(2,1)S(1)} %get-tuple-element.228.dlin, f32[3,576]{1,0:T(4,128)S(1)} %get-tuple-element.229.conv, ...), custom_call_target="tpu_custom_call" | custom-call | flops 1 | bytes 1 | tf_op jit(solution)/shard_map/proj_grads/pallas_call | solution.py:454
  143.5 1.3 collective-permute-start.44
  147.2 3.6 %collective-permute-done.44.low = bf16[128,768]{1,0:T(8,128)(2,1)S(1)} collective-permute-done((bf16[128,768]{1,0:T(8,128)(2,1)S(1)}, bf16[128,768]{1,0:T(8,128)(2,1)S(1)}, u32[]{:S(2)}, u32[]{:S(2)}) %collective-permute-start.44) | collective-permute-done | bytes 196640 | tf_op jit(solution)/shard_map/ppermute | solution.py:469
  154.2 1.3 collective-permute-start.47
  155.5 1.5 collective-permute-start.41
  157.6 1.7 collective-permute-start.51
  159.3 3.3 %collective-permute-done.42.got.refs_7_ = bf16[2,4,24,640]{3,2,1,0:T(8,128)(2,1)S(1)} collective-permute-done((bf16[2,4,24,640]{3,2,1,0:T(8,128)(2,1)S(1)}, bf16[2,4,24,640]{3,2,1,0:T(8,128)(2,1)S(1)}, u32[]{:S(2)}, u32[]{:S(2)}) %collective-permute-start.42) | collective-permute-done | bytes 245792 | tf_op jit(solution)/shard_map/ppermute | solution.py:475
  163.3 6.7 %collective-permute-done.51.refs_5_ = bf16[4,24,768]{2,1,0:T(8,128)(2,1)S(1)} collective-permute-done((bf16[4,24,768]{2,1,0:T(8,128)(2,1)S(1)}, bf16[4,24,768]{2,1,0:T(8,128)(2,1)S(1)}, u32[]{:S(2)}, u32[]{:S(2)}) %collective-permute-start.51) | collective-permute-done | bytes 147488 | tf_op jit(solution)/shard_map/ppermute | solution.py:475
  170.0 1.3 collective-permute-done.52.refs_8_
  171.3 1.4 sum_planes.1
  173.5 1.3 collective-permute-start.54
  174.8 1.4 collective-permute-start.55
  176.2 1.0 input_grad.1
  178.9 1.5 collective-permute-done.55.s3
  180.4 1.6 owned.1
  182.1 1.6 deliver.1
  (123 shorter events, 27.5 us)
Async XLA Ops:
  0.6 8.7 %collective-permute-start.8 = (bf16[2,1,128,768]{3,2,1,0:T(8,128)(2,1)}, bf16[2,1,128,768]{3,2,1,0:T(8,128)(2,1)S(1)}, u32[]{:S(2)}, u32[]{:S(2)}) collective-permute-start(bf16[2,1,128,768]{3,2,1,0:T(8,128)(2,1)} %mine.3), channel_id=1, source_target_pairs={{0,1},{1,0},{2,3},{3,2},{4,5},{5,4},{6,7},{7,6},{8,9},{9,8},{10,11... | collective-permute-start | bytes 1179656 | tf_op jit(solution)/shard_map/ppermute | solution.py:469
  3.1 6.2 %collective-permute-start = (bf16[24,2176]{1,0:T(8,128)(2,1)S(1)}, bf16[24,2176]{1,0:T(8,128)(2,1)S(1)}, u32[]{:S(2)}, u32[]{:S(2)}) collective-permute-start(bf16[24,2176]{1,0:T(8,128)(2,1)S(1)} %get-tuple-element.148), channel_id=1, source_target_pairs={{0,2},{1,3},{2,0},{3,1},{4,6},{5,7},{6,4},{7,5},{8,10},{9,11},{10,... | collective-permute-start | bytes 313352 | tf_op jit(solution)/shard_map/ppermute | solution.py:469
  5.7 6.9 %collective-permute-start.1 = (bf16[24,2176]{1,0:T(8,128)(2,1)S(1)}, bf16[24,2176]{1,0:T(8,128)(2,1)S(1)}, u32[]{:S(2)}, u32[]{:S(2)}) collective-permute-start(bf16[24,2176]{1,0:T(8,128)(2,1)S(1)} %get-tuple-element.149), channel_id=1, source_target_pairs={{0,4},{1,5},{2,6},{3,7},{4,0},{5,1},{6,2},{7,3},{8,12},{9,13},{10,... | collective-permute-start | bytes 313352 | tf_op jit(solution)/shard_map/ppermute | solution.py:469
  7.3 20.2 %copy-start.16 = (bf16[2,1,128,768]{3,2,1,0:T(8,128)(2,1)S(1)}, bf16[2,1,128,768]{3,2,1,0:T(8,128)(2,1)}, u32[]{:S(2)}) copy-start(bf16[2,1,128,768]{3,2,1,0:T(8,128)(2,1)} %mine.2) | copy-start | bytes 1179652
  7.3 5.7 %collective-permute-start.2 = (bf16[24,2176]{1,0:T(8,128)(2,1)S(1)}, bf16[24,2176]{1,0:T(8,128)(2,1)S(1)}, u32[]{:S(2)}, u32[]{:S(2)}) collective-permute-start(bf16[24,2176]{1,0:T(8,128)(2,1)S(1)} %get-tuple-element.150), channel_id=1, source_target_pairs={{0,6},{1,7},{2,4},{3,5},{4,2},{5,3},{6,0},{7,1},{8,14},{9,15},{10,... | collective-permute-start | bytes 313352 | tf_op jit(solution)/shard_map/ppermute | solution.py:469
  10.8 17.5 %collective-permute-start.10 = (bf16[256,768]{1,0:T(8,128)(2,1)S(1)}, bf16[256,768]{1,0:T(8,128)(2,1)S(1)}, u32[]{:S(2)}, u32[]{:S(2)}) collective-permute-start(bf16[256,768]{1,0:T(8,128)(2,1)S(1)} %place_x.1.refs_2_.xw), channel_id=1, source_target_pairs={{0,4},{1,5},{2,6},{3,7},{4,0},{5,1},{6,2},{7,3},{8,12},{9,13},{10,... | collective-permute-start | bytes 1179656 | tf_op jit(solution)/shard_map/ppermute | solution.py:469
  13.6 7.9 %collective-permute-start.5 = (bf16[4,24,640]{2,1,0:T(8,128)(2,1)S(1)}, bf16[4,24,640]{2,1,0:T(8,128)(2,1)S(1)}, u32[]{:S(2)}, u32[]{:S(2)}) collective-permute-start(bf16[4,24,640]{2,1,0:T(8,128)(2,1)S(1)} %get-tuple-element.151.s0), channel_id=1, source_target_pairs={{0,24},{1,25},{2,26},{3,27},{4,28},{5,29},{6,30},{7,31},{8,16},{9,... | collective-permute-start | bytes 368648 | tf_op jit(solution)/shard_map/ppermute | solution.py:475
  17.2 9.6 %collective-permute-start.4 = (bf16[4,24,640]{2,1,0:T(8,128)(2,1)S(1)}, bf16[4,24,640]{2,1,0:T(8,128)(2,1)S(1)}, u32[]{:S(2)}, u32[]{:S(2)}) collective-permute-start(bf16[4,24,640]{2,1,0:T(8,128)(2,1)S(1)} %get-tuple-element.151.s0), channel_id=1, source_target_pairs={{0,16},{1,17},{2,18},{3,19},{4,20},{5,21},{6,22},{7,23},{8,24},{9,... | collective-permute-start | bytes 368648 | tf_op jit(solution)/shard_map/ppermute | solution.py:475
  17.2 9.6 %collective-permute-start.3 = (bf16[4,24,640]{2,1,0:T(8,128)(2,1)S(1)}, bf16[4,24,640]{2,1,0:T(8,128)(2,1)S(1)}, u32[]{:S(2)}, u32[]{:S(2)}) collective-permute-start(bf16[4,24,640]{2,1,0:T(8,128)(2,1)S(1)} %get-tuple-element.151.s0), channel_id=1, source_target_pairs={{0,8},{1,9},{2,10},{3,11},{4,12},{5,13},{6,14},{7,15},{8,0},{9,1},... | collective-permute-start | bytes 368648 | tf_op jit(solution)/shard_map/ppermute | solution.py:475
  18.0 13.7 %collective-permute-start.9 = (bf16[256,768]{1,0:T(8,128)(2,1)S(1)}, bf16[256,768]{1,0:T(8,128)(2,1)S(1)}, u32[]{:S(2)}, u32[]{:S(2)}) collective-permute-start(bf16[256,768]{1,0:T(8,128)(2,1)S(1)} %place_x.1.refs_2_.xw), channel_id=1, source_target_pairs={{0,2},{1,3},{2,0},{3,1},{4,6},{5,7},{6,4},{7,5},{8,10},{9,11},{10,... | collective-permute-start | bytes 1179656 | tf_op jit(solution)/shard_map/ppermute | solution.py:469
  21.0 19.5 %copy-start.17 = (s32[2,1]{0,1:T(1,128)S(1)}, s32[2,1]{0,1:T(1,128)}, u32[]{:S(2)}) copy-start(s32[2,1]{0,1:T(1,128)} %param.19) | copy-start | bytes 28
  27.4 8.3 %collective-permute-start.7 = (bf16[4,4,24,640]{3,2,1,0:T(8,128)(2,1)S(1)}, bf16[4,4,24,640]{3,2,1,0:T(8,128)(2,1)S(1)}, u32[]{:S(2)}, u32[]{:S(2)}) collective-permute-start(bf16[4,4,24,640]{3,2,1,0:T(8,128)(2,1)S(1)} %stack_a.1.refs_0_), channel_id=1, source_target_pairs={{0,1},{1,0},{2,3},{3,2},{4,5},{5,4},{6,7},{7,6},{8,9},{9,8},{10,11... | collective-permute-start | bytes 1474568 | tf_op jit(solution)/shard_map/ppermute | solution.py:469
  27.5 6.2 %collective-permute-start.6 = (bf16[2,1,128,768]{3,2,1,0:T(8,128)(2,1)S(1)}, bf16[2,1,128,768]{3,2,1,0:T(8,128)(2,1)S(1)}, u32[]{:S(2)}, u32[]{:S(2)}) collective-permute-start(bf16[2,1,128,768]{3,2,1,0:T(8,128)(2,1)S(1)} %copy-done.16), channel_id=1, source_target_pairs={{0,1},{1,0},{2,3},{3,2},{4,5},{5,4},{6,7},{7,6},{8,9},{9,8},{10,11... | collective-permute-start | bytes 1179656 | tf_op jit(solution)/shard_map/ppermute | solution.py:469
  28.0 22.9 %collective-permute-start.17 = (bf16[12,24,768]{2,1,0:T(8,128)(2,1)S(1)}, bf16[12,24,768]{2,1,0:T(8,128)(2,1)}, u32[]{:S(2)}, u32[]{:S(2)}) collective-permute-start(bf16[12,24,768]{2,1,0:T(8,128)(2,1)S(1)} %with_down.1.s0), channel_id=1, source_target_pairs={{0,16},{1,17},{2,18},{3,19},{4,20},{5,21},{6,22},{7,23},{8,24},{9,... | collective-permute-start | bytes 1327112 | tf_op jit(solution)/shard_map/ppermute | solution.py:475
  28.3 22.6 %collective-permute-start.16 = (bf16[12,24,768]{2,1,0:T(8,128)(2,1)S(1)}, bf16[12,24,768]{2,1,0:T(8,128)(2,1)}, u32[]{:S(2)}, u32[]{:S(2)}) collective-permute-start(bf16[12,24,768]{2,1,0:T(8,128)(2,1)S(1)} %with_down.1.s0), channel_id=1, source_target_pairs={{0,8},{1,9},{2,10},{3,11},{4,12},{5,13},{6,14},{7,15},{8,0},{9,1},... | collective-permute-start | bytes 1327112 | tf_op jit(solution)/shard_map/ppermute | solution.py:475
  31.8 6.6 %collective-permute-start.11 = (bf16[128,768]{1,0:T(8,128)(2,1)S(1)}, bf16[128,768]{1,0:T(8,128)(2,1)S(1)}, u32[]{:S(2)}, u32[]{:S(2)}) collective-permute-start(bf16[128,768]{1,0:T(8,128)(2,1)S(1)} %slice.24), channel_id=1, source_target_pairs={{0,4},{1,5},{2,6},{3,7},{4,0},{5,1},{6,2},{7,3},{8,12},{9,13},{10,... | collective-permute-start | bytes 589832 | tf_op jit(solution)/shard_map/ppermute | solution.py:469
  33.7 6.9 %collective-permute-start.12 = (bf16[128,768]{1,0:T(8,128)(2,1)}, bf16[128,768]{1,0:T(8,128)(2,1)}, u32[]{:S(2)}, u32[]{:S(2)}) collective-permute-start(bf16[128,768]{1,0:T(8,128)(2,1)} %slice.25), channel_id=1, source_target_pairs={{0,2},{1,3},{2,0},{3,1},{4,6},{5,7},{6,4},{7,5},{8,10},{9,11},{10,... | collective-permute-start | bytes 589832 | tf_op jit(solution)/shard_map/ppermute | solution.py:469
  36.5 14.7 %collective-permute-start.20 = (bf16[256,768]{1,0:T(8,128)(2,1)S(1)}, bf16[256,768]{1,0:T(8,128)(2,1)S(1)}, u32[]{:S(2)}, u32[]{:S(2)}) collective-permute-start(bf16[256,768]{1,0:T(8,128)(2,1)S(1)} %place_g.1.g0.gw.g), channel_id=1, source_target_pairs={{0,4},{1,5},{2,6},{3,7},{4,0},{5,1},{6,2},{7,3},{8,12},{9,13},{10,... | collective-permute-start | bytes 1179656 | tf_op jit(solution)/shard_map/ppermute | solution.py:469
  38.4 12.9 %collective-permute-start.19 = (bf16[256,768]{1,0:T(8,128)(2,1)S(1)}, bf16[256,768]{1,0:T(8,128)(2,1)S(1)}, u32[]{:S(2)}, u32[]{:S(2)}) collective-permute-start(bf16[256,768]{1,0:T(8,128)(2,1)S(1)} %place_g.1.g0.gw.g), channel_id=1, source_target_pairs={{0,2},{1,3},{2,0},{3,1},{4,6},{5,7},{6,4},{7,5},{8,10},{9,11},{10,... | collective-permute-start | bytes 1179656 | tf_op jit(solution)/shard_map/ppermute | solution.py:469
  50.8 20.2 %copy-start.4 = (f32[16,768]{1,0:T(8,128)}, f32[16,768]{1,0:T(8,128)S(1)}, u32[]{:S(2)}) copy-start(f32[16,768]{1,0:T(8,128)S(1)} %get-tuple-element.174.small) | copy-start | bytes 147460
  50.8 20.2 %copy-start.6 = (bf16[256,192]{1,0:T(8,128)(2,1)}, bf16[256,192]{1,0:T(8,128)(2,1)S(1)}, u32[]{:S(2)}) copy-start(bf16[256,192]{1,0:T(8,128)(2,1)S(1)} %get-tuple-element.159.t0) | copy-start | bytes 294916
  50.9 12.0 %collective-permute-start.18 = (bf16[12,24,768]{2,1,0:T(8,128)(2,1)}, bf16[12,24,768]{2,1,0:T(8,128)(2,1)S(1)}, u32[]{:S(2)}, u32[]{:S(2)}) collective-permute-start(bf16[12,24,768]{2,1,0:T(8,128)(2,1)} %collective-permute-done.17.s2), channel_id=1, source_target_pairs={{0,8},{1,9},{2,10},{3,11},{4,12},{5,13},{6,14},{7,15},{8,0},{9,1},... | collective-permute-start | bytes 1327112 | tf_op jit(solution)/shard_map/ppermute | solution.py:475
  51.3 10.6 %collective-permute-start.22 = (bf16[128,768]{1,0:T(8,128)(2,1)S(1)}, bf16[128,768]{1,0:T(8,128)(2,1)S(1)}, u32[]{:S(2)}, u32[]{:S(2)}) collective-permute-start(bf16[128,768]{1,0:T(8,128)(2,1)S(1)} %slice.21), channel_id=1, source_target_pairs={{0,2},{1,3},{2,0},{3,1},{4,6},{5,7},{6,4},{7,5},{8,10},{9,11},{10,... | collective-permute-start | bytes 589832 | tf_op jit(solution)/shard_map/ppermute | solution.py:469
  52.8 9.2 %collective-permute-start.21 = (bf16[128,768]{1,0:T(8,128)(2,1)S(1)}, bf16[128,768]{1,0:T(8,128)(2,1)S(1)}, u32[]{:S(2)}, u32[]{:S(2)}) collective-permute-start(bf16[128,768]{1,0:T(8,128)(2,1)S(1)} %slice.20), channel_id=1, source_target_pairs={{0,4},{1,5},{2,6},{3,7},{4,0},{5,1},{6,2},{7,3},{8,12},{9,13},{10,... | collective-permute-start | bytes 589832 | tf_op jit(solution)/shard_map/ppermute | solution.py:469
  53.3 8.6 %collective-permute-start.14 = (bf16[256,192]{1,0:T(8,128)(2,1)S(1)}, bf16[256,192]{1,0:T(8,128)(2,1)S(1)}, u32[]{:S(2)}, u32[]{:S(2)}) collective-permute-start(bf16[256,192]{1,0:T(8,128)(2,1)S(1)} %get-tuple-element.161), channel_id=1, source_target_pairs={{0,4},{1,5},{2,6},{3,7},{4,0},{5,1},{6,2},{7,3},{8,12},{9,13},{10,... | collective-permute-start | bytes 294920 | tf_op jit(solution)/shard_map/ppermute | solution.py:469
  54.8 7.1 %collective-permute-start.13 = (bf16[256,192]{1,0:T(8,128)(2,1)S(1)}, bf16[256,192]{1,0:T(8,128)(2,1)S(1)}, u32[]{:S(2)}, u32[]{:S(2)}) collective-permute-start(bf16[256,192]{1,0:T(8,128)(2,1)S(1)} %get-tuple-element.160), channel_id=1, source_target_pairs={{0,2},{1,3},{2,0},{3,1},{4,6},{5,7},{6,4},{7,5},{8,10},{9,11},{10,... | collective-permute-start | bytes 294920 | tf_op jit(solution)/shard_map/ppermute | solution.py:469
  64.1 3.8 %collective-permute-start.23 = (bf16[4,12,24,768]{3,2,1,0:T(8,128)(2,1)S(1)}, bf16[4,12,24,768]{3,2,1,0:T(8,128)(2,1)S(1)}, u32[]{:S(2)}, u32[]{:S(2)}) collective-permute-start(bf16[4,12,24,768]{3,2,1,0:T(8,128)(2,1)S(1)} %stack_b.1.mine), channel_id=1, source_target_pairs={{0,1},{1,0},{2,3},{3,2},{4,5},{5,4},{6,7},{7,6},{8,9},{9,8},{10,11... | collective-permute-start | bytes 5308424 | tf_op jit(solution)/shard_map/ppermute | solution.py:469
  64.2 6.8 %collective-permute-start.15 = (bf16[256,192]{1,0:T(8,128)(2,1)S(1)}, bf16[256,192]{1,0:T(8,128)(2,1)S(1)}, u32[]{:S(2)}, u32[]{:S(2)}) collective-permute-start(bf16[256,192]{1,0:T(8,128)(2,1)S(1)} %get-tuple-element.163), channel_id=1, source_target_pairs={{0,6},{1,7},{2,4},{3,5},{4,2},{5,3},{6,0},{7,1},{8,14},{9,15},{10,... | collective-permute-start | bytes 294920 | tf_op jit(solution)/shard_map/ppermute | solution.py:469
  68.7 19.1 %copy-start = (bf16[32,24,768]{2,1,0:T(8,128)(2,1)}, bf16[32,24,768]{2,1,0:T(8,128)(2,1)S(1)}, u32[]{:S(2)}) copy-start(bf16[32,24,768]{2,1,0:T(8,128)(2,1)S(1)} %get-tuple-element.176) | copy-start | bytes 3538948
  68.7 19.1 %copy-start.2 = (bf16[32,24,768]{2,1,0:T(8,128)(2,1)}, bf16[32,24,768]{2,1,0:T(8,128)(2,1)S(1)}, u32[]{:S(2)}) copy-start(bf16[32,24,768]{2,1,0:T(8,128)(2,1)S(1)} %get-tuple-element.173) | copy-start | bytes 3538948
  72.3 10.9 %collective-permute-start.25 = (bf16[256,768]{1,0:T(8,128)(2,1)S(1)}, bf16[256,768]{1,0:T(8,128)(2,1)S(1)}, u32[]{:S(2)}, u32[]{:S(2)}) collective-permute-start(bf16[256,768]{1,0:T(8,128)(2,1)S(1)} %get-tuple-element.175.refs_0_), channel_id=1, source_target_pairs={{0,4},{1,5},{2,6},{3,7},{4,0},{5,1},{6,2},{7,3},{8,12},{9,13},{10,... | collective-permute-start | bytes 1179656 | tf_op jit(solution)/shard_map/ppermute | solution.py:469
  74.2 10.8 %collective-permute-start.24 = (bf16[256,768]{1,0:T(8,128)(2,1)S(1)}, bf16[256,768]{1,0:T(8,128)(2,1)S(1)}, u32[]{:S(2)}, u32[]{:S(2)}) collective-permute-start(bf16[256,768]{1,0:T(8,128)(2,1)S(1)} %get-tuple-element.175.refs_0_), channel_id=1, source_target_pairs={{0,2},{1,3},{2,0},{3,1},{4,6},{5,7},{6,4},{7,5},{8,10},{9,11},{10,... | collective-permute-start | bytes 1179656 | tf_op jit(solution)/shard_map/ppermute | solution.py:469
  83.1 5.8 %collective-permute-start.27 = (bf16[128,768]{1,0:T(8,128)(2,1)S(1)}, bf16[128,768]{1,0:T(8,128)(2,1)S(1)}, u32[]{:S(2)}, u32[]{:S(2)}) collective-permute-start(bf16[128,768]{1,0:T(8,128)(2,1)S(1)} %slice.27), channel_id=1, source_target_pairs={{0,2},{1,3},{2,0},{3,1},{4,6},{5,7},{6,4},{7,5},{8,10},{9,11},{10,... | collective-permute-start | bytes 589832 | tf_op jit(solution)/shard_map/ppermute | solution.py:469
  85.0 5.7 %collective-permute-start.26 = (bf16[128,768]{1,0:T(8,128)(2,1)S(1)}, bf16[128,768]{1,0:T(8,128)(2,1)S(1)}, u32[]{:S(2)}, u32[]{:S(2)}) collective-permute-start(bf16[128,768]{1,0:T(8,128)(2,1)S(1)} %slice.26), channel_id=1, source_target_pairs={{0,4},{1,5},{2,6},{3,7},{4,0},{5,1},{6,2},{7,3},{8,12},{9,13},{10,... | collective-permute-start | bytes 589832 | tf_op jit(solution)/shard_map/ppermute | solution.py:469
  94.9 6.0 %collective-permute-start.28 = (bf16[128,768]{1,0:T(8,128)(2,1)}, bf16[128,768]{1,0:T(8,128)(2,1)}, u32[]{:S(2)}, u32[]{:S(2)}) collective-permute-start(bf16[128,768]{1,0:T(8,128)(2,1)} %get-tuple-element.183), channel_id=1, source_target_pairs={{0,2},{1,3},{2,0},{3,1},{4,6},{5,7},{6,4},{7,5},{8,10},{9,11},{10,... | collective-permute-start | bytes 589832 | tf_op jit(solution)/shard_map/ppermute | solution.py:469
  95.1 6.0 %collective-permute-start.29 = (bf16[128,768]{1,0:T(8,128)(2,1)}, bf16[128,768]{1,0:T(8,128)(2,1)}, u32[]{:S(2)}, u32[]{:S(2)}) collective-permute-start(bf16[128,768]{1,0:T(8,128)(2,1)} %get-tuple-element.184), channel_id=1, source_target_pairs={{0,4},{1,5},{2,6},{3,7},{4,0},{5,1},{6,2},{7,3},{8,12},{9,13},{10,... | collective-permute-start | bytes 589832 | tf_op jit(solution)/shard_map/ppermute | solution.py:469
  102.4 2.9 %collective-permute-start.32 = (bf16[32,24,768]{2,1,0:T(8,128)(2,1)S(1)}, bf16[32,24,768]{2,1,0:T(8,128)(2,1)S(1)}, u32[]{:S(2)}, u32[]{:S(2)}) collective-permute-start(bf16[32,24,768]{2,1,0:T(8,128)(2,1)S(1)} %get-tuple-element.202), channel_id=1, source_target_pairs={{0,1},{1,0},{2,3},{3,2},{4,5},{5,4},{6,7},{7,6},{8,9},{9,8},{10,11... | collective-permute-start | bytes 3538952 | tf_op jit(solution)/shard_map/ppermute | solution.py:469
  102.5 11.5 %collective-permute-start.31 = (bf16[256,768]{1,0:T(8,128)(2,1)S(1)}, bf16[256,768]{1,0:T(8,128)(2,1)S(1)}, u32[]{:S(2)}, u32[]{:S(2)}) collective-permute-start(bf16[256,768]{1,0:T(8,128)(2,1)S(1)} %get-tuple-element.198), channel_id=1, source_target_pairs={{0,4},{1,5},{2,6},{3,7},{4,0},{5,1},{6,2},{7,3},{8,12},{9,13},{10,... | collective-permute-start | bytes 1179656 | tf_op jit(solution)/shard_map/ppermute | solution.py:469
  104.3 11.2 %collective-permute-start.30 = (bf16[256,768]{1,0:T(8,128)(2,1)S(1)}, bf16[256,768]{1,0:T(8,128)(2,1)S(1)}, u32[]{:S(2)}, u32[]{:S(2)}) collective-permute-start(bf16[256,768]{1,0:T(8,128)(2,1)S(1)} %get-tuple-element.191), channel_id=1, source_target_pairs={{0,2},{1,3},{2,0},{3,1},{4,6},{5,7},{6,4},{7,5},{8,10},{9,11},{10,... | collective-permute-start | bytes 1179656 | tf_op jit(solution)/shard_map/ppermute | solution.py:469
  106.1 9.3 %copy-start.3 = (bf16[32,24,768]{2,1,0:T(8,128)(2,1)S(1)}, bf16[32,24,768]{2,1,0:T(8,128)(2,1)}, u32[]{:S(2)}) copy-start(bf16[32,24,768]{2,1,0:T(8,128)(2,1)} %copy-done.2) | copy-start | bytes 3538948
  106.1 21.0 %collective-permute-start.38 = (bf16[2,8,24,768]{3,2,1,0:T(8,128)(2,1)S(1)}, bf16[2,8,24,768]{3,2,1,0:T(8,128)(2,1)S(1)}, u32[]{:S(2)}, u32[]{:S(2)}) collective-permute-start(bf16[2,8,24,768]{3,2,1,0:T(8,128)(2,1)S(1)} %get-tuple-element.213), channel_id=1, source_target_pairs={{0,8},{1,9},{2,10},{3,11},{4,12},{5,13},{6,14},{7,15},{8,0},{9,1},... | collective-permute-start | bytes 1769480 | tf_op jit(solution)/shard_map/ppermute | solution.py:475
  115.5 12.9 %copy-start.7 = (bf16[256,192]{1,0:T(8,128)(2,1)S(1)}, bf16[256,192]{1,0:T(8,128)(2,1)}, u32[]{:S(2)}) copy-start(bf16[256,192]{1,0:T(8,128)(2,1)} %copy-done.6) | copy-start | bytes 294916
  116.9 6.4 %collective-permute-start.33 = (bf16[256,192]{1,0:T(8,128)(2,1)S(1)}, bf16[256,192]{1,0:T(8,128)(2,1)S(1)}, u32[]{:S(2)}, u32[]{:S(2)}) collective-permute-start(bf16[256,192]{1,0:T(8,128)(2,1)S(1)} %get-tuple-element.205), channel_id=1, source_target_pairs={{0,2},{1,3},{2,0},{3,1},{4,6},{5,7},{6,4},{7,5},{8,10},{9,11},{10,... | collective-permute-start | bytes 294920 | tf_op jit(solution)/shard_map/ppermute | solution.py:469
  117.6 7.8 %collective-permute-start.34 = (bf16[256,192]{1,0:T(8,128)(2,1)S(1)}, bf16[256,192]{1,0:T(8,128)(2,1)S(1)}, u32[]{:S(2)}, u32[]{:S(2)}) collective-permute-start(bf16[256,192]{1,0:T(8,128)(2,1)S(1)} %get-tuple-element.206), channel_id=1, source_target_pairs={{0,4},{1,5},{2,6},{3,7},{4,0},{5,1},{6,2},{7,3},{8,12},{9,13},{10,... | collective-permute-start | bytes 294920 | tf_op jit(solution)/shard_map/ppermute | solution.py:469
  119.0 6.3 %collective-permute-start.35 = (bf16[256,192]{1,0:T(8,128)(2,1)S(1)}, bf16[256,192]{1,0:T(8,128)(2,1)S(1)}, u32[]{:S(2)}, u32[]{:S(2)}) collective-permute-start(bf16[256,192]{1,0:T(8,128)(2,1)S(1)} %get-tuple-element.207), channel_id=1, source_target_pairs={{0,6},{1,7},{2,4},{3,5},{4,2},{5,3},{6,0},{7,1},{8,14},{9,15},{10,... | collective-permute-start | bytes 294920 | tf_op jit(solution)/shard_map/ppermute | solution.py:469
  125.4 14.8 %collective-permute-start.36 = (bf16[256,768]{1,0:T(8,128)(2,1)S(1)}, bf16[256,768]{1,0:T(8,128)(2,1)S(1)}, u32[]{:S(2)}, u32[]{:S(2)}) collective-permute-start(bf16[256,768]{1,0:T(8,128)(2,1)S(1)} %get-tuple-element.208), channel_id=1, source_target_pairs={{0,2},{1,3},{2,0},{3,1},{4,6},{5,7},{6,4},{7,5},{8,10},{9,11},{10,... | collective-permute-start | bytes 1179656 | tf_op jit(solution)/shard_map/ppermute | solution.py:469
  126.4 13.8 %collective-permute-start.37 = (bf16[256,768]{1,0:T(8,128)(2,1)S(1)}, bf16[256,768]{1,0:T(8,128)(2,1)S(1)}, u32[]{:S(2)}, u32[]{:S(2)}) collective-permute-start(bf16[256,768]{1,0:T(8,128)(2,1)S(1)} %get-tuple-element.209), channel_id=1, source_target_pairs={{0,4},{1,5},{2,6},{3,7},{4,0},{5,1},{6,2},{7,3},{8,12},{9,13},{10,... | collective-permute-start | bytes 1179656 | tf_op jit(solution)/shard_map/ppermute | solution.py:469
  127.7 13.6 %collective-permute-start.39 = (bf16[8,24,768]{2,1,0:T(8,128)(2,1)S(1)}, bf16[8,24,768]{2,1,0:T(8,128)(2,1)S(1)}, u32[]{:S(2)}, u32[]{:S(2)}) collective-permute-start(bf16[8,24,768]{2,1,0:T(8,128)(2,1)S(1)} %pass_f.1), channel_id=1, source_target_pairs={{0,16},{1,17},{2,18},{3,19},{4,20},{5,21},{6,22},{7,23},{8,24},{9,... | collective-permute-start | bytes 884744 | tf_op jit(solution)/shard_map/ppermute | solution.py:475
  140.1 5.6 %collective-permute-start.49 = (bf16[16,24,768]{2,1,0:T(8,128)(2,1)S(1)}, bf16[16,24,768]{2,1,0:T(8,128)(2,1)S(1)}, u32[]{:S(2)}, u32[]{:S(2)}) collective-permute-start(bf16[16,24,768]{2,1,0:T(8,128)(2,1)S(1)} %get-tuple-element.255), channel_id=1, source_target_pairs={{0,1},{1,0},{2,3},{3,2},{4,5},{5,4},{6,7},{7,6},{8,9},{9,8},{10,11... | collective-permute-start | bytes 1769480 | tf_op jit(solution)/shard_map/ppermute | solution.py:469
  143.4 9.9 %collective-permute-start.40 = (bf16[16,24,640]{2,1,0:T(8,128)(2,1)S(1)}, bf16[16,24,640]{2,1,0:T(8,128)(2,1)S(1)}, u32[]{:S(2)}, u32[]{:S(2)}) collective-permute-start(bf16[16,24,640]{2,1,0:T(8,128)(2,1)S(1)} %get-tuple-element.232), channel_id=1, source_target_pairs={{0,1},{1,0},{2,3},{3,2},{4,5},{5,4},{6,7},{7,6},{8,9},{9,8},{10,11... | collective-permute-start | bytes 1474568 | tf_op jit(solution)/shard_map/ppermute | solution.py:469
  143.5 7.3 %collective-permute-start.44 = (bf16[128,768]{1,0:T(8,128)(2,1)S(1)}, bf16[128,768]{1,0:T(8,128)(2,1)S(1)}, u32[]{:S(2)}, u32[]{:S(2)}) collective-permute-start(bf16[128,768]{1,0:T(8,128)(2,1)S(1)} %get-tuple-element.243), channel_id=1, source_target_pairs={{0,2},{1,3},{2,0},{3,1},{4,6},{5,7},{6,4},{7,5},{8,10},{9,11},{10,... | collective-permute-start | bytes 589832 | tf_op jit(solution)/shard_map/ppermute | solution.py:469
  144.8 7.0 %collective-permute-start.45 = (bf16[128,768]{1,0:T(8,128)(2,1)S(1)}, bf16[128,768]{1,0:T(8,128)(2,1)S(1)}, u32[]{:S(2)}, u32[]{:S(2)}) collective-permute-start(bf16[128,768]{1,0:T(8,128)(2,1)S(1)} %get-tuple-element.244), channel_id=1, source_target_pairs={{0,4},{1,5},{2,6},{3,7},{4,0},{5,1},{6,2},{7,3},{8,12},{9,13},{10,... | collective-permute-start | bytes 589832 | tf_op jit(solution)/shard_map/ppermute | solution.py:469
  146.3 10.7 %collective-permute-start.50 = (bf16[2,4,24,768]{3,2,1,0:T(8,128)(2,1)S(1)}, bf16[2,4,24,768]{3,2,1,0:T(8,128)(2,1)S(1)}, u32[]{:S(2)}, u32[]{:S(2)}) collective-permute-start(bf16[2,4,24,768]{3,2,1,0:T(8,128)(2,1)S(1)} %get-tuple-element.257), channel_id=1, source_target_pairs={{0,8},{1,9},{2,10},{3,11},{4,12},{5,13},{6,14},{7,15},{8,0},{9,1},... | collective-permute-start | bytes 884744 | tf_op jit(solution)/shard_map/ppermute | solution.py:475
  152.4 22.4 %collective-permute-start.46 = (bf16[256,768]{1,0:T(8,128)(2,1)S(1)}, bf16[256,768]{1,0:T(8,128)(2,1)S(1)}, u32[]{:S(2)}, u32[]{:S(2)}) collective-permute-start(bf16[256,768]{1,0:T(8,128)(2,1)S(1)} %get-tuple-element.247), channel_id=1, source_target_pairs={{0,2},{1,3},{2,0},{3,1},{4,6},{5,7},{6,4},{7,5},{8,10},{9,11},{10,... | collective-permute-start | bytes 1179656 | tf_op jit(solution)/shard_map/ppermute | solution.py:469
  154.0 8.6 %collective-permute-start.42 = (bf16[2,4,24,640]{3,2,1,0:T(8,128)(2,1)S(1)}, bf16[2,4,24,640]{3,2,1,0:T(8,128)(2,1)S(1)}, u32[]{:S(2)}, u32[]{:S(2)}) collective-permute-start(bf16[2,4,24,640]{3,2,1,0:T(8,128)(2,1)S(1)} %get-tuple-element.236), channel_id=1, source_target_pairs={{0,8},{1,9},{2,10},{3,11},{4,12},{5,13},{6,14},{7,15},{8,0},{9,1},... | collective-permute-start | bytes 737288 | tf_op jit(solution)/shard_map/ppermute | solution.py:475
  154.2 22.0 %collective-permute-start.47 = (bf16[256,768]{1,0:T(8,128)(2,1)S(1)}, bf16[256,768]{1,0:T(8,128)(2,1)S(1)}, u32[]{:S(2)}, u32[]{:S(2)}) collective-permute-start(bf16[256,768]{1,0:T(8,128)(2,1)S(1)} %get-tuple-element.248), channel_id=1, source_target_pairs={{0,4},{1,5},{2,6},{3,7},{4,0},{5,1},{6,2},{7,3},{8,12},{9,13},{10,... | collective-permute-start | bytes 1179656 | tf_op jit(solution)/shard_map/ppermute | solution.py:469
  155.5 21.9 %collective-permute-start.41 = (bf16[256,768]{1,0:T(8,128)(2,1)S(1)}, bf16[256,768]{1,0:T(8,128)(2,1)S(1)}, u32[]{:S(2)}, u32[]{:S(2)}) collective-permute-start(bf16[256,768]{1,0:T(8,128)(2,1)S(1)} %get-tuple-element.234), channel_id=1, source_target_pairs={{0,6},{1,7},{2,4},{3,5},{4,2},{5,3},{6,0},{7,1},{8,14},{9,15},{10,... | collective-permute-start | bytes 1179656 | tf_op jit(solution)/shard_map/ppermute | solution.py:469
  157.6 12.4 %collective-permute-start.51 = (bf16[4,24,768]{2,1,0:T(8,128)(2,1)S(1)}, bf16[4,24,768]{2,1,0:T(8,128)(2,1)S(1)}, u32[]{:S(2)}, u32[]{:S(2)}) collective-permute-start(bf16[4,24,768]{2,1,0:T(8,128)(2,1)S(1)} %pass_o.1), channel_id=1, source_target_pairs={{0,16},{1,17},{2,18},{3,19},{4,20},{5,21},{6,22},{7,23},{8,24},{9,... | collective-permute-start | bytes 442376 | tf_op jit(solution)/shard_map/ppermute | solution.py:475
  163.2 8.2 %collective-permute-start.52 = (bf16[4,24,640]{2,1,0:T(8,128)(2,1)S(1)}, bf16[4,24,640]{2,1,0:T(8,128)(2,1)S(1)}, u32[]{:S(2)}, u32[]{:S(2)}) collective-permute-start(bf16[4,24,640]{2,1,0:T(8,128)(2,1)S(1)} %pass_r.1), channel_id=1, source_target_pairs={{0,16},{1,17},{2,18},{3,19},{4,20},{5,21},{6,22},{7,23},{8,24},{9,... | collective-permute-start | bytes 368648 | tf_op jit(solution)/shard_map/ppermute | solution.py:475
  172.8 6.0 %collective-permute-start.53 = (bf16[24,2176]{1,0:T(8,128)(2,1)S(1)}, bf16[24,2176]{1,0:T(8,128)(2,1)S(1)}, u32[]{:S(2)}, u32[]{:S(2)}) collective-permute-start(bf16[24,2176]{1,0:T(8,128)(2,1)S(1)} %get-tuple-element.261), channel_id=1, source_target_pairs={{0,2},{1,3},{2,0},{3,1},{4,6},{5,7},{6,4},{7,5},{8,10},{9,11},{10,... | collective-permute-start | bytes 313352 | tf_op jit(solution)/shard_map/ppermute | solution.py:469
  173.5 5.4 %collective-permute-start.54 = (bf16[24,2176]{1,0:T(8,128)(2,1)S(1)}, bf16[24,2176]{1,0:T(8,128)(2,1)S(1)}, u32[]{:S(2)}, u32[]{:S(2)}) collective-permute-start(bf16[24,2176]{1,0:T(8,128)(2,1)S(1)} %get-tuple-element.262), channel_id=1, source_target_pairs={{0,4},{1,5},{2,6},{3,7},{4,0},{5,1},{6,2},{7,3},{8,12},{9,13},{10,... | collective-permute-start | bytes 313352 | tf_op jit(solution)/shard_map/ppermute | solution.py:469
  174.8 5.6 %collective-permute-start.55 = (bf16[24,2176]{1,0:T(8,128)(2,1)S(1)}, bf16[24,2176]{1,0:T(8,128)(2,1)S(1)}, u32[]{:S(2)}, u32[]{:S(2)}) collective-permute-start(bf16[24,2176]{1,0:T(8,128)(2,1)S(1)} %get-tuple-element.263), channel_id=1, source_target_pairs={{0,6},{1,7},{2,4},{3,5},{4,2},{5,3},{6,0},{7,1},{8,14},{9,15},{10,... | collective-permute-start | bytes 313352 | tf_op jit(solution)/shard_map/ppermute | solution.py:469
  177.3 4.7 %collective-permute-start.48 = (f32[128,768]{1,0:T(8,128)S(1)}, f32[128,768]{1,0:T(8,128)S(1)}, u32[]{:S(2)}, u32[]{:S(2)}) collective-permute-start(f32[128,768]{1,0:T(8,128)S(1)} %get-tuple-element.251), channel_id=1, source_target_pairs={{0,1},{1,0},{2,3},{3,2},{4,5},{5,4},{6,7},{7,6},{8,9},{9,8},{10,11... | collective-permute-start | bytes 1179656 | tf_op jit(solution)/shard_map/ppermute | solution.py:469
  178.2 3.8 %collective-permute-start.43 = (bf16[128,768]{1,0:T(8,128)(2,1)S(1)}, bf16[128,768]{1,0:T(8,128)(2,1)S(1)}, u32[]{:S(2)}, u32[]{:S(2)}) collective-permute-start(bf16[128,768]{1,0:T(8,128)(2,1)S(1)} %get-tuple-element.239), channel_id=1, source_target_pairs={{0,1},{1,0},{2,3},{3,2},{4,5},{5,4},{6,7},{7,6},{8,9},{9,8},{10,11... | collective-permute-start | bytes 589832 | tf_op jit(solution)/shard_map/ppermute | solution.py:469
  (10 other events, 35.7 us)
